TPU v7x, 256 devices: a whole 4x4x8 slice. The times are simulated.
256 devices in a mesh: req: 128 (over x, y, z), head: 2 (over core).
Axes of the slice: x: 4, y: 4, z: 8, core: 2. Of those that a mesh axis runs over, the one named last changes fastest.
Arguments:
- verify_x: bfloat16 [128, 5, 2048], P('req'), may hold values from -6 to 6
- prefill_x: bfloat16 [32768, 2048], P('req'), may hold values from -6 to 6
- attn_gain: float32 [2048], replicated, may hold values from 0.25 to 1.75
- w_query: bfloat16 [2048, 2048], P(None, 'head'), may hold values from -0.125 to 0.125
- w_keyval: bfloat16 [2048, 1024], P(None, 'head'), may hold values from -0.125 to 0.125
- qk_gain: float32 [2, 256], replicated, may hold values from 0.25 to 8
- w_out: bfloat16 [2048, 2048], P('head'), may hold values from -0.125 to 0.125
- post_gain: float32 [2048], replicated, may hold values from 0.1 to 1.9
- page_pool: bfloat16 [8192, 16, 1024], P('req', None, 'head'), may hold values from -6 to 6
- outbound: int32 [128, 128], P('req'), may hold values from -1 to 63, as said below
- page_table: int32 [128, 64], P('req'), may hold values from 0 to 191, as said below
- cache_len: int32 [128], P('req'), may hold values from 1 to 1024, as said below
- prompt_len: int32 [128, 4], P('req'), may hold values from 1 to 128, 256 in all within a row
- accepted: int32 [128], P('req'), may hold values from 0 to 5
Outputs:
- verify_out: bfloat16 [128, 5, 2048], P('req', None, 'head')
- prefill_out: bfloat16 [32768, 2048], P('req', 'head')
- verify_kv: bfloat16 [128, 5, 1024], P('req', None, 'head')
- prefill_kv: bfloat16 [32768, 1024], P('req', 'head')
Inputs may be any that keep to these rules, and one draw needn't show every extreme that they name: `outbound`: row s names a page of device s's pool for every device d other than s; the entry at d = s is -1. `page_table`: an entry below 64 names a page of the device's own pool; an entry 64 + s names the page received from device s, s never the device itself. `cache_len`: some request has exactly 1024 cached tokens.
All inputs are finite; a program needn't handle non-finite values.
Results may differ from a plain program's by a relative error of at most 0.015.
The roundings to bfloat16 on the way count: a program that leaves them out, or rounds other values in their place, can miss the bound.
Values may be sent and summed in bfloat16 or wider, within the bound.
No kernel may reach another device: no remote copies, remote signals or barrier semaphores. Data moves between devices by JAX's collectives and lax.ppermute only.
A program may use at most 64 MiB of HBM per device.

v0:
```python
import jax
import jax.numpy as jnp
from jax import lax
from jax.sharding import PartitionSpec as P

HEAD = 256


eps_norm = 1e-06
rope_base = 1000000.0
neg_large = -1e30


def rms_scale(values):
    return values * lax.rsqrt(jnp.mean(values * values, axis=-1, keepdims=True) + eps_norm)


def rotate(values, position):
    half_dim = values.shape[-1] // 2
    inv_freq = rope_base ** (-(jnp.arange(half_dim, dtype=jnp.float32) * 2.0) / values.shape[-1])
    angles = position[:, None, None] * inv_freq[None, None, :]
    cosine = jnp.cos(angles)
    sine_part = jnp.sin(angles)
    first = values[..., :half_dim]
    second = values[..., half_dim:]
    return jnp.concatenate(
        [first * cosine - second * sine_part, second * cosine + first * sine_part], axis=-1
    )


def project(hidden_rows, attn_gain, w_query, w_keyval, qk_gain, position):
    row_count = hidden_rows.shape[0]
    normed = (rms_scale(hidden_rows.astype(jnp.float32)) * attn_gain).astype(jnp.bfloat16)
    query_rows = jnp.dot(normed, w_query, preferred_element_type=jnp.float32).reshape(
        row_count, -1, HEAD
    )
    query_rows = rotate(rms_scale(query_rows) * qk_gain[0], position).astype(jnp.bfloat16)
    keyval = jnp.dot(normed, w_keyval, preferred_element_type=jnp.float32).reshape(
        row_count, -1, 2, HEAD
    )
    key_rows = rotate(rms_scale(keyval[:, :, 0]) * qk_gain[1], position).astype(jnp.bfloat16)
    value_rows = rms_scale(keyval[:, :, 1]).astype(jnp.bfloat16)
    return (query_rows, key_rows, value_rows)


def attend(query_rows, key_rows, value_rows, allowed):
    row_count = query_rows.shape[0]
    groups = key_rows.shape[1]
    grouped = query_rows.reshape(row_count, groups, -1, HEAD)
    scores = jnp.einsum("tgqe,jge->gqtj", grouped, key_rows, preferred_element_type=jnp.float32)
    scores = jnp.where(allowed[None, None], scores, neg_large)
    peak_score = jnp.max(scores, axis=-1, keepdims=True)
    weights = jnp.exp(scores - peak_score)
    denom_sum = jnp.sum(weights, axis=-1, keepdims=True)
    attn_probs = (weights / denom_sum).astype(jnp.bfloat16)
    mixed_heads = jnp.einsum(
        "gqtj,jge->tgqe", attn_probs, value_rows, preferred_element_type=jnp.float32
    )
    return mixed_heads.reshape(row_count, -1).astype(jnp.bfloat16)


def prompt_layout(lengths, row_count):
    prompt_ends = jnp.cumsum(lengths)
    row_index = jnp.arange(row_count, dtype=jnp.int32)
    segment = jnp.sum((row_index[:, None] >= prompt_ends[None, :]).astype(jnp.int32), axis=1)
    starts = prompt_ends - lengths
    which = segment[:, None] == jnp.arange(lengths.shape[0], dtype=jnp.int32)[None, :]
    start_row = jnp.sum(jnp.where(which, starts[None, :], 0), axis=1)
    position = (row_index - start_row).astype(jnp.float32)
    allowed = (segment[:, None] == segment[None, :]) & (row_index[None, :] <= row_index[:, None])
    return (position, allowed)


def on_device(
    verify_x,
    prefill_x,
    attn_gain,
    w_query,
    w_keyval,
    qk_gain,
    w_out,
    post_gain,
    page_pool,
    outbound,
    page_table,
    cache_len,
    prompt_len,
    accepted,
):
    req_count, draft_len, width = verify_x.shape
    pref_rows = prefill_x.shape[0]
    sent_page = outbound[0]
    outgoing = jnp.take(page_pool, jnp.clip(sent_page, 0, page_pool.shape[0] - 1), axis=0)
    outgoing = jnp.where((sent_page >= 0)[:, None, None], outgoing, jnp.zeros_like(outgoing))
    arrived = lax.all_to_all(outgoing, "req", split_axis=0, concat_axis=0, tiled=True)
    pool_now = jnp.concatenate([page_pool, arrived], axis=0)
    verify_pos = (
        (cache_len[:, None] + jnp.arange(draft_len, dtype=jnp.int32)[None, :])
        .astype(jnp.float32)
        .reshape(-1)
    )
    prefill_pos, prefill_allowed = prompt_layout(prompt_len[0], pref_rows)
    all_rows = jnp.concatenate([verify_x.reshape(-1, width), prefill_x], axis=0)
    position = jnp.concatenate([verify_pos, prefill_pos], axis=0)
    query_rows, key_rows, value_rows = project(
        all_rows, attn_gain, w_query, w_keyval, qk_gain, position
    )
    groups = key_rows.shape[1]
    verify_count = req_count * draft_len

    def verify_one(query_part, key_part, value_part, page_list, length):
        cached = jnp.take(pool_now, page_list, axis=0).reshape(-1, groups, 2, HEAD)
        cache_rows = cached.shape[0]
        all_keys = jnp.concatenate([cached[:, :, 0], key_part], axis=0)
        all_values = jnp.concatenate([cached[:, :, 1], value_part], axis=0)
        slot = jnp.arange(cache_rows + draft_len, dtype=jnp.int32)
        step_index = jnp.arange(draft_len, dtype=jnp.int32)
        allowed = jnp.where(
            slot[None, :] < cache_rows,
            slot[None, :] < length,
            slot[None, :] - cache_rows <= step_index[:, None],
        )
        return attend(query_part, all_keys, all_values, allowed)

    verify_attn = jax.vmap(verify_one)(
        query_rows[:verify_count].reshape(req_count, draft_len, -1, HEAD),
        key_rows[:verify_count].reshape(req_count, draft_len, groups, HEAD),
        value_rows[:verify_count].reshape(req_count, draft_len, groups, HEAD),
        page_table,
        cache_len,
    )
    prefill_attn = attend(
        query_rows[verify_count:],
        key_rows[verify_count:],
        value_rows[verify_count:],
        prefill_allowed,
    )
    all_attn = jnp.concatenate([verify_attn.reshape(verify_count, -1), prefill_attn], axis=0)
    partial_rows = jnp.dot(all_attn, w_out, preferred_element_type=jnp.float32)
    half_cols = width // lax.axis_size("head")
    offset = lax.axis_index("head") * half_cols
    summed = lax.psum(partial_rows, "head")
    own_part = lax.dynamic_slice_in_dim(rms_scale(summed), offset, half_cols, 1)
    residual = lax.dynamic_slice_in_dim(all_rows, offset, half_cols, 1).astype(jnp.float32)
    gain_part = lax.dynamic_slice_in_dim(post_gain, offset, half_cols, 0)
    final = (residual + own_part * gain_part).astype(jnp.bfloat16)
    verify_out = final[:verify_count].reshape(req_count, draft_len, half_cols)
    prefill_out = final[verify_count:]
    new_cache = jnp.stack([key_rows, value_rows], axis=2).reshape(all_rows.shape[0], -1)
    verify_cache = new_cache[:verify_count].reshape(req_count, draft_len, -1)
    keep_rows = jnp.arange(draft_len, dtype=jnp.int32)[None, :, None] < accepted[:, None, None]
    verify_kv = jnp.where(keep_rows, verify_cache, jnp.zeros_like(verify_cache))
    prefill_kv = new_cache[verify_count:]
    return (verify_out, prefill_out, verify_kv, prefill_kv)


def solution(mesh):
    placed = (
        P("req", None, None),
        P("req", None),
        P(),
        P(None, "head"),
        P(None, "head"),
        P(),
        P("head", None),
        P(),
        P("req", None, "head"),
        P("req", None),
        P("req", None),
        P("req"),
        P("req", None),
        P("req"),
    )
    return jax.shard_map(
        on_device,
        mesh=mesh,
        in_specs=placed,
        out_specs=(
            P("req", None, "head"),
            P("req", "head"),
            P("req", None, "head"),
            P("req", "head"),
        ),
        check_vma=False,
    )
```

profile of v0, /device:TPU:1, one launch (start us, length us, event | category | flops | bytes accessed | tf_op | source)
XLA Modules:
  0.0 138.2 jit_solution(2135943802772641248)
XLA Ops:
  9.3 3.3 %gather_fusion = bf16[128,16,512]{2,1,0:T(8,128)(2,1)} fusion(bf16[64,16,512]{2,1,0:T(8,128)(2,1)} %param.22, s32[1024]{0:T(1024)S(1)} %pad_clamp_fusion.1), kind=kCustom, calls=%fused_computation | custom fusion | bytes 4194816 | tf_op jit(solution)/shard_map/jit(_take)/gather | solution.py:93
  12.6 3.0 %select_select_fusion = bf16[128,16,512]{2,1,0:T(8,128)(2,1)} fusion(bf16[128,16,512]{2,1,0:T(8,128)(2,1)} %gather_fusion, pred[128]{0:T(512)(128)(4,1)S(1)} %compare_and_fusion, pred[128]{0:T(512)(128)(4,1)S(1)} %compare_bitcast_fusion), kind=kLoop, calls=%fused_computation.11 | loop fusion | flops 2097152 | bytes 4194560 | tf_op jit(solution)/shard_map/jit(_where)/select_n | solution.py:94
  15.6 17.0 %all-to-all-start = ((bf16[128,16,512]{2,1,0:T(8,128)(2,1)}), bf16[128,16,512]{2,1,0:T(8,128)(2,1)}, u32[]{:S(2)}, u32[]{:S(2)}) async-start(bf16[128,16,512]{2,1,0:T(8,128)(2,1)} %select_select_fusion), calls=%async_computation | async-start | bytes 4194304 | tf_op jit(solution)/shard_map/all_to_all | solution.py:95
  34.0 1.6 %fusion.51 = f32[261,512]{1,0:T(8,128)} fusion(bf16[2048,512]{1,0:T(8,128)(2,1)S(1)} %copy-done, f32[2048]{0:T(1024)S(1)} %copy-done.17, f32[261]{0:T(512)S(1)} %add_rsqrt_fusion.4, bf16[256,2048]{1,0:T(8,128)(2,1)S(1)} %copy-done.3, bf16[5,2048]{1,0:T(8,128)(2,1)S(1)} %bitcast.115), kind=kOutput, calls=%fused_computation.125 | convolution fusion | flops 551098368 | bytes 3709972 | tf_op jit(solution)/shard_map/dot_general | solution.py:38
  35.6 2.2 %reshape.682 = f32[261,1,2,256]{3,2,0,1:T(2,128)} reshape(f32[261,512]{1,0:T(8,128)} %fusion.51) | data formatting | bytes 1069056 | tf_op jit(solution)/shard_map/reshape | solution.py:38
  37.8 1.7 %fusion.53 = (f32[261,1,1,256]{3,2,0,1:T(1,128)S(1)}, f32[261,1,1,256]{3,2,0,1:T(1,128)S(1)}) fusion(f32[261,1,2,256]{3,2,0,1:T(2,128)} %reshape.682), kind=kLoop, calls=%fused_computation.126 | loop fusion | bytes 1069056 | tf_op jit(solution)/shard_map/slice | solution.py:42
  41.3 4.6 %fusion.49 = f32[261,1024]{1,0:T(8,128)} fusion(bf16[2048,1024]{1,0:T(8,128)(2,1)} %param.17, f32[2048]{0:T(1024)S(1)} %copy-done.17, f32[261]{0:T(512)S(1)} %add_rsqrt_fusion.4, bf16[256,2048]{1,0:T(8,128)(2,1)S(1)} %copy-done.3, bf16[5,2048]{1,0:T(8,128)(2,1)S(1)} %bitcast.116), kind=kOutput, calls=%fused_computation.124 | convolution fusion | flops 1098455040 | bytes 6341652 | tf_op jit(solution)/shard_map/dot_general | solution.py:34
  45.9 1.8 %reshape.689 = f32[261,4,256]{2,1,0:T(4,128)S(1)} reshape(f32[261,1024]{1,0:T(8,128)} %fusion.49) | data formatting | bytes 2138112 | tf_op jit(solution)/shard_map/reshape | solution.py:34
  47.7 1.0 multiply_reduce_fusion.1
  48.7 1.0 copy.55
  51.8 1.1 fusion.21
  52.9 1.3 fusion.29
  54.3 1.2 multiply_cosine_fusion
  56.7 1.2 convolution_convert_fusion
  57.9 27.0 %all-to-all-done = bf16[128,16,512]{2,1,0:T(8,128)(2,1)} async-done(((bf16[128,16,512]{2,1,0:T(8,128)(2,1)}), bf16[128,16,512]{2,1,0:T(8,128)(2,1)}, u32[]{:S(2)}, u32[]{:S(2)}) %all-to-all-start) | async-done | bytes 2097184 | tf_op jit(solution)/shard_map/all_to_all | solution.py:95
  84.9 3.5 %pad_maximum_fusion = bf16[192,16,512]{2,1,0:T(8,128)(2,1)} fusion(bf16[128,16,512]{2,1,0:T(8,128)(2,1)} %all-to-all-done, bf16[64,16,512]{2,1,0:T(8,128)(2,1)S(1)} %copy-done.1), kind=kLoop, calls=%fused_computation.2 | loop fusion | flops 1572864 | bytes 6291456 | tf_op jit(solution)/shard_map/concatenate | solution.py:96
  88.4 2.6 %gather_fusion.1 = bf16[64,16,512]{2,1,0:T(8,128)(2,1)S(1)} fusion(bf16[192,16,512]{2,1,0:T(8,128)(2,1)} %pad_maximum_fusion, s32[1024]{0:T(1024)} %pad_clamp_fusion), kind=kCustom, calls=%fused_computation.1 | custom fusion | bytes 2097408 | tf_op jit(solution)/shard_map/vmap(jit(_take))/gather | solution.py:112
  91.1 1.1 gather.12
  92.2 1.5 %copy_select_fusion = bf16[1,1024,1,2,256]{4,1,3,2,0:T(8,128)(2,1)S(1)} fusion(bf16[1,1024,1,2,256]{4,3,1,2,0:T(2,128)(2,1)} %gather.12, pred[1024]{0:T(1024)(128)(4,1)S(1)} %copy-done.15), kind=kLoop, calls=%fused_computation.25 | loop fusion | flops 524288 | bytes 2098176 | tf_op jit(solution)/shard_map/vmap(jit(_take))/select_n | solution.py:112
  94.8 4.9 %fusion.10 = f32[261,2048]{1,0:T(8,128)} fusion(bf16[1024,2048]{1,0:T(8,128)(2,1)} %param.20, bf16[256,1024]{0,1:T(8,128)(2,1)S(1)} %bitcast.123, bf16[5,1024]{0,1:T(8,128)(2,1)S(1)} %copy.59), kind=kOutput, calls=%fused_computation.30 | convolution fusion | flops 1095782400 | bytes 6866944 | tf_op jit(solution)/shard_map/dot_general | solution.py:139
  100.5 1.7 %pad_maximum_fusion.4 = bf16[256,1,2,256]{3,0,2,1:T(8,128)(2,1)} fusion(bf16[261,1,1,256]{3,0,2,1:T(8,128)(2,1)S(1)} %multiply_convert_fusion, bf16[261,1,1,128]{3,0,2,1:T(8,128)(2,1)} %bitcast.111, bf16[261,1,1,128]{3,0,2,1:T(8,128)(2,1)S(1)} %bitcast.109), kind=kLoop, calls=%fused_computation.56 | loop fusion | flops 786432 | bytes 529408 | tf_op jit(solution)/shard_map/stack | solution.py:149
  102.2 1.1 copy.60
  106.2 20.9 %all-reduce.2.cloned.1.call-done = f32[261,2048]{1,0:T(8,128)} async-done(((f32[261,2048]{1,0:T(8,128)}), f32[261,2048]{1,0:T(8,128)}) %all-reduce.2.cloned.1.call-update) | async-done | bytes 2138128 | tf_op jit(solution)/shard_map/psum | solution.py:142
  127.1 2.0 %multiply_reduce_fusion = f32[261]{0:T(512)S(1)} fusion(f32[261,2048]{1,0:T(8,128)} %all-reduce.2.cloned.1.call-done), kind=kLoop, calls=%fused_computation.10 | loop fusion | flops 1068795 | bytes 2139156 | tf_op jit(solution)/shard_map/reduce_sum | solution.py:15
  (95 shorter events, 14.3 us)
Async XLA Ops:
  7.2 26.8 %copy-start = (bf16[2048,512]{1,0:T(8,128)(2,1)S(1)}, bf16[2048,512]{1,0:T(8,128)(2,1)}, u32[]{:S(2)}) copy-start(bf16[2048,512]{1,0:T(8,128)(2,1)} %param.18) | copy-start | bytes 6291460
  15.6 17.9 %copy-start.18 = (s32[1,64]{1,0:T(1,128)S(1)}, s32[1,64]{1,0:T(1,128)}, u32[]{:S(2)}) copy-start(s32[1,64]{1,0:T(1,128)} %param.24) | copy-start | bytes 772
  15.6 17.9 %copy-start.3 = (bf16[256,2048]{1,0:T(8,128)(2,1)S(1)}, bf16[256,2048]{1,0:T(8,128)(2,1)}, u32[]{:S(2)}) copy-start(bf16[256,2048]{1,0:T(8,128)(2,1)} %param.15) | copy-start | bytes 3145732
  15.6 17.9 %copy-start.12 = (bf16[1,5,2048]{2,1,0:T(8,128)(2,1)S(1)}, bf16[1,5,2048]{2,1,0:T(8,128)(2,1)}, u32[]{:S(2)}) copy-start(bf16[1,5,2048]{2,1,0:T(8,128)(2,1)} %param.14) | copy-start | bytes 61444
  15.6 18.4 %copy-start.17 = (f32[2048]{0:T(1024)S(1)}, f32[2048]{0:T(1024)}, u32[]{:S(2)}) copy-start(f32[2048]{0:T(1024)} %param.16) | copy-start | bytes 24580
  15.6 69.3 %all-to-all-start = ((bf16[128,16,512]{2,1,0:T(8,128)(2,1)}), bf16[128,16,512]{2,1,0:T(8,128)(2,1)}, u32[]{:S(2)}, u32[]{:S(2)}) async-start(bf16[128,16,512]{2,1,0:T(8,128)(2,1)} %select_select_fusion), calls=%async_computation | async-start | bytes 4194304 | tf_op jit(solution)/shard_map/all_to_all | solution.py:95
  32.6 94.4 %all-reduce.2.cloned.1.call-start = ((), (), s32[]{:S(2)}) async-start(), calls=%async_computation.1 | async-start | bytes 4325376 | tf_op jit(solution)/shard_map/psum | solution.py:142
  35.6 4.7 %copy-start.19 = (s32[1,4]{1,0:T(1,128)S(1)}, s32[1,4]{1,0:T(1,128)}, u32[]{:S(2)}) copy-start(s32[1,4]{1,0:T(1,128)} %param.26) | copy-start | bytes 52
  39.4 0.7 copy-start.5
  45.9 5.8 %copy-start.16 = (f32[2,256]{1,0:T(2,128)S(1)}, f32[2,256]{1,0:T(2,128)}, u32[]{:S(2)}) copy-start(f32[2,256]{1,0:T(2,128)} %param.19) | copy-start | bytes 6148
  54.2 1.8 %copy-start.7 = (bf16[261,1,128]{2,0,1:T(8,128)(2,1)}, bf16[261,1,128]{2,0,1:T(8,128)(2,1)S(1)}, u32[]{:S(2)}) copy-start(bf16[261,1,128]{2,0,1:T(8,128)(2,1)S(1)} %get-tuple-element.27) | copy-start | bytes 200452
  56.0 1.9 %copy-start.8 = (bf16[261,4,128]{2,0,1:T(8,128)(2,1)}, bf16[261,4,128]{2,0,1:T(8,128)(2,1)S(1)}, u32[]{:S(2)}) copy-start(bf16[261,4,128]{2,0,1:T(8,128)(2,1)S(1)} %get-tuple-element.20) | copy-start | bytes 801796
  56.0 1.9 %copy-start.10 = (bf16[261,4,128]{2,0,1:T(8,128)(2,1)}, bf16[261,4,128]{2,0,1:T(8,128)(2,1)S(1)}, u32[]{:S(2)}) copy-start(bf16[261,4,128]{2,0,1:T(8,128)(2,1)S(1)} %get-tuple-element.21) | copy-start | bytes 801796
  56.7 1.2 copy-start.13
  56.7 1.2 copy-start.14
  56.7 28.2 %copy-start.1 = (bf16[64,16,512]{2,1,0:T(8,128)(2,1)S(1)}, bf16[64,16,512]{2,1,0:T(8,128)(2,1)}, u32[]{:S(2)}) copy-start(bf16[64,16,512]{2,1,0:T(8,128)(2,1)} %param.22) | copy-start | bytes 3145732
  88.4 3.8 %copy-start.15 = (pred[1024]{0:T(1024)(128)(4,1)S(1)}, pred[1024]{0:T(1024)(128)(4,1)}, u32[]{:S(2)}) copy-start(pred[1024]{0:T(1024)(128)(4,1)} %broadcast_in_dim.141) | copy-start | bytes 3076
  92.2 1.6 %copy-start.9 = (bf16[261,4,128]{2,0,1:T(8,128)(2,1)S(1)}, bf16[261,4,128]{2,0,1:T(8,128)(2,1)}, u32[]{:S(2)}) copy-start(bf16[261,4,128]{2,0,1:T(8,128)(2,1)} %copy-done.8) | copy-start | bytes 801796
  92.2 1.6 %copy-start.11 = (bf16[261,4,128]{2,0,1:T(8,128)(2,1)S(1)}, bf16[261,4,128]{2,0,1:T(8,128)(2,1)}, u32[]{:S(2)}) copy-start(bf16[261,4,128]{2,0,1:T(8,128)(2,1)} %copy-done.10) | copy-start | bytes 801796
  93.8 1.0 copy-start.20
  99.9 0.7 copy-start.6
  99.9 29.2 %copy-start.4 = (bf16[256,2048]{1,0:T(8,128)(2,1)S(1)}, bf16[256,2048]{1,0:T(8,128)(2,1)}, u32[]{:S(2)}) copy-start(bf16[256,2048]{1,0:T(8,128)(2,1)} %param.15) | copy-start | bytes 3145732
  104.8 24.3 %dynamic-slice-start = ((f32[2048]{0:T(1024)}, s32[]{:T(128)}), f32[1024]{0:T(1024)S(1)}, s32[]{:S(2)}) async-start(f32[2048]{0:T(1024)} %param.21, s32[]{:T(128)} %select_n.81), calls=%async_computation.2 | async-start | bytes 8704 | tf_op jit(solution)/shard_map/dynamic_slice | solution.py:145
  127.1 2.3 %copy-start.2 = (f32[261,2048]{1,0:T(8,128)S(1)}, f32[261,2048]{1,0:T(8,128)}, u32[]{:S(2)}) copy-start(f32[261,2048]{1,0:T(8,128)} %all-reduce.2.cloned.1.call-done) | copy-start | bytes 6414340
Sparse Core Ops, SparseCore 0:
  99.9 27.1 all-reduce.1
where the time goes:
time: 139 us; the launch traced here: 138 us
  waiting for transfers between devices  47.9 us (34%)
  other arithmetic  24.3 us (17%)
  local copies, waits for them, and re-layouts  19.8 us (14%)
  starting transfers between devices  17.2 us (12%)
  between operations  15.7 us (11%)
  matrix products  13.3 us (10%)
    all_to_all x1, waiting for transfers between devices, on_device(): lax.all_to_all(outgoing, 'req', split_axis=0, concat_axis=0, tiled=True)  27 us
    psum x1, waiting for transfers between devices, on_device(): summed = lax.psum(partial_rows, 'head')  20.9 us
    all_to_all x1, starting transfers between devices, on_device(): lax.all_to_all(outgoing, 'req', split_axis=0, concat_axis=0, tiled=True)  17 us
    dot_general x1, matrix products, on_device(): partial_rows = jnp.dot(all_attn, w_out, preferred_element_type=jnp.float32)  4.91 us
    reduce_sum x5, other arithmetic, rms_scale(): jnp.mean(values * values, axis=-1, keepdims=True) + eps_norm  4.76 us
    dot_general x1, matrix products, project(): jnp.dot(normed, w_query, preferred_element_type=jnp.float32)  4.6 us
    gather x2, local copies, waits for them, and re-layouts, verify_one(): cached = jnp.take(pool_now, page_list, axis=0).reshape(-1, groups, 2, HEAD)  3.76 us
    concatenate x1, other arithmetic, on_device(): pool_now = jnp.concatenate([page_pool, arrived], axis=0)  3.53 us
  transfers between devices with their start and end apart: 2, of which 2 were waited for; matrix products, arithmetic and copies ran while one was open for 21% of the time, Pallas kernels for 0%

commit v1 on v0

v1 whole, which is shorter than its diff:
```python
import functools

import jax
import jax.numpy as jnp
from jax import lax
from jax.experimental import pallas as pl
from jax.experimental.pallas import tpu as pltpu
from jax.sharding import PartitionSpec as P

HEAD = 256
PAGE = 16
eps_norm = 1e-06
rope_base = 1000000.0
neg_large = -1e30
bf16, f32 = jnp.bfloat16, jnp.float32
PAD = 8


def dot_t(a, b):
    return lax.dot_general(a, b, (((1,), (1,)), ((), ())), preferred_element_type=f32)


def dot_n(a, b):
    return jnp.dot(a, b, preferred_element_type=f32)


def pick_kernel(index, pool, out):
    base = pl.program_id(0) * out.shape[0]
    for i in range(out.shape[0]):
        page = jnp.clip(index[base + i], 0, pool.shape[0] - 1)
        out[i] = pool[page]


def pick_pages(pool, index):
    count, steps = index.shape[0], 4
    rows = count // steps
    return pl.pallas_call(
        pick_kernel,
        grid_spec=pltpu.PrefetchScalarGridSpec(
            num_scalar_prefetch=1,
            grid=(steps,),
            in_specs=[pl.BlockSpec(pool.shape, lambda i, idx: (0, 0, 0))],
            out_specs=pl.BlockSpec((rows,) + pool.shape[1:], lambda i, idx: (i, 0, 0)),
        ),
        out_shape=jax.ShapeDtypeStruct((count,) + pool.shape[1:], pool.dtype),
        cost_estimate=pl.CostEstimate(flops=0, transcendentals=0, bytes_accessed=3 << 20),
        name="pick_pages",
    )(index, pool)


def project_kernel(x, gain, wq, wkv, qk_gain, cosine, sine, out, kv_out, normed):
    step = pl.program_id(0)
    tail = kv_out.shape[0]

    @pl.when(step == 0)
    def _():
        rows = x[...].astype(f32)
        scale = lax.rsqrt(jnp.mean(rows * rows, axis=-1, keepdims=True) + eps_norm)
        normed[...] = (rows * scale * gain[...]).astype(bf16)

    def normalised(weights):
        acc = dot_n(normed[...], weights)
        return acc * lax.rsqrt(jnp.mean(acc * acc, axis=-1, keepdims=True) + eps_norm)

    def rotated(values):
        half = HEAD // 2
        a, b = values[:, :half], values[:, half:]
        c, s = cosine[...], sine[...]
        return jnp.concatenate([a * c - b * s, b * c + a * s], axis=-1).astype(bf16)

    @pl.when(step < 4)
    def _():
        out[0] = rotated(normalised(wq[...]) * qk_gain[0:1, :])

    @pl.when(step == 4)
    def _():
        key = rotated(normalised(wkv[...]) * qk_gain[1:2, :])
        out[0] = key
        kv_out[...] = key[:tail]

    @pl.when(step == 5)
    def _():
        value = normalised(wkv[...]).astype(bf16)
        out[0] = value
        kv_out[...] = value[:tail]


def project(rows, gain, w_query, w_keyval, qk_gain, cosine, sine, tail):
    count, width = rows.shape
    whole = lambda shape: pl.BlockSpec(shape, lambda i: (0, 0))
    return pl.pallas_call(
        project_kernel,
        grid=(6,),
        in_specs=[
            whole((count, width)),
            whole((1, width)),
            pl.BlockSpec((width, HEAD), lambda i: (0, jnp.minimum(i, 3))),
            pl.BlockSpec((width, HEAD), lambda i: (0, jnp.maximum(i - 4, 0))),
            whole((2, HEAD)),
            whole((count, HEAD // 2)),
            whole((count, HEAD // 2)),
        ],
        out_specs=[
            pl.BlockSpec((1, count, HEAD), lambda i: (i, 0, 0)),
            pl.BlockSpec((tail, HEAD), lambda i: (0, jnp.maximum(i - 4, 0))),
        ],
        out_shape=[
            jax.ShapeDtypeStruct((6, count, HEAD), bf16),
            jax.ShapeDtypeStruct((tail, 2 * HEAD), bf16),
        ],
        scratch_shapes=[pltpu.VMEM((count, width), bf16)],
        compiler_params=pltpu.CompilerParams(vmem_limit_bytes=24 << 20),
        cost_estimate=pl.CostEstimate(
            flops=2 * count * width * 1536, transcendentals=0, bytes_accessed=9 << 20
        ),
        name="project",
    )(rows, gain, w_query, w_keyval, qk_gain, cosine, sine)


def prompt_kernel(ends, q, k, v, w_out, out, attn):
    rows = attn.shape[0]

    @pl.when(pl.program_id(0) == 0)
    def _():
        row = lax.broadcasted_iota(jnp.int32, (rows, rows), 0)
        col = lax.broadcasted_iota(jnp.int32, (rows, rows), 1)
        start = jnp.zeros((rows, rows), jnp.int32)
        for i in range(3):
            start = jnp.where(row >= ends[i], ends[i], start)
        allowed = (col <= row) & (col >= start)
        key, value = k[0, :rows], v[0, :rows]
        for h in range(4):
            scores = jnp.where(allowed, dot_t(q[h, :rows], key), neg_large)
            weights = jnp.exp(scores - jnp.max(scores, axis=-1, keepdims=True))
            probs = (weights / jnp.sum(weights, axis=-1, keepdims=True)).astype(bf16)
            attn[:, h * HEAD : (h + 1) * HEAD] = dot_n(probs, value).astype(bf16)

    out[...] = dot_n(attn[...], w_out[...]).astype(out.dtype)


def prompts(ends, qkv, w_out, rows):
    count = qkv.shape[1]
    depth, width = w_out.shape
    cols = 512
    return pl.pallas_call(
        prompt_kernel,
        grid_spec=pltpu.PrefetchScalarGridSpec(
            num_scalar_prefetch=1,
            grid=(width // cols,),
            in_specs=[
                pl.BlockSpec((4, count, HEAD), lambda i, e: (0, 0, 0)),
                pl.BlockSpec((1, count, HEAD), lambda i, e: (4, 0, 0)),
                pl.BlockSpec((1, count, HEAD), lambda i, e: (5, 0, 0)),
                pl.BlockSpec((depth, cols), lambda i, e: (0, i)),
            ],
            out_specs=pl.BlockSpec((rows, cols), lambda i, e: (0, i)),
            scratch_shapes=[pltpu.VMEM((rows, depth), bf16)],
        ),
        out_shape=jax.ShapeDtypeStruct((rows, width), bf16),
        compiler_params=pltpu.CompilerParams(vmem_limit_bytes=24 << 20),
        cost_estimate=pl.CostEstimate(
            flops=2 * rows * depth * width, transcendentals=4 * rows * rows, bytes_accessed=6 << 20
        ),
        name="prompts",
    )(ends, qkv, qkv, qkv, w_out)


def piece(scores, count):
    live = count > 0.0
    scores = jnp.where(live, scores, neg_large)
    peak = jnp.max(scores, axis=-1, keepdims=True).astype(bf16).astype(f32)
    weights = jnp.where(live, jnp.exp(scores - peak) * count, 0.0)
    return weights, peak, jnp.sum(weights, axis=-1, keepdims=True)


def remote_kernel(queries, pages, out):
    groups, rows = queries.shape[0], queries.shape[1]
    lane = lax.broadcasted_iota(jnp.int32, (rows, 128), 1)
    for z in range(groups):
        query = queries[z]
        count = query[5:6, :].astype(f32)
        held = pages[:, z].reshape(-1, 2 * HEAD)
        weights, peak, denom = piece(dot_t(query, held[:, :HEAD]), count)
        total = dot_n(weights.astype(bf16), held[:, HEAD:])
        high = denom.astype(bf16).astype(f32)
        stats = jnp.where(lane < 32, peak, jnp.where(lane < 64, high, denom - high))
        out[z, :, :HEAD] = total.astype(bf16)
        out[z, :, HEAD:] = stats.astype(bf16)


def remote_pieces(queries, pages):
    groups, rows, _ = queries.shape
    return pl.pallas_call(
        remote_kernel,
        out_shape=jax.ShapeDtypeStruct((groups, rows, HEAD + 128), bf16),
        compiler_params=pltpu.CompilerParams(vmem_limit_bytes=24 << 20),
        cost_estimate=pl.CostEstimate(flops=1 << 26, transcendentals=1 << 16, bytes_accessed=3 << 20),
        name="remote_pieces",
    )(queries, pages)


def local_kernel(qkv, pool, count, out):
    rows = 4 * PAD
    query = qkv[0:4].reshape(rows, HEAD)
    key, value = qkv[4], qkv[5]
    scores = dot_t(query, pool[:, :HEAD])
    live = count[...] > 0.0
    scores = jnp.where(live, scores, neg_large)
    fresh = dot_t(query, key)
    token = lax.broadcasted_iota(jnp.int32, fresh.shape, 0) % PAD
    col = lax.broadcasted_iota(jnp.int32, fresh.shape, 1)
    allowed = col <= token
    fresh = jnp.where(allowed, fresh, neg_large)
    peak = jnp.maximum(
        jnp.max(scores, axis=-1, keepdims=True), jnp.max(fresh, axis=-1, keepdims=True)
    )
    weights = jnp.where(live, jnp.exp(scores - peak) * count[...], 0.0)
    fresh = jnp.where(allowed, jnp.exp(fresh - peak), 0.0)
    denom = jnp.sum(weights, axis=-1, keepdims=True) + jnp.sum(fresh, axis=-1, keepdims=True)
    out[:, :HEAD] = dot_n(weights.astype(bf16), pool[:, HEAD:]) + dot_n(
        fresh.astype(bf16), value
    )
    out[:, HEAD : HEAD + 128] = jnp.broadcast_to(peak, (rows, 128))
    out[:, HEAD + 128 :] = jnp.broadcast_to(denom, (rows, 128))


def local_piece(qkv, pool, count):
    return pl.pallas_call(
        local_kernel,
        out_shape=jax.ShapeDtypeStruct((4 * PAD, 2 * HEAD), f32),
        compiler_params=pltpu.CompilerParams(vmem_limit_bytes=24 << 20),
        cost_estimate=pl.CostEstimate(flops=1 << 26, transcendentals=1 << 15, bytes_accessed=2 << 20),
        name="local_piece",
    )(qkv, pool, count)


def join_kernel(pieces, local, w_out, out, attn):
    @pl.when(pl.program_id(0) == 0)
    def _():
        groups = pieces.shape[0]
        peaks = [pieces[z, :, HEAD : HEAD + 1].astype(f32) for z in range(groups)]
        own = local[:, HEAD : HEAD + 1]
        top = functools.reduce(jnp.maximum, peaks, own)
        scale = jnp.exp(own - top)
        total = local[:, :HEAD] * scale
        denom = local[:, HEAD + 128 : HEAD + 129] * scale
        for z in range(groups):
            scale = jnp.exp(peaks[z] - top)
            total += pieces[z, :, :HEAD].astype(f32) * scale
            denom += scale * (
                pieces[z, :, HEAD + 32 : HEAD + 33].astype(f32)
                + pieces[z, :, HEAD + 64 : HEAD + 65].astype(f32)
            )
        attn[...] = total / denom

    acc = None
    for h in range(4):
        part = dot_n(
            attn[h * PAD : (h + 1) * PAD, :].astype(bf16), w_out[h * HEAD : (h + 1) * HEAD, :]
        )
        acc = part if acc is None else acc + part
    out[...] = acc


def join(pieces, local, w_out):
    depth, width = w_out.shape
    cols = 512
    return pl.pallas_call(
        join_kernel,
        grid=(width // cols,),
        in_specs=[
            pl.BlockSpec(pieces.shape, lambda i: (0, 0, 0)),
            pl.BlockSpec(local.shape, lambda i: (0, 0)),
            pl.BlockSpec((depth, cols), lambda i: (0, i)),
        ],
        out_specs=pl.BlockSpec((PAD, cols), lambda i: (0, i)),
        out_shape=jax.ShapeDtypeStruct((PAD, width), f32),
        scratch_shapes=[pltpu.VMEM((4 * PAD, HEAD), f32)],
        compiler_params=pltpu.CompilerParams(vmem_limit_bytes=24 << 20),
        cost_estimate=pl.CostEstimate(flops=1 << 25, transcendentals=0, bytes_accessed=4 << 20),
        name="join",
    )(pieces, local, w_out)


def finish_kernel(side, own, other, x, gain, out):
    half = out.shape[1]
    total = own[...].astype(f32) + other[...].astype(f32)
    scale = lax.rsqrt(jnp.mean(total * total, axis=-1, keepdims=True) + eps_norm)
    mine = jnp.where(side[0] == 0, total[:, :half], total[:, half:])
    out[...] = (x[...].astype(f32) + mine * scale * gain[...]).astype(bf16)


def finish(side, own, other, x, gain, name):
    rows, width = own.shape
    half = width // 2
    block = min(rows, 64)
    return pl.pallas_call(
        finish_kernel,
        grid_spec=pltpu.PrefetchScalarGridSpec(
            num_scalar_prefetch=1,
            grid=(rows // block,),
            in_specs=[
                pl.BlockSpec((block, width), lambda i, s: (i, 0)),
                pl.BlockSpec((block, width), lambda i, s: (i, 0)),
                pl.BlockSpec((block, half), lambda i, s: (i, s[0])),
                pl.BlockSpec((1, half), lambda i, s: (0, s[0])),
            ],
            out_specs=pl.BlockSpec((block, half), lambda i, s: (i, 0)),
        ),
        out_shape=jax.ShapeDtypeStruct((rows, half), bf16),
        cost_estimate=pl.CostEstimate(
            flops=8 * rows * width, transcendentals=0, bytes_accessed=6 * rows * width
        ),
        name=name,
    )(side, own, other, x, gain)


def on_device(
    plane,
    column,
    verify_x,
    prefill_x,
    attn_gain,
    w_query,
    w_keyval,
    qk_gain,
    w_out,
    post_gain,
    page_pool,
    outbound,
    page_table,
    cache_len,
    prompt_len,
    accepted,
):
    _, draft, width = verify_x.shape
    rows = prefill_x.shape[0]
    pool_pages = page_pool.shape[0]
    planes, depth = len(plane[0]), len(column[0])

    outgoing = pick_pages(page_pool, outbound[0])
    arrived = lax.all_to_all(
        outgoing, "req", 0, 0, tiled=True, axis_index_groups=plane
    )

    length = cache_len[0]
    slot_page = page_table[0]
    pages = pool_pages + planes * depth
    slots = slot_page.shape[0]
    offset = (
        jnp.arange(slots, dtype=jnp.int32)[:, None] * PAGE
        + jnp.arange(PAGE, dtype=jnp.int32)[None, :]
    )
    valid = (offset < length).astype(bf16)
    names = (slot_page[None, :] == jnp.arange(pages, dtype=jnp.int32)[:, None]).astype(bf16)
    counts = jnp.dot(names, valid, preferred_element_type=f32)
    own_count = counts[:pool_pages].reshape(1, pool_pages * PAGE)
    sent_count = (
        counts[pool_pages:]
        .reshape(planes, depth, PAGE)
        .transpose(1, 0, 2)
        .reshape(depth, 1, planes * PAGE)
        .astype(bf16)
    )

    lengths = prompt_len[0]
    ends = jnp.stack([lengths[0], lengths[0] + lengths[1], lengths[0] + lengths[1] + lengths[2]])
    row = jnp.arange(rows, dtype=jnp.int32)
    start = jnp.max(
        jnp.where(row[:, None] >= ends[None, :], ends[None, :], 0), axis=1
    )
    position = jnp.concatenate(
        [row - start, length + jnp.arange(PAD, dtype=jnp.int32)]
    ).astype(f32)
    half_dim = HEAD // 2
    inv_freq = rope_base ** (-(jnp.arange(half_dim, dtype=f32) * 2.0) / HEAD)
    angles = position[:, None] * inv_freq[None, :]
    cosine, sine = jnp.cos(angles), jnp.sin(angles)

    drafted = jnp.pad(verify_x[0], ((0, PAD - draft), (0, 0)))
    all_rows = jnp.concatenate([prefill_x, drafted], axis=0)
    qkv, prefill_kv = project(
        all_rows, attn_gain[None], w_query, w_keyval, qk_gain, cosine, sine, rows
    )
    draft_qkv = qkv[:, rows:]
    query = draft_qkv[:4].reshape(1, 4 * PAD, HEAD)
    mark = jnp.arange(4 * PAD, dtype=jnp.int32)[None, :, None] == draft
    queries = lax.all_to_all(
        jnp.where(mark, sent_count, query),
        "req", 0, 0, tiled=True, axis_index_groups=column,
    )

    own = local_piece(draft_qkv, page_pool.reshape(pool_pages * PAGE, -1), own_count)
    side = lax.axis_index("head").reshape(1)
    swap = [(0, 1), (1, 0)]
    partial = prompts(ends, qkv, w_out, rows)
    other = lax.ppermute(partial, "head", swap)
    prefill_out = finish(side, partial, other, prefill_x, post_gain[None], "finish_prompts")

    sent = remote_pieces(queries, arrived.reshape(planes, depth, PAGE, -1))
    pieces = lax.all_to_all(sent, "req", 0, 0, tiled=True, axis_index_groups=column)
    partial_v = join(pieces, own, w_out)
    other_v = lax.ppermute(partial_v, "head", swap)
    verify_out = finish(side, partial_v, other_v, drafted, post_gain[None], "finish_drafts")
    verify_out = verify_out[None, :draft]

    fresh = jnp.concatenate([draft_qkv[4, :draft], draft_qkv[5, :draft]], axis=-1)
    keep = jnp.arange(draft, dtype=jnp.int32)[:, None] < accepted[0]
    verify_kv = jnp.where(keep, fresh, jnp.zeros_like(fresh))[None]
    return (verify_out, prefill_out, verify_kv, prefill_kv)


def solution(mesh):
    devices = mesh.shape["req"]
    deep = 8
    plane = [[i for i in range(devices) if i % deep == z] for z in range(deep)]
    column = [list(range(i, i + deep)) for i in range(0, devices, deep)]
    placed = (
        P("req", None, None),
        P("req", None),
        P(),
        P(None, "head"),
        P(None, "head"),
        P(),
        P("head", None),
        P(),
        P("req", None, "head"),
        P("req", None),
        P("req", None),
        P("req"),
        P("req", None),
        P("req"),
    )
    return jax.shard_map(
        functools.partial(on_device, plane, column),
        mesh=mesh,
        in_specs=placed,
        out_specs=(
            P("req", None, "head"),
            P("req", "head"),
            P("req", None, "head"),
            P("req", "head"),
        ),
        check_vma=False,
    )
```

time: 139 us -> 101 us (0.73)
  Pallas kernels: 0 us -> 24.5 us
  waiting for transfers between devices: 47.9 us -> 25.5 us
  other arithmetic: 24.3 us -> 4.14 us
  matrix products: 13.3 us -> 0.89 us
  between operations: 15.7 us -> 4.22 us
  starting transfers between devices: 17.2 us -> 28.3 us
  local copies, waits for them, and re-layouts: 19.8 us -> 12.4 us
    pallas_call x0 -> x8, Pallas kernels: none -> 24.5 us  [the longest x2 5.43 us: finish(): pl.pallas_call(finish_kernel, grid_spec=pltpu.PrefetchScalarGridSpec(num_...]
    psum x1 -> x0, waiting for transfers between devices: 20.9 us -> none  [on_device(): summed = lax.psum(partial_rows, 'head')]
    dot_general x7 -> x1, matrix products: 13.3 us -> 0.89 us  [on_device(): counts = jnp.dot(names, valid, preferred_element_type=f32)]
    ppermute x0 -> x2, starting transfers between devices: none -> 9.14 us  [the longest x1 6.57 us: on_device(): other_v = lax.ppermute(partial_v, 'head', swap)]
    gather x3 -> x0, local copies, waits for them, and re-layouts: 7.02 us -> none  [the longest x2 3.76 us: verify_one(): cached = jnp.take(pool_now, page_list, axis=0).reshape(-1, groups, 2, HEAD)]
    unnamed x43 -> x20, local copies, waits for them, and re-layouts: 2.52 us -> 8.41 us
    reduce_sum x9 -> x0, other arithmetic: 5.28 us -> none  [the longest x5 4.76 us: rms_scale(): jnp.mean(values * values, axis=-1, keepdims=True) + eps_norm]
    select_n x5 -> x2, other arithmetic: 6.01 us -> 1.4 us  [the longest x1 0.74 us: on_device(): jnp.where(mark, sent_count, query)]
  transfers between devices with their start and end apart: 2 -> 5, of which waited for: 2 -> 3; matrix products, arithmetic and copies ran while one was open for 21% -> 1% of each run, Pallas kernels for 0% -> 18%
where the time goes in v1:
time: 101 us; the launch traced here: 100 us
  starting transfers between devices  28.3 us (28%)
  waiting for transfers between devices  25.5 us (25%)
  Pallas kernels  24.5 us (24%)
  local copies, waits for them, and re-layouts  12.4 us (12%)
  between operations  4.22 us (4%)
  other arithmetic  4.14 us (4%)
    all_to_all x1, waiting for transfers between devices, on_device(): lax.all_to_all(outgoing, 'req', 0, 0, tiled=True, axis_index_groups=plane)  15.8 us
    all_to_all x1, starting transfers between devices, on_device(): lax.all_to_all(jnp.where(mark, sent_count, query), 'req', 0, 0, tiled=Tru...  9.02 us
    unnamed x20, local copies, waits for them, and re-layouts  8.41 us
    all_to_all x1, starting transfers between devices, on_device(): lax.all_to_all(outgoing, 'req', 0, 0, tiled=True, axis_index_groups=plane)  6.75 us
    ppermute x1, starting transfers between devices, on_device(): other_v = lax.ppermute(partial_v, 'head', swap)  6.57 us
    all_to_all x1, waiting for transfers between devices, on_device(): lax.all_to_all(sent, 'req', 0, 0, tiled=True, axis_index_groups=column)  5.79 us
    pallas_call x2, Pallas kernels, finish(): pl.pallas_call(finish_kernel, grid_spec=pltpu.PrefetchScalarGridSpec(num_...  5.43 us
    pallas_call x1, Pallas kernels, project(): pl.pallas_call(project_kernel, grid=(6,), in_specs=[whole((count, width))...  5.33 us
  transfers between devices with their start and end apart: 5, of which 3 were waited for; matrix products, arithmetic and copies ran while one was open for 1% of the time, Pallas kernels for 18%

profile of v1, /device:TPU:1, one launch (start us, length us, event | category | flops | bytes accessed | tf_op | source)
XLA Modules:
  0.0 100.0 jit_solution(6873110211474535629)
XLA Ops:
  1.5 1.4 %fusion.5 = (s32[1,1]{1,0:T(1,128)}, s32[1,1]{1,0:T(1,128)}, s32[1,1]{1,0:T(1,128)}) fusion(s32[1,4]{1,0:T(1,128)} %param.26), kind=kLoop, calls=%fused_computation.25 | loop fusion | bytes 24 | tf_op jit(solution)/shard_map/slice | solution.py:367
  5.6 0.9 fusion
  6.9 0.8 pad.4.x
  8.2 1.3 %pad_maximum_fusion.x = bf16[264,2048]{1,0:T(8,128)(2,1)S(1)} fusion(bf16[8,2048]{1,0:T(8,128)(2,1)S(1)} %pad.4.x, bf16[256,2048]{1,0:T(8,128)(2,1)} %x.3), kind=kLoop, calls=%fused_computation | loop fusion | flops 2162688 | bytes 2162688 | tf_op jit(solution)/shard_map/concatenate | solution.py:381
  9.6 2.2 %copy-done.2 = bf16[2048,1024]{1,0:T(8,128)(2,1)S(1)} copy-done((bf16[2048,1024]{1,0:T(8,128)(2,1)S(1)}, bf16[2048,1024]{1,0:T(8,128)(2,1)}, u32[]{:S(2)}) %copy-start.2) | copy-done | bytes 4194328
  11.7 5.3 %project.1 = (bf16[6,264,256]{2,1,0:T(8,128)(2,1)S(1)}, bf16[256,512]{1,0:T(8,128)(2,1)}) custom-call(bf16[264,2048]{1,0:T(8,128)(2,1)S(1)} %pad_maximum_fusion.x, f32[1,2048]{1,0:T(1,128)S(1)} %bitcast.25, bf16[2048,1024]{1,0:T(8,128)(2,1)S(1)} %copy-done.2, bf16[2048,512]{1,0:T(8,128)(2,1)S(1)} %copy-done.4, f32[2,256]{1,0:T(2,128)S(1)} %copy-done.7, ...), custom_call_target="tpu_custom_call" | custom-call | flops 1660944384 | bytes 9437184 | tf_op jit(solution)/shard_map/project/pallas_call | solution.py:91
  17.8 9.0 %all-to-all-start = ((bf16[8,32,256]{2,1,0:T(8,128)(2,1)}), bf16[8,32,256]{2,1,0:T(8,128)(2,1)S(1)}, u32[]{:S(2)}, u32[]{:S(2)}) async-start(bf16[8,32,256]{2,1,0:T(8,128)(2,1)} %broadcast_select_fusion), calls=%async_computation | async-start | bytes 262144 | tf_op jit(solution)/shard_map/all_to_all | solution.py:388
  26.8 3.8 %pick_pages.1 = bf16[128,16,512]{2,1,0:T(8,128)(2,1)} custom-call(s32[128]{0:T(128)} %bitcast.30, bf16[64,16,512]{2,1,0:T(8,128)(2,1)} %pool.1), custom_call_target="tpu_custom_call" | custom-call | bytes 3145728 | tf_op jit(solution)/shard_map/pick_pages/pallas_call | solution.py:37
  30.7 3.9 %all-to-all-done.queries = bf16[8,32,256]{2,1,0:T(8,128)(2,1)S(1)} async-done(((bf16[8,32,256]{2,1,0:T(8,128)(2,1)}), bf16[8,32,256]{2,1,0:T(8,128)(2,1)S(1)}, u32[]{:S(2)}, u32[]{:S(2)}) %all-to-all-start) | async-done | bytes 131104 | tf_op jit(solution)/shard_map/all_to_all | solution.py:388
  34.6 6.8 %all-to-all-start.1 = ((bf16[128,16,512]{2,1,0:T(8,128)(2,1)}), bf16[128,16,512]{2,1,0:T(8,128)(2,1)S(1)}, u32[]{:S(2)}, u32[]{:S(2)}) async-start(bf16[128,16,512]{2,1,0:T(8,128)(2,1)} %pick_pages.1), calls=%async_computation.1 | async-start | bytes 4194304 | tf_op jit(solution)/shard_map/all_to_all | solution.py:342
  41.4 2.2 %copy-done = bf16[1024,2048]{1,0:T(8,128)(2,1)S(1)} copy-done((bf16[1024,2048]{1,0:T(8,128)(2,1)S(1)}, bf16[1024,2048]{1,0:T(8,128)(2,1)}, u32[]{:S(2)}) %copy-start) | copy-done | bytes 4194328
  43.6 4.7 %prompts.1.own = bf16[256,2048]{1,0:T(8,128)(2,1)} custom-call(s32[3]{0:T(128)S(1)} %pad_add_fusion.ends, bf16[6,264,256]{2,1,0:T(8,128)(2,1)S(1)} %get-tuple-element.6.q.k.v, bf16[6,264,256]{2,1,0:T(8,128)(2,1)S(1)} %get-tuple-element.6.q.k.v, bf16[6,264,256]{2,1,0:T(8,128)(2,1)S(1)} %get-tuple-element.6.q.k.v, bf16[1024,2048]{1,0:T(8,128)(2,1)S(1)} %copy-done), custom_call_target="tpu_custom_call" | custom-call | flops 1073741824 | bytes 6291456 | tf_op jit(solution)/shard_map/prompts/pallas_call | solution.py:145
  48.3 2.6 %collective-permute-start.1 = (bf16[256,2048]{1,0:T(8,128)(2,1)}, bf16[256,2048]{1,0:T(8,128)(2,1)}, u32[]{:S(2)}, u32[]{:S(2)}) collective-permute-start(bf16[256,2048]{1,0:T(8,128)(2,1)} %prompts.1.own), channel_id=1, source_target_pairs={{0,1},{1,0},{2,3},{3,2},{4,5},{5,4},{6,7},{7,6},{8,9},{9,8},{10,11... | collective-permute-start | bytes 3145736 | tf_op jit(solution)/shard_map/ppermute | solution.py:397
  50.8 15.8 %all-to-all-done.1 = bf16[128,16,512]{2,1,0:T(8,128)(2,1)S(1)} async-done(((bf16[128,16,512]{2,1,0:T(8,128)(2,1)}), bf16[128,16,512]{2,1,0:T(8,128)(2,1)S(1)}, u32[]{:S(2)}, u32[]{:S(2)}) %all-to-all-start.1) | async-done | bytes 2097184 | tf_op jit(solution)/shard_map/all_to_all | solution.py:342
  66.7 3.0 %remote_pieces.1 = bf16[8,32,384]{2,1,0:T(8,128)(2,1)} custom-call(bf16[8,32,256]{2,1,0:T(8,128)(2,1)S(1)} %all-to-all-done.queries, bf16[16,8,16,512]{3,2,1,0:T(8,128)(2,1)S(1)} %bitcast.23), custom_call_target="tpu_custom_call" | custom-call | flops 67108864 | bytes 3145728 | tf_op jit(solution)/shard_map/remote_pieces/pallas_call | solution.py:193
  69.6 3.4 %all-to-all-start.2 = ((bf16[8,32,384]{2,1,0:T(8,128)(2,1)}), bf16[8,32,384]{2,1,0:T(8,128)(2,1)S(1)}, u32[]{:S(2)}, u32[]{:S(2)}) async-start(bf16[8,32,384]{2,1,0:T(8,128)(2,1)} %remote_pieces.1), calls=%async_computation.2 | async-start | bytes 393216 | tf_op jit(solution)/shard_map/all_to_all | solution.py:401
  73.9 1.2 %copy-done.3 = bf16[64,16,512]{2,1,0:T(8,128)(2,1)S(1)} copy-done((bf16[64,16,512]{2,1,0:T(8,128)(2,1)S(1)}, bf16[64,16,512]{2,1,0:T(8,128)(2,1)}, u32[]{:S(2)}) %copy-start.3) | copy-done | bytes 1048600
  75.8 5.8 %all-to-all-done.2.pieces = bf16[8,32,384]{2,1,0:T(8,128)(2,1)S(1)} async-done(((bf16[8,32,384]{2,1,0:T(8,128)(2,1)}), bf16[8,32,384]{2,1,0:T(8,128)(2,1)S(1)}, u32[]{:S(2)}, u32[]{:S(2)}) %all-to-all-start.2) | async-done | bytes 196640 | tf_op jit(solution)/shard_map/all_to_all | solution.py:401
  81.6 2.2 %copy-done.1 = bf16[1024,2048]{1,0:T(8,128)(2,1)S(1)} copy-done((bf16[1024,2048]{1,0:T(8,128)(2,1)S(1)}, bf16[1024,2048]{1,0:T(8,128)(2,1)}, u32[]{:S(2)}) %copy-start.1) | copy-done | bytes 4194328
  83.8 1.6 %join.1.own = f32[8,2048]{1,0:T(8,128)S(1)} custom-call(bf16[8,32,384]{2,1,0:T(8,128)(2,1)S(1)} %all-to-all-done.2.pieces, f32[32,512]{1,0:T(8,128)S(1)} %local_piece.1.local, bf16[1024,2048]{1,0:T(8,128)(2,1)S(1)} %copy-done.1), custom_call_target="tpu_custom_call" | custom-call | flops 33554432 | bytes 4194304 | tf_op jit(solution)/shard_map/join/pallas_call | solution.py:268
  85.4 6.6 %collective-permute-start = (f32[8,2048]{1,0:T(8,128)S(1)}, f32[8,2048]{1,0:T(8,128)S(1)}, u32[]{:S(2)}, u32[]{:S(2)}) collective-permute-start(f32[8,2048]{1,0:T(8,128)S(1)} %join.1.own), channel_id=1, source_target_pairs={{0,1},{1,0},{2,3},{3,2},{4,5},{5,4},{6,7},{7,6},{8,9},{9,8},{10,11... | collective-permute-start | bytes 196616 | tf_op jit(solution)/shard_map/ppermute | solution.py:403
  92.6 3.8 %finish_prompts.1 = bf16[256,1024]{1,0:T(8,128)(2,1)} custom-call(s32[1]{0:T(128)} %bitcast.side, bf16[256,2048]{1,0:T(8,128)(2,1)} %prompts.1.own, bf16[256,2048]{1,0:T(8,128)(2,1)} %collective-permute-done.1.other, bf16[256,2048]{1,0:T(8,128)(2,1)} %x.3, f32[1,2048]{1,0:T(1,128)} %bitcast.27), custom_call_target="tpu_custom_call" | custom-call | flops 4194304 | bytes 3145728 | tf_op jit(solution)/shard_map/finish_prompts/pallas_call | solution.py:297
  97.1 1.6 %finish_drafts.1 = bf16[8,1024]{1,0:T(8,128)(2,1)} custom-call(s32[1]{0:T(128)} %bitcast.side, f32[8,2048]{1,0:T(8,128)} %copy-done.5, f32[8,2048]{1,0:T(8,128)} %copy-done.9, bf16[8,2048]{1,0:T(8,128)(2,1)} %copy-done.8, f32[1,2048]{1,0:T(1,128)} %bitcast.28), custom_call_target="tpu_custom_call" | custom-call | flops 131072 | bytes 98304 | tf_op jit(solution)/shard_map/finish_drafts/pallas_call | solution.py:297
  98.7 1.3 %slice_bitcast_fusion = bf16[1,5,1024]{2,1,0:T(8,128)(2,1)} fusion(bf16[8,1024]{1,0:T(8,128)(2,1)} %finish_drafts.1), kind=kLoop, calls=%fused_computation.8 | loop fusion | bytes 20480 | tf_op jit(solution)/shard_map/broadcast_in_dim | solution.py:405
  (41 shorter events, 4.6 us)
Async XLA Ops:
  0.6 8.9 %copy-start.7 = (f32[2,256]{1,0:T(2,128)S(1)}, f32[2,256]{1,0:T(2,128)}, u32[]{:S(2)}) copy-start(f32[2,256]{1,0:T(2,128)} %qk_gain.1) | copy-start | bytes 6148
  0.6 8.9 %copy-start.4 = (bf16[2048,512]{1,0:T(8,128)(2,1)S(1)}, bf16[2048,512]{1,0:T(8,128)(2,1)}, u32[]{:S(2)}) copy-start(bf16[2048,512]{1,0:T(8,128)(2,1)} %wkv.1) | copy-start | bytes 6291460
  0.7 8.9 %copy-start.6 = (f32[2048]{0:T(1024)S(1)}, f32[2048]{0:T(1024)}, u32[]{:S(2)}) copy-start(f32[2048]{0:T(1024)} %param.16) | copy-start | bytes 24580
  7.6 9.4 %copy-start.8 = (bf16[8,2048]{1,0:T(8,128)(2,1)}, bf16[8,2048]{1,0:T(8,128)(2,1)S(1)}, u32[]{:S(2)}) copy-start(bf16[8,2048]{1,0:T(8,128)(2,1)S(1)} %pad.4.x) | copy-start | bytes 98308
  9.6 2.2 %copy-start.2 = (bf16[2048,1024]{1,0:T(8,128)(2,1)S(1)}, bf16[2048,1024]{1,0:T(8,128)(2,1)}, u32[]{:S(2)}) copy-start(bf16[2048,1024]{1,0:T(8,128)(2,1)} %wq.1) | copy-start | bytes 12582916
  17.8 16.8 %all-to-all-start = ((bf16[8,32,256]{2,1,0:T(8,128)(2,1)}), bf16[8,32,256]{2,1,0:T(8,128)(2,1)S(1)}, u32[]{:S(2)}, u32[]{:S(2)}) async-start(bf16[8,32,256]{2,1,0:T(8,128)(2,1)} %broadcast_select_fusion), calls=%async_computation | async-start | bytes 262144 | tf_op jit(solution)/shard_map/all_to_all | solution.py:388
  34.6 32.0 %all-to-all-start.1 = ((bf16[128,16,512]{2,1,0:T(8,128)(2,1)}), bf16[128,16,512]{2,1,0:T(8,128)(2,1)S(1)}, u32[]{:S(2)}, u32[]{:S(2)}) async-start(bf16[128,16,512]{2,1,0:T(8,128)(2,1)} %pick_pages.1), calls=%async_computation.1 | async-start | bytes 4194304 | tf_op jit(solution)/shard_map/all_to_all | solution.py:342
  41.4 2.2 %copy-start = (bf16[1024,2048]{1,0:T(8,128)(2,1)S(1)}, bf16[1024,2048]{1,0:T(8,128)(2,1)}, u32[]{:S(2)}) copy-start(bf16[1024,2048]{1,0:T(8,128)(2,1)} %w_out.3) | copy-start | bytes 12582916
  48.3 44.3 %collective-permute-start.1 = (bf16[256,2048]{1,0:T(8,128)(2,1)}, bf16[256,2048]{1,0:T(8,128)(2,1)}, u32[]{:S(2)}, u32[]{:S(2)}) collective-permute-start(bf16[256,2048]{1,0:T(8,128)(2,1)} %prompts.1.own), channel_id=1, source_target_pairs={{0,1},{1,0},{2,3},{3,2},{4,5},{5,4},{6,7},{7,6},{8,9},{9,8},{10,11... | collective-permute-start | bytes 3145736 | tf_op jit(solution)/shard_map/ppermute | solution.py:397
  69.6 11.9 %all-to-all-start.2 = ((bf16[8,32,384]{2,1,0:T(8,128)(2,1)}), bf16[8,32,384]{2,1,0:T(8,128)(2,1)S(1)}, u32[]{:S(2)}, u32[]{:S(2)}) async-start(bf16[8,32,384]{2,1,0:T(8,128)(2,1)} %remote_pieces.1), calls=%async_computation.2 | async-start | bytes 393216 | tf_op jit(solution)/shard_map/all_to_all | solution.py:401
  73.9 1.2 %copy-start.3 = (bf16[64,16,512]{2,1,0:T(8,128)(2,1)S(1)}, bf16[64,16,512]{2,1,0:T(8,128)(2,1)}, u32[]{:S(2)}) copy-start(bf16[64,16,512]{2,1,0:T(8,128)(2,1)} %pool.1) | copy-start | bytes 3145732
  81.6 2.2 %copy-start.1 = (bf16[1024,2048]{1,0:T(8,128)(2,1)S(1)}, bf16[1024,2048]{1,0:T(8,128)(2,1)}, u32[]{:S(2)}) copy-start(bf16[1024,2048]{1,0:T(8,128)(2,1)} %w_out.3) | copy-start | bytes 12582916
  85.4 11.1 %copy-start.5 = (f32[8,2048]{1,0:T(8,128)}, f32[8,2048]{1,0:T(8,128)S(1)}, u32[]{:S(2)}) copy-start(f32[8,2048]{1,0:T(8,128)S(1)} %join.1.own) | copy-start | bytes 196612
  85.4 11.1 %collective-permute-start = (f32[8,2048]{1,0:T(8,128)S(1)}, f32[8,2048]{1,0:T(8,128)S(1)}, u32[]{:S(2)}, u32[]{:S(2)}) collective-permute-start(f32[8,2048]{1,0:T(8,128)S(1)} %join.1.own), channel_id=1, source_target_pairs={{0,1},{1,0},{2,3},{3,2},{4,5},{5,4},{6,7},{7,6},{8,9},{9,8},{10,11... | collective-permute-start | bytes 196616 | tf_op jit(solution)/shard_map/ppermute | solution.py:403
  96.5 0.6 copy-start.9

commit v2 on v0

v2 whole, which is shorter than its diff:
```python
import functools

import jax
import jax.numpy as jnp
from jax import lax
from jax.experimental import pallas as pl
from jax.experimental.pallas import tpu as pltpu
from jax.sharding import PartitionSpec as P

HEAD = 256
PAGE = 16
QH = 4
PAD = 8
DEEP = 8
eps_norm = 1e-06
rope_base = 1000000.0
neg_large = -1e30
bf16, f32, i32 = jnp.bfloat16, jnp.float32, jnp.int32
HBM = pl.BlockSpec(memory_space=pltpu.MemorySpace.HBM)
VMEM = pl.BlockSpec(memory_space=pltpu.MemorySpace.VMEM)
SMEM = pl.BlockSpec(memory_space=pltpu.MemorySpace.SMEM)


def dot_t(a, b):
    return lax.dot_general(a, b, (((1,), (1,)), ((), ())), preferred_element_type=f32)


def dot_n(a, b):
    return jnp.dot(a, b, preferred_element_type=f32)


def iota(shape, dim):
    return lax.broadcasted_iota(i32, shape, dim)


def unit(values):
    return values * lax.rsqrt(jnp.mean(values * values, axis=-1, keepdims=True) + eps_norm)


def pick_kernel(index, pool, out, sem):
    def send(i, carry):
        page = jnp.clip(index[0, i], 0, pool.shape[0] - 1)
        pltpu.make_async_copy(pool.at[page], out.at[i], sem).start()
        return carry

    lax.fori_loop(0, out.shape[0], send, 0, unroll=8)
    pltpu.make_async_copy(out, out, sem).wait()


def pick_pages(index, pool):
    count = index.shape[1]
    return pl.pallas_call(
        pick_kernel,
        in_specs=[SMEM, HBM],
        out_specs=HBM,
        out_shape=jax.ShapeDtypeStruct((count,) + pool.shape[1:], pool.dtype),
        scratch_shapes=[pltpu.SemaphoreType.DMA],
        cost_estimate=pl.CostEstimate(flops=0, transcendentals=0, bytes_accessed=4 << 20),
        name="pick_pages",
    )(index, pool)


def project_kernel(
    length, accepted, x, draft, gain, wq, wkv, qk_gain, cosine, sine, table,
    queries, prompt_kv, sent, draft_kv, own_count, verify_kv,
    weights, normed, wide, rows_q, sems,
):
    rows, drafted = x.shape[0], draft.shape[1]
    copies = []
    for h in range(QH + 2):
        part = wq if h < QH else wkv
        col = (h if h < QH else h - QH) * HEAD
        copy = pltpu.make_async_copy(part.at[:, col : col + HEAD], weights.at[h], sems.at[h])
        copy.start()
        copies.append(copy)

    normed[:rows] = (unit(x[...].astype(f32)) * gain[...]).astype(bf16)
    wide[...] = jnp.zeros_like(wide)
    wide[:drafted] = unit(draft[0].astype(f32)) * gain[...]
    normed[rows:] = wide[...].astype(bf16)

    slots = table.shape[1]
    eye = iota((slots, slots), 0) == iota((slots, slots), 1)
    page = jnp.sum(jnp.where(eye, table[...], 0), axis=1, keepdims=True)
    base = iota((slots, 1), 0) * PAGE

    def tally(lanes, first, step):
        lane = iota((slots, lanes), 1)
        named = page == first + (lane // PAGE) * step
        valid = base + lane % PAGE < length[0]
        return jnp.sum(jnp.where(named & valid, 1.0, 0.0), axis=0, keepdims=True)

    own = own_count.shape[1]
    own_count[...] = tally(own, 0, 1)
    far = [tally(HEAD, own // PAGE + z, DEEP) for z in range(DEEP)]

    half = HEAD // 2
    cos, sin = cosine[...], sine[...]

    def rotated(values):
        a, b = values[:, :half], values[:, half:]
        return jnp.concatenate([a * cos - b * sin, b * cos + a * sin], axis=-1)

    row = iota((PAD, HEAD), 0)
    for h in range(QH):
        copies[h].wait()
        query = rotated(unit(dot_n(normed[...], weights[h])) * qk_gain[0:1, :])
        queries[h] = query[:rows].astype(bf16)
        mine = query[rows : rows + PAD]
        mine = jnp.where(row == drafted, far[h], mine)
        mine = jnp.where(row == drafted + 1, far[h + QH], mine)
        rows_q[h * PAD : (h + 1) * PAD, :] = mine
    sent[...] = rows_q[...].astype(bf16)

    keep = iota((PAD, HEAD), 0) < accepted[0]
    for part in range(2):
        copies[QH + part].wait()
        value = unit(dot_n(normed[...], weights[QH + part]))
        if part == 0:
            value = rotated(value * qk_gain[1:2, :])
        cols = slice(part * HEAD, (part + 1) * HEAD)
        prompt_kv[:, cols] = value[:rows].astype(bf16)
        mine = value[rows : rows + PAD]
        draft_kv[:, cols] = mine
        verify_kv[0, :, cols] = jnp.where(keep, mine, 0.0)[:drafted].astype(bf16)


def project(length, accepted, x, draft, gain, wq, wkv, qk_gain, cosine, sine, table, own):
    rows, width = x.shape
    drafted = draft.shape[1]
    total = rows + 16
    shapes = [
        jax.ShapeDtypeStruct((QH, rows, HEAD), bf16),
        jax.ShapeDtypeStruct((rows, 2 * HEAD), bf16),
        jax.ShapeDtypeStruct((QH * PAD, HEAD), bf16),
        jax.ShapeDtypeStruct((PAD, 2 * HEAD), f32),
        jax.ShapeDtypeStruct((1, own), f32),
        jax.ShapeDtypeStruct((1, drafted, 2 * HEAD), bf16),
    ]
    return pl.pallas_call(
        project_kernel,
        in_specs=[SMEM, SMEM, VMEM, VMEM, VMEM, HBM, HBM, VMEM, VMEM, VMEM, VMEM],
        out_specs=[VMEM] * len(shapes),
        out_shape=shapes,
        scratch_shapes=[
            pltpu.VMEM((QH + 2, width, HEAD), bf16),
            pltpu.VMEM((total, width), bf16),
            pltpu.VMEM((16, width), f32),
            pltpu.VMEM((QH * PAD, HEAD), f32),
            pltpu.SemaphoreType.DMA((QH + 2,)),
        ],
        compiler_params=pltpu.CompilerParams(vmem_limit_bytes=24 << 20),
        cost_estimate=pl.CostEstimate(
            flops=2 * total * width * 6 * HEAD, transcendentals=0, bytes_accessed=9 << 20
        ),
        name="project",
    )(length, accepted, x, draft, gain, wq, wkv, qk_gain, cosine, sine, table)


def prompt_kernel(
    lengths, q, kv, w_out, query, draft_kv, pool, count, out, local, attn, weights, sem
):
    copy = pltpu.make_async_copy(w_out, weights, sem)
    copy.start()
    rows = attn.shape[0]
    row, col = iota((rows, rows), 0), iota((rows, rows), 1)
    start = jnp.zeros((rows, rows), i32)
    end = jnp.int32(0)
    for i in range(3):
        end = end + lengths[0, i]
        start = jnp.where(row >= end, end, start)
    allowed = (col <= row) & (col >= start)
    key, value = kv[:, :HEAD], kv[:, HEAD:]
    for h in range(QH):
        scores = jnp.where(allowed, dot_t(q[h], key), neg_large)
        parts = jnp.exp(scores - jnp.max(scores, axis=-1, keepdims=True))
        probs = (parts / jnp.sum(parts, axis=-1, keepdims=True)).astype(bf16)
        attn[:, h * HEAD : (h + 1) * HEAD] = dot_n(probs, value).astype(bf16)

    mine = query[...]
    times = count[...]
    scores = jnp.where(times > 0.0, dot_t(mine, pool[:, :HEAD]), neg_large)
    fresh = dot_t(mine, draft_kv[:, :HEAD].astype(bf16))
    allowed = iota(fresh.shape, 1) <= iota(fresh.shape, 0) % PAD
    fresh = jnp.where(allowed, fresh, neg_large)
    peak = jnp.maximum(
        jnp.max(scores, axis=-1, keepdims=True), jnp.max(fresh, axis=-1, keepdims=True)
    )
    parts = jnp.where(times > 0.0, jnp.exp(scores - peak) * times, 0.0)
    fresh = jnp.where(allowed, jnp.exp(fresh - peak), 0.0)
    denom = jnp.sum(parts, axis=-1, keepdims=True) + jnp.sum(fresh, axis=-1, keepdims=True)
    local[:, :HEAD] = dot_n(parts.astype(bf16), pool[:, HEAD:]) + dot_n(
        fresh.astype(bf16), draft_kv[:, HEAD:].astype(bf16)
    )
    local[:, HEAD : HEAD + 128] = jnp.broadcast_to(peak, (QH * PAD, 128))
    local[:, HEAD + 128 :] = jnp.broadcast_to(denom, (QH * PAD, 128))

    copy.wait()
    cols = 512
    for i in range(out.shape[1] // cols):
        part = slice(i * cols, (i + 1) * cols)
        out[:, part] = dot_n(attn[...], weights[:, part]).astype(bf16)


def prompts(lengths, q, kv, w_out, query, draft_kv, pool, count):
    rows = kv.shape[0]
    depth, width = w_out.shape
    return pl.pallas_call(
        prompt_kernel,
        in_specs=[SMEM, VMEM, VMEM, HBM, VMEM, VMEM, VMEM, VMEM],
        out_specs=[VMEM, VMEM],
        out_shape=[
            jax.ShapeDtypeStruct((rows, width), bf16),
            jax.ShapeDtypeStruct((QH * PAD, 2 * HEAD), f32),
        ],
        scratch_shapes=[
            pltpu.VMEM((rows, depth), bf16),
            pltpu.VMEM((depth, width), bf16),
            pltpu.SemaphoreType.DMA,
        ],
        compiler_params=pltpu.CompilerParams(vmem_limit_bytes=24 << 20),
        cost_estimate=pl.CostEstimate(
            flops=2 * rows * depth * width, transcendentals=4 * rows * rows, bytes_accessed=6 << 20
        ),
        name="prompts",
    )(lengths, q, kv, w_out, query, draft_kv, pool, count)


def remote_kernel(where, queries, pages, out):
    here = where[0]
    groups, rows = queries.shape[0], queries.shape[1]
    pick = iota((rows, HEAD), 0) == (here % QH) * PAD + 5 + here // QH
    asked = [here ^ mask for mask in ORDER]
    scores, counts = [], []
    for e in range(groups):
        query = queries[e]
        count = jnp.sum(jnp.where(pick, query.astype(f32), 0.0), axis=0, keepdims=True)
        held = pages[:, asked[e], :, :HEAD].reshape(HEAD, HEAD)
        scores.append(jnp.where(count > 0.0, dot_t(query, held), neg_large))
        counts.append(jnp.broadcast_to(count, (rows, HEAD)))
    score = jnp.concatenate(scores, axis=0)
    count = jnp.concatenate(counts, axis=0)
    peak = jnp.max(score, axis=-1, keepdims=True).astype(bf16).astype(f32)
    parts = jnp.where(count > 0.0, jnp.exp(score - peak) * count, 0.0)
    denom = jnp.sum(parts, axis=-1, keepdims=True)
    high = denom.astype(bf16).astype(f32)
    lane = iota((groups * rows, 128), 1)
    stats = jnp.where(lane < 32, peak, jnp.where(lane < 64, high, denom - high)).astype(bf16)
    parts = parts.astype(bf16)
    for e in range(groups):
        own = slice(e * rows, (e + 1) * rows)
        held = pages[:, asked[e], :, HEAD:].reshape(HEAD, HEAD)
        out[asked[e], :, :HEAD] = dot_n(parts[own], held).astype(bf16)
        out[asked[e], :, HEAD:] = stats[own]


ORDER = (0, 4, 2, 6, 1, 5, 3, 7)


def remote_pieces(where, queries, pages):
    groups, rows, _ = queries.shape
    return pl.pallas_call(
        remote_kernel,
        in_specs=[SMEM, VMEM, VMEM],
        out_specs=VMEM,
        out_shape=jax.ShapeDtypeStruct((groups, rows, HEAD + 128), bf16),
        compiler_params=pltpu.CompilerParams(vmem_limit_bytes=12 << 20),
        cost_estimate=pl.CostEstimate(flops=1 << 26, transcendentals=1 << 16, bytes_accessed=3 << 20),
        name="remote_pieces",
    )(where, queries, pages)


def join_kernel(pieces, local, w_out, out, attn, weights, sems):
    depth, width = w_out.shape
    parts = sems.shape[0]
    cols = width // parts
    copies = []
    for i in range(parts):
        part = slice(i * cols, (i + 1) * cols)
        copy = pltpu.make_async_copy(w_out.at[:, part], weights.at[:, part], sems.at[i])
        copy.start()
        copies.append(copy)
    groups = pieces.shape[0]
    peaks = [pieces[z, :, HEAD : HEAD + 1].astype(f32) for z in range(groups)]
    own = local[:, HEAD : HEAD + 1]
    top = functools.reduce(jnp.maximum, peaks, own)
    scale = jnp.exp(own - top)
    total = local[:, :HEAD] * scale
    denom = local[:, HEAD + 128 : HEAD + 129] * scale
    for z in range(groups):
        scale = jnp.exp(peaks[z] - top)
        total += pieces[z, :, :HEAD].astype(f32) * scale
        denom += scale * (
            pieces[z, :, HEAD + 32 : HEAD + 33].astype(f32)
            + pieces[z, :, HEAD + 64 : HEAD + 65].astype(f32)
        )
    attn[...] = total / denom
    heads = [attn[h * PAD : (h + 1) * PAD, :].astype(bf16) for h in range(QH)]
    for i in range(parts):
        copies[i].wait()
        part = slice(i * cols, (i + 1) * cols)
        out[:, part] = functools.reduce(
            jnp.add,
            [dot_n(heads[h], weights[h * HEAD : (h + 1) * HEAD, part]) for h in range(QH)],
        )


def join(pieces, local, w_out):
    depth, width = w_out.shape
    return pl.pallas_call(
        join_kernel,
        in_specs=[VMEM, VMEM, HBM],
        out_specs=VMEM,
        out_shape=jax.ShapeDtypeStruct((PAD, width), f32),
        scratch_shapes=[
            pltpu.VMEM((QH * PAD, HEAD), f32),
            pltpu.VMEM((depth, width), bf16),
            pltpu.SemaphoreType.DMA((4,)),
        ],
        compiler_params=pltpu.CompilerParams(vmem_limit_bytes=12 << 20),
        cost_estimate=pl.CostEstimate(flops=1 << 25, transcendentals=0, bytes_accessed=4 << 20),
        name="join",
    )(pieces, local, w_out)


def finish_kernel(side, own, other, x, gain, out):
    half = out.shape[-1]
    total = own[...].astype(f32) + other[...].astype(f32)
    scale = lax.rsqrt(jnp.mean(total * total, axis=-1, keepdims=True) + eps_norm)
    mine = jnp.where(side[0] == 0, total[:, :half], total[:, half:]) * scale * gain[...]
    if len(out.shape) == 3:
        out[0] = (x[0].astype(f32) + mine[: out.shape[1]]).astype(bf16)
    else:
        out[...] = (x[...].astype(f32) + mine).astype(bf16)


def finish(side, own, other, x, gain, name):
    rows, width = own.shape
    half = width // 2
    block = min(rows, 128)
    if x.ndim == 3:
        shape = x.shape[:2] + (half,)
        x_spec = pl.BlockSpec(shape, lambda i, s: (0, 0, s[0]))
        o_spec = pl.BlockSpec(shape, lambda i, s: (0, 0, 0))
    else:
        shape = (rows, half)
        x_spec = pl.BlockSpec((block, half), lambda i, s: (i, s[0]))
        o_spec = pl.BlockSpec((block, half), lambda i, s: (i, 0))
    return pl.pallas_call(
        finish_kernel,
        grid_spec=pltpu.PrefetchScalarGridSpec(
            num_scalar_prefetch=1,
            grid=(rows // block,),
            in_specs=[
                pl.BlockSpec((block, width), lambda i, s: (i, 0)),
                pl.BlockSpec((block, width), lambda i, s: (i, 0)),
                x_spec,
                pl.BlockSpec((1, half), lambda i, s: (0, s[0])),
            ],
            out_specs=o_spec,
        ),
        out_shape=jax.ShapeDtypeStruct(shape, bf16),
        compiler_params=pltpu.CompilerParams(vmem_limit_bytes=12 << 20),
        cost_estimate=pl.CostEstimate(
            flops=8 * rows * width, transcendentals=0, bytes_accessed=6 * rows * width
        ),
        name=name,
    )(side, own, other, x, gain)


def on_device(
    plane,
    verify_x,
    prefill_x,
    attn_gain,
    w_query,
    w_keyval,
    qk_gain,
    w_out,
    post_gain,
    page_pool,
    outbound,
    page_table,
    cache_len,
    prompt_len,
    accepted,
):
    devices = outbound.shape[1]
    rows = prefill_x.shape[0]
    pool_pages = page_pool.shape[0]
    planes = len(plane[0])
    column = [list(range(i, i + DEEP)) for i in range(0, devices, DEEP)]

    outgoing = pick_pages(outbound, page_pool)
    outgoing, prefill_x = lax.optimization_barrier((outgoing, prefill_x))
    arrived = lax.all_to_all(outgoing, "req", 0, 0, tiled=True, axis_index_groups=plane)

    lengths = prompt_len[0]
    order = jnp.arange(3, dtype=i32)[:, None] >= jnp.arange(4, dtype=i32)[None, :]
    ends = jnp.sum(jnp.where(order, lengths[None, :], 0), axis=1)
    row = jnp.arange(rows, dtype=i32)
    start = jnp.max(jnp.where(row[:, None] >= ends[None, :], ends[None, :], 0), axis=1)
    position = jnp.concatenate(
        [row - start, cache_len[0] + jnp.arange(16, dtype=i32)]
    ).astype(f32)
    inv_freq = rope_base ** (-(jnp.arange(HEAD // 2, dtype=f32) * 2.0) / HEAD)
    angles = position[:, None] * inv_freq[None, :]

    queries, prefill_kv, sent, draft_kv, own_count, verify_kv = project(
        cache_len, accepted, prefill_x, verify_x, attn_gain[None], w_query, w_keyval,
        qk_gain, jnp.cos(angles), jnp.sin(angles), page_table, pool_pages * PAGE,
    )

    asked = sent[None]
    for mask in (4, 2, 1):
        pairs = [(i, i ^ mask) for i in range(devices)]
        asked = jnp.concatenate([asked, lax.ppermute(asked, "req", pairs)], axis=0)

    side = lax.axis_index("head").reshape(1)
    where = (lax.axis_index("req") % DEEP).reshape(1)
    swap = [(0, 1), (1, 0)]
    partial, own = prompts(
        prompt_len, queries, prefill_kv, w_out, sent, draft_kv,
        page_pool.reshape(pool_pages * PAGE, -1), own_count,
    )
    other = lax.ppermute(partial, "head", swap)
    prefill_out = finish(side, partial, other, prefill_x, post_gain[None], "finish_prompts")

    arrived, prefill_out = lax.optimization_barrier((arrived, prefill_out))
    pieces = remote_pieces(where, asked, arrived.reshape(planes, DEEP, PAGE, -1))
    pieces = lax.all_to_all(pieces, "req", 0, 0, tiled=True, axis_index_groups=column)
    partial = join(pieces, own, w_out)
    other = lax.ppermute(partial, "head", swap)
    verify_out = finish(side, partial, other, verify_x, post_gain[None], "finish_drafts")
    return (verify_out, prefill_out, verify_kv, prefill_kv)


def solution(mesh):
    devices = mesh.shape["req"]
    plane = [list(range(z, devices, DEEP)) for z in range(DEEP)]
    placed = (
        P("req", None, None),
        P("req", None),
        P(),
        P(None, "head"),
        P(None, "head"),
        P(),
        P("head", None),
        P(),
        P("req", None, "head"),
        P("req", None),
        P("req", None),
        P("req"),
        P("req", None),
        P("req"),
    )
    return jax.shard_map(
        functools.partial(on_device, plane),
        mesh=mesh,
        in_specs=placed,
        out_specs=(
            P("req", None, "head"),
            P("req", "head"),
            P("req", None, "head"),
            P("req", "head"),
        ),
        check_vma=False,
    )
```

time: 139 us -> 138 us (level)
  Pallas kernels: 0 us -> 83.3 us
  waiting for transfers between devices: 47.9 us -> 8.06 us
  other arithmetic: 24.3 us -> 0.82 us
  blocking collectives: 0 us -> 14.6 us
  between operations: 15.7 us -> 2.18 us
  matrix products: 13.3 us -> 0 us
  local copies, waits for them, and re-layouts: 19.8 us -> 6.96 us
  starting transfers between devices: 17.2 us -> 22.1 us
    pallas_call x0 -> x7, Pallas kernels: none -> 83.3 us  [the longest x1 65.3 us: pick_pages(): pl.pallas_call(pick_kernel, in_specs=[SMEM, HBM], out_specs=HBM, out_shap...]
    all_to_all x1, waiting for transfers between devices: 27 us -> 0.01 us  [on_device(): lax.all_to_all(outgoing, 'req', 0, 0, tiled=True, axis_index_groups=plane)]
    psum x1 -> x0, waiting for transfers between devices: 20.9 us -> none  [on_device(): summed = lax.psum(partial_rows, 'head')]
    all_to_all x0 -> x1, blocking collectives: none -> 14.6 us  [on_device(): lax.all_to_all(pieces, 'req', 0, 0, tiled=True, axis_index_groups=column)]
    ppermute x0 -> x5, starting transfers between devices: none -> 14.4 us  [the longest x3 8.39 us: on_device(): asked = jnp.concatenate([asked, lax.ppermute(asked, 'req', pairs)], axis=0)]
    dot_general x7 -> x0, matrix products: 13.3 us -> none  [the longest x1 4.91 us: on_device(): partial_rows = jnp.dot(all_attn, w_out, preferred_element_type=jnp.float32)]
    all_to_all x1, starting transfers between devices: 17 us -> 7.73 us  [on_device(): lax.all_to_all(outgoing, 'req', 0, 0, tiled=True, axis_index_groups=plane)]
    ppermute x0 -> x5, waiting for transfers between devices: none -> 8.06 us  [the longest x3 7.15 us: on_device(): asked = jnp.concatenate([asked, lax.ppermute(asked, 'req', pairs)], axis=0)]
  transfers between devices with their start and end apart: 2 -> 6, of which waited for: 2 -> 4; matrix products, arithmetic and copies ran while one was open for 21% -> 1% of each run, Pallas kernels for 0% -> 10%
where the time goes in v2:
time: 138 us
  Pallas kernels  83.3 us (60%)
  starting transfers between devices  22.1 us (16%)
  blocking collectives  14.6 us (11%)
  waiting for transfers between devices  8.06 us (6%)
  local copies, waits for them, and re-layouts  6.96 us (5%)
  between operations  2.18 us (2%)
    pallas_call x1, Pallas kernels, pick_pages(): pl.pallas_call(pick_kernel, in_specs=[SMEM, HBM], out_specs=HBM, out_shap...  65.3 us
    all_to_all x1, blocking collectives, on_device(): lax.all_to_all(pieces, 'req', 0, 0, tiled=True, axis_index_groups=column)  14.6 us
    ppermute x3, starting transfers between devices, on_device(): asked = jnp.concatenate([asked, lax.ppermute(asked, 'req', pairs)], axis=0)  8.39 us
    all_to_all x1, starting transfers between devices, on_device(): lax.all_to_all(outgoing, 'req', 0, 0, tiled=True, axis_index_groups=plane)  7.73 us
    ppermute x3, waiting for transfers between devices, on_device(): asked = jnp.concatenate([asked, lax.ppermute(asked, 'req', pairs)], axis=0)  7.15 us
    unnamed x26, local copies, waits for them, and re-layouts  6.96 us
    pallas_call x1, Pallas kernels, project(): pl.pallas_call(project_kernel, in_specs=[SMEM, SMEM, VMEM, VMEM, VMEM, HB...  6.91 us
    ppermute x2, starting transfers between devices, on_device(): other = lax.ppermute(partial, 'head', swap)  5.97 us
  transfers between devices with their start and end apart: 6, of which 4 were waited for; matrix products, arithmetic and copies ran while one was open for 1% of the time, Pallas kernels for 10%

profile of v2, /device:TPU:1, one launch (start us, length us, event | category | flops | bytes accessed | tf_op | source)
XLA Modules:
  0.0 138.0 jit_solution(7711582543767215187)
XLA Ops:
  0.6 65.3 %pick_pages.1 = bf16[128,16,512]{2,1,0:T(8,128)(2,1)} custom-call(s32[1,128]{1,0:T(1,128)} %index.1, bf16[64,16,512]{2,1,0:T(8,128)(2,1)} %pool.1), custom_call_target="tpu_custom_call" | custom-call | bytes 4194304 | tf_op jit(solution)/shard_map/pick_pages/pallas_call | solution.py:52
  66.0 7.7 %all-to-all-start = ((bf16[128,16,512]{2,1,0:T(8,128)(2,1)}), bf16[128,16,512]{2,1,0:T(8,128)(2,1)S(1)}, u32[]{:S(2)}, u32[]{:S(2)}) async-start(bf16[128,16,512]{2,1,0:T(8,128)(2,1)} %pick_pages.1), calls=%async_computation | async-start | bytes 4194304 | tf_op jit(solution)/shard_map/all_to_all | solution.py:396
  74.4 0.1 select_reduce_fusion.1
  75.3 0.6 multiply_sine_fusion
  76.0 2.2 %copy-done.2 = bf16[2048,1024]{1,0:T(8,128)(2,1)S(1)} copy-done((bf16[2048,1024]{1,0:T(8,128)(2,1)S(1)}, bf16[2048,1024]{1,0:T(8,128)(2,1)}, u32[]{:S(2)}) %copy-start.2) | copy-done | bytes 4194328
  78.1 1.6 %copy-done.5 = bf16[2048,512]{1,0:T(8,128)(2,1)S(1)} copy-done((bf16[2048,512]{1,0:T(8,128)(2,1)S(1)}, bf16[2048,512]{1,0:T(8,128)(2,1)}, u32[]{:S(2)}) %copy-start.5) | copy-done | bytes 2097176
  79.7 6.9 %project.1 = (bf16[4,256,256]{2,1,0:T(8,128)(2,1)S(1)}, bf16[256,512]{1,0:T(8,128)(2,1)}, bf16[32,256]{1,0:T(8,128)(2,1)S(1)}, f32[8,512]{1,0:T(8,128)S(1)}, f32...) custom-call(s32[1]{0:T(128)} %copy.18.length, s32[1]{0:T(128)S(6)} %copy.19.accepted, bf16[256,2048]{1,0:T(8,128)(2,1)S(1)} %copy-done.4, ...), custom_call_target="tpu_custom_call" | custom-call | flops 1711276032 | bytes 9437184 | tf_op jit(solution)/shard_map/project/pallas_call | solution.py:140
  86.7 0.9 copy-done.6
  87.6 4.7 %prompts.1 = (bf16[256,2048]{1,0:T(8,128)(2,1)}, f32[32,512]{1,0:T(8,128)S(1)}) custom-call(s32[1,4]{1,0:T(1,128)S(1)} %copy-done.12, bf16[4,256,256]{2,1,0:T(8,128)(2,1)S(1)} %get-tuple-element.19.q, bf16[256,512]{1,0:T(8,128)(2,1)S(1)} %copy-done.6, bf16[1024,2048]{1,0:T(8,128)(2,1)S(1)} %copy-done, bf16[32,256]{1,0:T(8,128)(2,1)S(1)} %get-tuple-element.17.query, ...), custom_call_target="tpu_custom_call" | custom-call | flops 1073741824 | bytes 6291456 | tf_op jit(solution)/shard_map/prompts/pallas_call | solution.py:208
  92.3 1.0 collective-permute-start.3
  93.4 6.9 %collective-permute-start = (bf16[1,32,256]{2,1,0:T(8,128)(2,1)S(1)}, bf16[1,32,256]{2,1,0:T(8,128)(2,1)S(1)}, u32[]{:S(2)}, u32[]{:S(2)}) collective-permute-start(bf16[1,32,256]{2,1,0:T(8,128)(2,1)S(1)} %bitcast.12), channel_id=1, source_target_pairs={{0,8},{2,10},{4,12},{6,14},{8,0},{10,2},{12,4},{14,6},{16,24},{18,... | collective-permute-start | bytes 49160 | tf_op jit(solution)/shard_map/ppermute | solution.py:417
  100.3 1.4 %collective-permute-done = bf16[1,32,256]{2,1,0:T(8,128)(2,1)S(1)} collective-permute-done((bf16[1,32,256]{2,1,0:T(8,128)(2,1)S(1)}, bf16[1,32,256]{2,1,0:T(8,128)(2,1)S(1)}, u32[]{:S(2)}, u32[]{:S(2)}) %collective-permute-start) | collective-permute-done | bytes 16416 | tf_op jit(solution)/shard_map/ppermute | solution.py:417
  101.7 1.2 collective-permute-start.1
  102.9 2.8 %collective-permute-done.1 = bf16[2,32,256]{2,1,0:T(8,128)(2,1)S(1)} collective-permute-done((bf16[2,32,256]{2,1,0:T(8,128)(2,1)S(1)}, bf16[2,32,256]{2,1,0:T(8,128)(2,1)S(1)}, u32[]{:S(2)}, u32[]{:S(2)}) %collective-permute-start.1) | collective-permute-done | bytes 32800 | tf_op jit(solution)/shard_map/ppermute | solution.py:417
  105.8 0.3 collective-permute-start.2
  106.0 2.9 %collective-permute-done.2 = bf16[4,32,256]{2,1,0:T(8,128)(2,1)S(1)} collective-permute-done((bf16[4,32,256]{2,1,0:T(8,128)(2,1)S(1)}, bf16[4,32,256]{2,1,0:T(8,128)(2,1)S(1)}, u32[]{:S(2)}, u32[]{:S(2)}) %collective-permute-start.2) | collective-permute-done | bytes 65568 | tf_op jit(solution)/shard_map/ppermute | solution.py:417
  109.0 2.6 %finish_prompts.1 = bf16[256,1024]{1,0:T(8,128)(2,1)} custom-call(s32[1]{0:T(128)} %bitcast.side, bf16[256,2048]{1,0:T(8,128)(2,1)} %get-tuple-element.23.own, bf16[256,2048]{1,0:T(8,128)(2,1)} %collective-permute-done.3.other, bf16[256,2048]{1,0:T(8,128)(2,1)S(1)} %copy-done.4, f32[1,2048]{1,0:T(1,128)S(1)} %bitcast.16), custom_call_target="tpu_custom_call" | custom-call | flops 4194304 | bytes 3145728 | tf_op jit(solution)/shard_map/finish_prompts/pallas_call | solution.py:349
  111.6 0.7 remote_pieces.1
  112.3 14.6 %all_to_all.10.pieces = bf16[8,32,384]{2,1,0:T(8,128)(2,1)S(1)} all-to-all(bf16[8,32,384]{2,1,0:T(8,128)(2,1)S(1)} %remote_pieces.1), channel_id=1, replica_groups={{0,2,4,6,8,10,12,14},{16,18,20,22,24,26,28,30},{32,34,36,38,40,42,44,46..., dimensions={0} | all-to-all | bytes 393216 | tf_op jit(solution)/shard_map/all_to_all | solution.py:431
  126.9 2.2 %copy-done.1 = bf16[1024,2048]{1,0:T(8,128)(2,1)S(1)} copy-done((bf16[1024,2048]{1,0:T(8,128)(2,1)S(1)}, bf16[1024,2048]{1,0:T(8,128)(2,1)}, u32[]{:S(2)}) %copy-start.1) | copy-done | bytes 4194328
  129.1 2.3 %join.1.own = f32[8,2048]{1,0:T(8,128)S(1)} custom-call(bf16[8,32,384]{2,1,0:T(8,128)(2,1)S(1)} %all_to_all.10.pieces, f32[32,512]{1,0:T(8,128)S(1)} %get-tuple-element.25.local, bf16[1024,2048]{1,0:T(8,128)(2,1)S(1)} %copy-done.1), custom_call_target="tpu_custom_call" | custom-call | flops 33554432 | bytes 4194304 | tf_op jit(solution)/shard_map/join/pallas_call | solution.py:310
  131.4 4.9 %collective-permute-start.4 = (f32[8,2048]{1,0:T(8,128)S(1)}, f32[8,2048]{1,0:T(8,128)S(1)}, u32[]{:S(2)}, u32[]{:S(2)}) collective-permute-start(f32[8,2048]{1,0:T(8,128)S(1)} %join.1.own), channel_id=1, source_target_pairs={{0,1},{1,0},{2,3},{3,2},{4,5},{5,4},{6,7},{7,6},{8,9},{9,8},{10,11... | collective-permute-start | bytes 196616 | tf_op jit(solution)/shard_map/ppermute | solution.py:433
  136.3 0.9 collective-permute-done.4.other
  137.2 0.7 finish_drafts.1
  (32 shorter events, 0.2 us)
Async XLA Ops:
  65.9 8.5 %copy-start.12 = (s32[1,4]{1,0:T(1,128)S(1)}, s32[1,4]{1,0:T(1,128)}, u32[]{:S(2)}) copy-start(s32[1,4]{1,0:T(1,128)} %lengths.1) | copy-start | bytes 52
  66.0 9.9 %copy-start.4 = (bf16[256,2048]{1,0:T(8,128)(2,1)S(1)}, bf16[256,2048]{1,0:T(8,128)(2,1)}, u32[]{:S(2)}) copy-start(bf16[256,2048]{1,0:T(8,128)(2,1)} %x.2) | copy-start | bytes 3145732
  66.0 9.9 %copy-start.7 = (bf16[1,5,2048]{2,1,0:T(8,128)(2,1)S(1)}, bf16[1,5,2048]{2,1,0:T(8,128)(2,1)}, u32[]{:S(2)}) copy-start(bf16[1,5,2048]{2,1,0:T(8,128)(2,1)} %x.3) | copy-start | bytes 61444
  66.0 9.9 %copy-start.9 = (f32[2048]{0:T(1024)S(1)}, f32[2048]{0:T(1024)}, u32[]{:S(2)}) copy-start(f32[2048]{0:T(1024)} %param.16) | copy-start | bytes 24580
  66.0 9.9 %copy-start.10 = (f32[2,256]{1,0:T(2,128)S(1)}, f32[2,256]{1,0:T(2,128)}, u32[]{:S(2)}) copy-start(f32[2,256]{1,0:T(2,128)} %qk_gain.1) | copy-start | bytes 6148
  66.0 9.9 %copy-start.11 = (s32[1,64]{1,0:T(1,128)S(1)}, s32[1,64]{1,0:T(1,128)}, u32[]{:S(2)}) copy-start(s32[1,64]{1,0:T(1,128)} %table.1) | copy-start | bytes 772
  66.0 45.6 %all-to-all-start = ((bf16[128,16,512]{2,1,0:T(8,128)(2,1)}), bf16[128,16,512]{2,1,0:T(8,128)(2,1)S(1)}, u32[]{:S(2)}, u32[]{:S(2)}) async-start(bf16[128,16,512]{2,1,0:T(8,128)(2,1)} %pick_pages.1), calls=%async_computation | async-start | bytes 4194304 | tf_op jit(solution)/shard_map/all_to_all | solution.py:396
  75.9 2.2 %copy-start.2 = (bf16[2048,1024]{1,0:T(8,128)(2,1)S(1)}, bf16[2048,1024]{1,0:T(8,128)(2,1)}, u32[]{:S(2)}) copy-start(bf16[2048,1024]{1,0:T(8,128)(2,1)} %wq.1) | copy-start | bytes 12582916
  78.1 1.6 %copy-start.5 = (bf16[2048,512]{1,0:T(8,128)(2,1)S(1)}, bf16[2048,512]{1,0:T(8,128)(2,1)}, u32[]{:S(2)}) copy-start(bf16[2048,512]{1,0:T(8,128)(2,1)} %wkv.1) | copy-start | bytes 6291460
  79.7 6.9 %copy-start = (bf16[1024,2048]{1,0:T(8,128)(2,1)S(1)}, bf16[1024,2048]{1,0:T(8,128)(2,1)}, u32[]{:S(2)}) copy-start(bf16[1024,2048]{1,0:T(8,128)(2,1)} %w_out.3) | copy-start | bytes 12582916
  79.7 6.9 %copy-start.3 = (bf16[64,16,512]{2,1,0:T(8,128)(2,1)S(1)}, bf16[64,16,512]{2,1,0:T(8,128)(2,1)}, u32[]{:S(2)}) copy-start(bf16[64,16,512]{2,1,0:T(8,128)(2,1)} %pool.1) | copy-start | bytes 3145732
  86.7 1.0 copy-start.6
  87.6 21.4 %copy-start.8 = (f32[2048]{0:T(1024)S(1)}, f32[2048]{0:T(1024)}, u32[]{:S(2)}) copy-start(f32[2048]{0:T(1024)} %param.21) | copy-start | bytes 24580
  92.3 16.6 %collective-permute-start.3 = (bf16[256,2048]{1,0:T(8,128)(2,1)}, bf16[256,2048]{1,0:T(8,128)(2,1)}, u32[]{:S(2)}, u32[]{:S(2)}) collective-permute-start(bf16[256,2048]{1,0:T(8,128)(2,1)} %get-tuple-element.23.own), channel_id=1, source_target_pairs={{0,1},{1,0},{2,3},{3,2},{4,5},{5,4},{6,7},{7,6},{8,9},{9,8},{10,11... | collective-permute-start | bytes 3145736 | tf_op jit(solution)/shard_map/ppermute | solution.py:426
  93.4 8.3 %collective-permute-start = (bf16[1,32,256]{2,1,0:T(8,128)(2,1)S(1)}, bf16[1,32,256]{2,1,0:T(8,128)(2,1)S(1)}, u32[]{:S(2)}, u32[]{:S(2)}) collective-permute-start(bf16[1,32,256]{2,1,0:T(8,128)(2,1)S(1)} %bitcast.12), channel_id=1, source_target_pairs={{0,8},{2,10},{4,12},{6,14},{8,0},{10,2},{12,4},{14,6},{16,24},{18,... | collective-permute-start | bytes 49160 | tf_op jit(solution)/shard_map/ppermute | solution.py:417
  101.7 4.0 %collective-permute-start.1 = (bf16[2,32,256]{2,1,0:T(8,128)(2,1)S(1)}, bf16[2,32,256]{2,1,0:T(8,128)(2,1)S(1)}, u32[]{:S(2)}, u32[]{:S(2)}) collective-permute-start(bf16[2,32,256]{2,1,0:T(8,128)(2,1)S(1)} %pad_maximum_fusion.2), channel_id=1, source_target_pairs={{0,4},{2,6},{4,0},{6,2},{8,12},{10,14},{12,8},{14,10},{16,20},{18,... | collective-permute-start | bytes 98312 | tf_op jit(solution)/shard_map/ppermute | solution.py:417
  105.8 3.2 %collective-permute-start.2 = (bf16[4,32,256]{2,1,0:T(8,128)(2,1)S(1)}, bf16[4,32,256]{2,1,0:T(8,128)(2,1)S(1)}, u32[]{:S(2)}, u32[]{:S(2)}) collective-permute-start(bf16[4,32,256]{2,1,0:T(8,128)(2,1)S(1)} %pad_maximum_fusion.1), channel_id=1, source_target_pairs={{0,2},{2,0},{4,6},{6,4},{8,10},{10,8},{12,14},{14,12},{16,18},{18,... | collective-permute-start | bytes 196616 | tf_op jit(solution)/shard_map/ppermute | solution.py:417
  126.9 2.2 %copy-start.1 = (bf16[1024,2048]{1,0:T(8,128)(2,1)S(1)}, bf16[1024,2048]{1,0:T(8,128)(2,1)}, u32[]{:S(2)}) copy-start(bf16[1024,2048]{1,0:T(8,128)(2,1)} %w_out.3) | copy-start | bytes 12582916
  131.4 5.8 %collective-permute-start.4 = (f32[8,2048]{1,0:T(8,128)S(1)}, f32[8,2048]{1,0:T(8,128)S(1)}, u32[]{:S(2)}, u32[]{:S(2)}) collective-permute-start(f32[8,2048]{1,0:T(8,128)S(1)} %join.1.own), channel_id=1, source_target_pairs={{0,1},{1,0},{2,3},{3,2},{4,5},{5,4},{6,7},{7,6},{8,9},{9,8},{10,11... | collective-permute-start | bytes 196616 | tf_op jit(solution)/shard_map/ppermute | solution.py:433

commit v3 on v2

--- a/solution.py
+++ b/solution.py
@@ -15,6 +15,7 @@
 eps_norm = 1e-06
 rope_base = 1000000.0
 neg_large = -1e30
+BIG = 52 << 20
 bf16, f32, i32 = jnp.bfloat16, jnp.float32, jnp.int32
 HBM = pl.BlockSpec(memory_space=pltpu.MemorySpace.HBM)
 VMEM = pl.BlockSpec(memory_space=pltpu.MemorySpace.VMEM)
@@ -37,24 +38,18 @@
     return values * lax.rsqrt(jnp.mean(values * values, axis=-1, keepdims=True) + eps_norm)
 
 
-def pick_kernel(index, pool, out, sem):
-    def send(i, carry):
-        page = jnp.clip(index[0, i], 0, pool.shape[0] - 1)
-        pltpu.make_async_copy(pool.at[page], out.at[i], sem).start()
-        return carry
-
-    lax.fori_loop(0, out.shape[0], send, 0, unroll=8)
-    pltpu.make_async_copy(out, out, sem).wait()
+def pick_kernel(index, pool, out):
+    for i in range(out.shape[0]):
+        out[i] = pool[jnp.clip(index[0, i], 0, pool.shape[0] - 1)]
 
 
 def pick_pages(index, pool):
     count = index.shape[1]
     return pl.pallas_call(
         pick_kernel,
-        in_specs=[SMEM, HBM],
-        out_specs=HBM,
+        in_specs=[SMEM, VMEM],
+        out_specs=VMEM,
         out_shape=jax.ShapeDtypeStruct((count,) + pool.shape[1:], pool.dtype),
-        scratch_shapes=[pltpu.SemaphoreType.DMA],
         cost_estimate=pl.CostEstimate(flops=0, transcendentals=0, bytes_accessed=4 << 20),
         name="pick_pages",
     )(index, pool)
@@ -86,8 +81,8 @@
 
     def tally(lanes, first, step):
         lane = iota((slots, lanes), 1)
-        named = page == first + (lane // PAGE) * step
-        valid = base + lane % PAGE < length[0]
+        named = page == first + (lane >> 4) * step
+        valid = base + (lane & (PAGE - 1)) < length[0]
         return jnp.sum(jnp.where(named & valid, 1.0, 0.0), axis=0, keepdims=True)
 
     own = own_count.shape[1]
@@ -149,7 +144,7 @@
             pltpu.VMEM((QH * PAD, HEAD), f32),
             pltpu.SemaphoreType.DMA((QH + 2,)),
         ],
-        compiler_params=pltpu.CompilerParams(vmem_limit_bytes=24 << 20),
+        compiler_params=pltpu.CompilerParams(vmem_limit_bytes=BIG),
         cost_estimate=pl.CostEstimate(
             flops=2 * total * width * 6 * HEAD, transcendentals=0, bytes_accessed=9 << 20
         ),
@@ -157,11 +152,7 @@
     )(length, accepted, x, draft, gain, wq, wkv, qk_gain, cosine, sine, table)
 
 
-def prompt_kernel(
-    lengths, q, kv, w_out, query, draft_kv, pool, count, out, local, attn, weights, sem
-):
-    copy = pltpu.make_async_copy(w_out, weights, sem)
-    copy.start()
+def prompt_kernel(lengths, q, kv, query, draft_kv, pool, count, attn, local):
     rows = attn.shape[0]
     row, col = iota((rows, rows), 0), iota((rows, rows), 1)
     start = jnp.zeros((rows, rows), i32)
@@ -181,7 +172,7 @@
     times = count[...]
     scores = jnp.where(times > 0.0, dot_t(mine, pool[:, :HEAD]), neg_large)
     fresh = dot_t(mine, draft_kv[:, :HEAD].astype(bf16))
-    allowed = iota(fresh.shape, 1) <= iota(fresh.shape, 0) % PAD
+    allowed = iota(fresh.shape, 1) <= (iota(fresh.shape, 0) & (PAD - 1))
     fresh = jnp.where(allowed, fresh, neg_large)
     peak = jnp.maximum(
         jnp.max(scores, axis=-1, keepdims=True), jnp.max(fresh, axis=-1, keepdims=True)
@@ -195,35 +186,55 @@
     local[:, HEAD : HEAD + 128] = jnp.broadcast_to(peak, (QH * PAD, 128))
     local[:, HEAD + 128 :] = jnp.broadcast_to(denom, (QH * PAD, 128))
 
-    copy.wait()
-    cols = 512
-    for i in range(out.shape[1] // cols):
+
+def prompts(lengths, q, kv, query, draft_kv, pool, count):
+    rows = kv.shape[0]
+    return pl.pallas_call(
+        prompt_kernel,
+        in_specs=[SMEM] + [VMEM] * 6,
+        out_specs=[VMEM, VMEM],
+        out_shape=[
+            jax.ShapeDtypeStruct((rows, QH * HEAD), bf16),
+            jax.ShapeDtypeStruct((QH * PAD, 2 * HEAD), f32),
+        ],
+        compiler_params=pltpu.CompilerParams(vmem_limit_bytes=16 << 20),
+        cost_estimate=pl.CostEstimate(
+            flops=16 * rows * rows * HEAD, transcendentals=4 * rows * rows, bytes_accessed=4 << 20
+        ),
+        name="prompts",
+    )(lengths, q, kv, query, draft_kv, pool, count)
+
+
+def spread_kernel(attn, w_out, out, weights, sems):
+    parts = sems.shape[0]
+    cols = out.shape[1] // parts
+    copies = []
+    for i in range(parts):
+        part = slice(i * cols, (i + 1) * cols)
+        copy = pltpu.make_async_copy(w_out.at[:, part], weights.at[:, part], sems.at[i])
+        copy.start()
+        copies.append(copy)
+    for i in range(parts):
+        copies[i].wait()
         part = slice(i * cols, (i + 1) * cols)
         out[:, part] = dot_n(attn[...], weights[:, part]).astype(bf16)
 
 
-def prompts(lengths, q, kv, w_out, query, draft_kv, pool, count):
-    rows = kv.shape[0]
+def spread(attn, w_out):
+    rows = attn.shape[0]
     depth, width = w_out.shape
     return pl.pallas_call(
-        prompt_kernel,
-        in_specs=[SMEM, VMEM, VMEM, HBM, VMEM, VMEM, VMEM, VMEM],
-        out_specs=[VMEM, VMEM],
-        out_shape=[
-            jax.ShapeDtypeStruct((rows, width), bf16),
-            jax.ShapeDtypeStruct((QH * PAD, 2 * HEAD), f32),
-        ],
-        scratch_shapes=[
-            pltpu.VMEM((rows, depth), bf16),
-            pltpu.VMEM((depth, width), bf16),
-            pltpu.SemaphoreType.DMA,
-        ],
-        compiler_params=pltpu.CompilerParams(vmem_limit_bytes=24 << 20),
+        spread_kernel,
+        in_specs=[VMEM, HBM],
+        out_specs=VMEM,
+        out_shape=jax.ShapeDtypeStruct((rows, width), bf16),
+        scratch_shapes=[pltpu.VMEM((depth, width), bf16), pltpu.SemaphoreType.DMA((4,))],
+        compiler_params=pltpu.CompilerParams(vmem_limit_bytes=BIG),
         cost_estimate=pl.CostEstimate(
-            flops=2 * rows * depth * width, transcendentals=4 * rows * rows, bytes_accessed=6 << 20
-        ),
-        name="prompts",
-    )(lengths, q, kv, w_out, query, draft_kv, pool, count)
+            flops=2 * rows * depth * width, transcendentals=0, bytes_accessed=6 << 20
+        ),
+        name="spread",
+    )(attn, w_out)
 
 
 def remote_kernel(where, queries, pages, out):
@@ -317,7 +328,7 @@
             pltpu.VMEM((depth, width), bf16),
             pltpu.SemaphoreType.DMA((4,)),
         ],
-        compiler_params=pltpu.CompilerParams(vmem_limit_bytes=12 << 20),
+        compiler_params=pltpu.CompilerParams(vmem_limit_bytes=BIG),
         cost_estimate=pl.CostEstimate(flops=1 << 25, transcendentals=0, bytes_accessed=4 << 20),
         name="join",
     )(pieces, local, w_out)
@@ -411,24 +422,30 @@
         qk_gain, jnp.cos(angles), jnp.sin(angles), page_table, pool_pages * PAGE,
     )
 
-    asked = sent[None]
-    for mask in (4, 2, 1):
+    side = lax.axis_index("head").reshape(1)
+    where = (lax.axis_index("req") & (DEEP - 1)).reshape(1)
+    swap = [(0, 1), (1, 0)]
+
+    def beside(values, mask):
         pairs = [(i, i ^ mask) for i in range(devices)]
-        asked = jnp.concatenate([asked, lax.ppermute(asked, "req", pairs)], axis=0)
-
-    side = lax.axis_index("head").reshape(1)
-    where = (lax.axis_index("req") % DEEP).reshape(1)
-    swap = [(0, 1), (1, 0)]
-    partial, own = prompts(
-        prompt_len, queries, prefill_kv, w_out, sent, draft_kv,
+        return jnp.concatenate([values, lax.ppermute(values, "req", pairs)], axis=0)
+
+    asked = beside(sent[None], 4)
+    attn, own = prompts(
+        prompt_len, queries, prefill_kv, sent, draft_kv,
         page_pool.reshape(pool_pages * PAGE, -1), own_count,
     )
+    asked, attn = lax.optimization_barrier((asked, attn))
+    asked = beside(asked, 2)
+    partial = spread(attn, w_out)
+    asked, partial = lax.optimization_barrier((asked, partial))
+    asked = beside(asked, 1)
     other = lax.ppermute(partial, "head", swap)
+    pieces = remote_pieces(where, asked, arrived.reshape(planes, DEEP, PAGE, -1))
+    pieces, other = lax.optimization_barrier((pieces, other))
     prefill_out = finish(side, partial, other, prefill_x, post_gain[None], "finish_prompts")
-
-    arrived, prefill_out = lax.optimization_barrier((arrived, prefill_out))
-    pieces = remote_pieces(where, asked, arrived.reshape(planes, DEEP, PAGE, -1))
     pieces = lax.all_to_all(pieces, "req", 0, 0, tiled=True, axis_index_groups=column)
+    pieces, prefill_out = lax.optimization_barrier((pieces, prefill_out))
     partial = join(pieces, own, w_out)
     other = lax.ppermute(partial, "head", swap)
     verify_out = finish(side, partial, other, verify_x, post_gain[None], "finish_drafts")

time: 138 us -> 66.8 us (0.48)
  Pallas kernels: 83.3 us -> 23.1 us
  blocking collectives: 14.6 us -> 0 us
  starting transfers between devices: 22.1 us -> 29.6 us
  local copies, waits for them, and re-layouts: 6.96 us -> 0.99 us
  waiting for transfers between devices: 8.06 us -> 9.83 us
    pallas_call x2 -> x3, Pallas kernels: 70 us -> 8.87 us  [the longest x1 4.01 us: spread(): pl.pallas_call(spread_kernel, in_specs=[VMEM, HBM], out_specs=VMEM, out_s...]
    all_to_all x1 -> x0, blocking collectives: 14.6 us -> none  [on_device(): lax.all_to_all(pieces, 'req', 0, 0, tiled=True, axis_index_groups=column)]
    all_to_all x0 -> x1, starting transfers between devices: none -> 6.25 us  [on_device(): lax.all_to_all(pieces, 'req', 0, 0, tiled=True, axis_index_groups=column)]
    all_to_all x0 -> x1, waiting for transfers between devices: none -> 6.08 us  [on_device(): lax.all_to_all(pieces, 'req', 0, 0, tiled=True, axis_index_groups=column)]
    unnamed x26 -> x18, local copies, waits for them, and re-layouts: 6.96 us -> 0.99 us
    ppermute x3, waiting for transfers between devices: 7.15 us -> 2.84 us  [beside(): return jnp.concatenate([values, lax.ppermute(values, 'req', pairs)], axis=0)]
  transfers between devices with their start and end apart: 6 -> 7, of which waited for: 4 -> 3; matrix products, arithmetic and copies ran while one was open for 1% -> 1% of each run, Pallas kernels for 10% -> 26%
where the time goes in v3:
time: 66.8 us; the launch traced here: 66.5 us
  starting transfers between devices  29.6 us (44%)
  Pallas kernels  23.1 us (35%)
  waiting for transfers between devices  9.83 us (15%)
  between operations  2.12 us (3%)
  local copies, waits for them, and re-layouts  0.99 us (1%)
  other arithmetic  0.83 us (1%)
    ppermute x3, starting transfers between devices, beside(): return jnp.concatenate([values, lax.ppermute(values, 'req', pairs)], axis=0)  9.1 us
    all_to_all x1, starting transfers between devices, on_device(): lax.all_to_all(outgoing, 'req', 0, 0, tiled=True, axis_index_groups=plane)  7.73 us
    pallas_call x1, Pallas kernels, project(): pl.pallas_call(project_kernel, in_specs=[SMEM, SMEM, VMEM, VMEM, VMEM, HB...  6.97 us
    ppermute x2, starting transfers between devices, on_device(): other = lax.ppermute(partial, 'head', swap)  6.47 us
    all_to_all x1, starting transfers between devices, on_device(): lax.all_to_all(pieces, 'req', 0, 0, tiled=True, axis_index_groups=column)  6.25 us
    all_to_all x1, waiting for transfers between devices, on_device(): lax.all_to_all(pieces, 'req', 0, 0, tiled=True, axis_index_groups=column)  6.08 us
    pallas_call x1, Pallas kernels, spread(): pl.pallas_call(spread_kernel, in_specs=[VMEM, HBM], out_specs=VMEM, out_s...  4.01 us
    pallas_call x2, Pallas kernels, finish(): pl.pallas_call(finish_kernel, grid_spec=pltpu.PrefetchScalarGridSpec(num_...  3.36 us
  transfers between devices with their start and end apart: 7, of which 3 were waited for; matrix products, arithmetic and copies ran while one was open for 1% of the time, Pallas kernels for 26%

profile of v3, /device:TPU:1, one launch (start us, length us, event | category | flops | bytes accessed | tf_op | source)
XLA Modules:
  0.0 66.5 jit_solution(8767347733710762663)
XLA Ops:
  0.6 2.8 %pick_pages.1 = bf16[128,16,512]{2,1,0:T(8,128)(2,1)} custom-call(s32[1,128]{1,0:T(1,128)} %index.1, bf16[64,16,512]{2,1,0:T(8,128)(2,1)} %pool.1), custom_call_target="tpu_custom_call" | custom-call | bytes 4194304 | tf_op jit(solution)/shard_map/pick_pages/pallas_call | solution.py:48
  3.5 0.0 copy-start.6
  3.5 0.0 copy-start.7
  3.5 7.7 %all-to-all-start = ((bf16[128,16,512]{2,1,0:T(8,128)(2,1)}), bf16[128,16,512]{2,1,0:T(8,128)(2,1)S(1)}, u32[]{:S(2)}, u32[]{:S(2)}) async-start(bf16[128,16,512]{2,1,0:T(8,128)(2,1)} %pick_pages.1), calls=%async_computation | async-start | bytes 4194304 | tf_op jit(solution)/shard_map/all_to_all | solution.py:407
  12.6 0.1 select_reduce_fusion.1
  12.7 0.1 select_reduce_fusion
  12.8 0.6 multiply_sine_fusion
  13.4 7.0 %project.1 = (bf16[4,256,256]{2,1,0:T(8,128)(2,1)S(1)}, bf16[256,512]{1,0:T(8,128)(2,1)}, bf16[32,256]{1,0:T(8,128)(2,1)S(1)}, f32[8,512]{1,0:T(8,128)S(1)}, f32...) custom-call(s32[1]{0:T(128)} %copy.18.length, s32[1]{0:T(128)S(6)} %copy.19.accepted, bf16[256,2048]{1,0:T(8,128)(2,1)S(1)} %copy-done.1, ...), custom_call_target="tpu_custom_call" | custom-call | flops 1711276032 | bytes 9437184 | tf_op jit(solution)/shard_map/project/pallas_call | solution.py:135
  20.4 7.0 %collective-permute-start = (bf16[1,32,256]{2,1,0:T(8,128)(2,1)S(1)}, bf16[1,32,256]{2,1,0:T(8,128)(2,1)S(1)}, u32[]{:S(2)}, u32[]{:S(2)}) collective-permute-start(bf16[1,32,256]{2,1,0:T(8,128)(2,1)S(1)} %bitcast.12), channel_id=1, source_target_pairs={{0,8},{2,10},{4,12},{6,14},{8,0},{10,2},{12,4},{14,6},{16,24},{18,... | collective-permute-start | bytes 49160 | tf_op jit(solution)/shard_map/ppermute | solution.py:431
  27.4 0.9 %copy-done.2 = bf16[256,512]{1,0:T(8,128)(2,1)S(1)} copy-done((bf16[256,512]{1,0:T(8,128)(2,1)S(1)}, bf16[256,512]{1,0:T(8,128)(2,1)}, u32[]{:S(2)}) %copy-start.2) | copy-done | bytes 262168
  28.4 2.0 %prompts.1 = (bf16[256,1024]{1,0:T(8,128)(2,1)S(1)}, f32[32,512]{1,0:T(8,128)S(1)}) custom-call(s32[1,4]{1,0:T(1,128)S(1)} %copy-done.8, bf16[4,256,256]{2,1,0:T(8,128)(2,1)S(1)} %get-tuple-element.24.q, bf16[256,512]{1,0:T(8,128)(2,1)S(1)} %copy-done.2, bf16[32,256]{1,0:T(8,128)(2,1)S(1)} %get-tuple-element.23.query, ...), custom_call_target="tpu_custom_call" | custom-call | flops 268435456 | bytes 4194304 | tf_op jit(solution)/shard_map/prompts/pallas_call | solution.py:192
  30.4 1.3 %collective-permute-start.1 = (bf16[2,32,256]{2,1,0:T(8,128)(2,1)S(1)}, bf16[2,32,256]{2,1,0:T(8,128)(2,1)S(1)}, u32[]{:S(2)}, u32[]{:S(2)}) collective-permute-start(bf16[2,32,256]{2,1,0:T(8,128)(2,1)S(1)} %pad_maximum_fusion.2), channel_id=1, source_target_pairs={{0,4},{2,6},{4,0},{6,2},{8,12},{10,14},{12,8},{14,10},{16,20},{18,... | collective-permute-start | bytes 98312 | tf_op jit(solution)/shard_map/ppermute | solution.py:431
  31.7 4.0 %spread.1.own = bf16[256,2048]{1,0:T(8,128)(2,1)} custom-call(bf16[256,1024]{1,0:T(8,128)(2,1)S(1)} %get-tuple-element.30.attn, bf16[1024,2048]{1,0:T(8,128)(2,1)} %w_out.3), custom_call_target="tpu_custom_call" | custom-call | flops 1073741824 | bytes 6291456 | tf_op jit(solution)/shard_map/spread/pallas_call | solution.py:226
  35.8 1.6 %collective-permute-start.3 = (bf16[256,2048]{1,0:T(8,128)(2,1)}, bf16[256,2048]{1,0:T(8,128)(2,1)}, u32[]{:S(2)}, u32[]{:S(2)}) collective-permute-start(bf16[256,2048]{1,0:T(8,128)(2,1)} %spread.1.own), channel_id=1, source_target_pairs={{0,1},{1,0},{2,3},{3,2},{4,5},{5,4},{6,7},{7,6},{8,9},{9,8},{10,11... | collective-permute-start | bytes 3145736 | tf_op jit(solution)/shard_map/ppermute | solution.py:443
  37.4 0.8 %collective-permute-start.2 = (bf16[4,32,256]{2,1,0:T(8,128)(2,1)S(1)}, bf16[4,32,256]{2,1,0:T(8,128)(2,1)S(1)}, u32[]{:S(2)}, u32[]{:S(2)}) collective-permute-start(bf16[4,32,256]{2,1,0:T(8,128)(2,1)S(1)} %pad_maximum_fusion.1), channel_id=1, source_target_pairs={{0,2},{2,0},{4,6},{6,4},{8,10},{10,8},{12,14},{14,12},{16,18},{18,... | collective-permute-start | bytes 196616 | tf_op jit(solution)/shard_map/ppermute | solution.py:431
  38.2 2.8 %collective-permute-done.2 = bf16[4,32,256]{2,1,0:T(8,128)(2,1)S(1)} collective-permute-done((bf16[4,32,256]{2,1,0:T(8,128)(2,1)S(1)}, bf16[4,32,256]{2,1,0:T(8,128)(2,1)S(1)}, u32[]{:S(2)}, u32[]{:S(2)}) %collective-permute-start.2) | collective-permute-done | bytes 65568 | tf_op jit(solution)/shard_map/ppermute | solution.py:431
  41.0 1.3 %remote_pieces.1 = bf16[8,32,384]{2,1,0:T(8,128)(2,1)} custom-call(s32[1]{0:T(128)} %bitcast.1.where, bf16[8,32,256]{2,1,0:T(8,128)(2,1)S(1)} %pad_maximum_fusion.queries, bf16[16,8,16,512]{3,2,1,0:T(8,128)(2,1)S(1)} %bitcast.10), custom_call_target="tpu_custom_call" | custom-call | flops 67108864 | bytes 3145728 | tf_op jit(solution)/shard_map/remote_pieces/pallas_call | solution.py:273
  42.4 6.3 %all-to-all-start.1 = ((bf16[8,32,384]{2,1,0:T(8,128)(2,1)}), bf16[8,32,384]{2,1,0:T(8,128)(2,1)S(1)}, u32[]{:S(2)}, u32[]{:S(2)}) async-start(bf16[8,32,384]{2,1,0:T(8,128)(2,1)} %remote_pieces.1), calls=%async_computation.1 | async-start | bytes 393216 | tf_op jit(solution)/shard_map/all_to_all | solution.py:447
  48.6 2.6 %finish_prompts.1 = bf16[256,1024]{1,0:T(8,128)(2,1)} custom-call(s32[1]{0:T(128)} %bitcast.side, bf16[256,2048]{1,0:T(8,128)(2,1)} %spread.1.own, bf16[256,2048]{1,0:T(8,128)(2,1)} %collective-permute-done.3.other, bf16[256,2048]{1,0:T(8,128)(2,1)S(1)} %copy-done.1, f32[1,2048]{1,0:T(1,128)S(1)} %bitcast.14), custom_call_target="tpu_custom_call" | custom-call | flops 4194304 | bytes 3145728 | tf_op jit(solution)/shard_map/finish_prompts/pallas_call | solution.py:360
  51.3 6.1 %all-to-all-done.1.pieces = bf16[8,32,384]{2,1,0:T(8,128)(2,1)S(1)} async-done(((bf16[8,32,384]{2,1,0:T(8,128)(2,1)}), bf16[8,32,384]{2,1,0:T(8,128)(2,1)S(1)}, u32[]{:S(2)}, u32[]{:S(2)}) %all-to-all-start.1) | async-done | bytes 196640 | tf_op jit(solution)/shard_map/all_to_all | solution.py:447
  57.4 2.6 %join.1.own = f32[8,2048]{1,0:T(8,128)S(1)} custom-call(bf16[8,32,384]{2,1,0:T(8,128)(2,1)S(1)} %all-to-all-done.1.pieces, f32[32,512]{1,0:T(8,128)S(1)} %get-tuple-element.37.local, bf16[1024,2048]{1,0:T(8,128)(2,1)} %w_out.3), custom_call_target="tpu_custom_call" | custom-call | flops 33554432 | bytes 4194304 | tf_op jit(solution)/shard_map/join/pallas_call | solution.py:321
  60.0 4.9 %collective-permute-start.4 = (f32[8,2048]{1,0:T(8,128)S(1)}, f32[8,2048]{1,0:T(8,128)S(1)}, u32[]{:S(2)}, u32[]{:S(2)}) collective-permute-start(f32[8,2048]{1,0:T(8,128)S(1)} %join.1.own), channel_id=1, source_target_pairs={{0,1},{1,0},{2,3},{3,2},{4,5},{5,4},{6,7},{7,6},{8,9},{9,8},{10,11... | collective-permute-start | bytes 196616 | tf_op jit(solution)/shard_map/ppermute | solution.py:450
  64.9 0.9 %collective-permute-done.4.other = f32[8,2048]{1,0:T(8,128)S(1)} collective-permute-done((f32[8,2048]{1,0:T(8,128)S(1)}, f32[8,2048]{1,0:T(8,128)S(1)}, u32[]{:S(2)}, u32[]{:S(2)}) %collective-permute-start.4) | collective-permute-done | bytes 65568 | tf_op jit(solution)/shard_map/ppermute | solution.py:450
  65.8 0.7 %finish_drafts.1 = bf16[1,5,1024]{2,1,0:T(8,128)(2,1)} custom-call(s32[1]{0:T(128)} %bitcast.side, f32[8,2048]{1,0:T(8,128)S(1)} %join.1.own, f32[8,2048]{1,0:T(8,128)S(1)} %collective-permute-done.4.other, bf16[1,5,2048]{2,1,0:T(8,128)(2,1)S(1)} %copy-done.3, f32[1,2048]{1,0:T(1,128)S(1)} %bitcast.15), custom_call_target="tpu_custom_call" | custom-call | flops 131072 | bytes 98304 | tf_op jit(solution)/shard_map/finish_drafts/pallas_call | solution.py:360
  (26 shorter events, 0.1 us)
Async XLA Ops:
  3.5 9.1 %copy-start.8 = (s32[1,4]{1,0:T(1,128)S(1)}, s32[1,4]{1,0:T(1,128)}, u32[]{:S(2)}) copy-start(s32[1,4]{1,0:T(1,128)} %lengths.1) | copy-start | bytes 52
  3.5 9.9 %copy-start.1 = (bf16[256,2048]{1,0:T(8,128)(2,1)S(1)}, bf16[256,2048]{1,0:T(8,128)(2,1)}, u32[]{:S(2)}) copy-start(bf16[256,2048]{1,0:T(8,128)(2,1)} %x.2) | copy-start | bytes 3145732
  3.5 9.9 %copy-start.3 = (bf16[1,5,2048]{2,1,0:T(8,128)(2,1)S(1)}, bf16[1,5,2048]{2,1,0:T(8,128)(2,1)}, u32[]{:S(2)}) copy-start(bf16[1,5,2048]{2,1,0:T(8,128)(2,1)} %x.3) | copy-start | bytes 61444
  3.5 9.9 %copy-start.5 = (f32[2048]{0:T(1024)S(1)}, f32[2048]{0:T(1024)}, u32[]{:S(2)}) copy-start(f32[2048]{0:T(1024)} %param.16) | copy-start | bytes 24580
  3.5 9.9 %copy-start.6 = (f32[2,256]{1,0:T(2,128)S(1)}, f32[2,256]{1,0:T(2,128)}, u32[]{:S(2)}) copy-start(f32[2,256]{1,0:T(2,128)} %qk_gain.1) | copy-start | bytes 6148
  3.5 9.9 %copy-start.7 = (s32[1,64]{1,0:T(1,128)S(1)}, s32[1,64]{1,0:T(1,128)}, u32[]{:S(2)}) copy-start(s32[1,64]{1,0:T(1,128)} %table.1) | copy-start | bytes 772
  3.5 37.5 %all-to-all-start = ((bf16[128,16,512]{2,1,0:T(8,128)(2,1)}), bf16[128,16,512]{2,1,0:T(8,128)(2,1)S(1)}, u32[]{:S(2)}, u32[]{:S(2)}) async-start(bf16[128,16,512]{2,1,0:T(8,128)(2,1)} %pick_pages.1), calls=%async_computation | async-start | bytes 4194304 | tf_op jit(solution)/shard_map/all_to_all | solution.py:407
  13.4 14.0 %copy-start = (bf16[64,16,512]{2,1,0:T(8,128)(2,1)S(1)}, bf16[64,16,512]{2,1,0:T(8,128)(2,1)}, u32[]{:S(2)}) copy-start(bf16[64,16,512]{2,1,0:T(8,128)(2,1)} %pool.1) | copy-start | bytes 3145732
  20.4 10.0 %collective-permute-start = (bf16[1,32,256]{2,1,0:T(8,128)(2,1)S(1)}, bf16[1,32,256]{2,1,0:T(8,128)(2,1)S(1)}, u32[]{:S(2)}, u32[]{:S(2)}) collective-permute-start(bf16[1,32,256]{2,1,0:T(8,128)(2,1)S(1)} %bitcast.12), channel_id=1, source_target_pairs={{0,8},{2,10},{4,12},{6,14},{8,0},{10,2},{12,4},{14,6},{16,24},{18,... | collective-permute-start | bytes 49160 | tf_op jit(solution)/shard_map/ppermute | solution.py:431
  27.4 1.0 %copy-start.2 = (bf16[256,512]{1,0:T(8,128)(2,1)S(1)}, bf16[256,512]{1,0:T(8,128)(2,1)}, u32[]{:S(2)}) copy-start(bf16[256,512]{1,0:T(8,128)(2,1)} %get-tuple-element.21.kv) | copy-start | bytes 786436
  30.4 5.3 %collective-permute-start.1 = (bf16[2,32,256]{2,1,0:T(8,128)(2,1)S(1)}, bf16[2,32,256]{2,1,0:T(8,128)(2,1)S(1)}, u32[]{:S(2)}, u32[]{:S(2)}) collective-permute-start(bf16[2,32,256]{2,1,0:T(8,128)(2,1)S(1)} %pad_maximum_fusion.2), channel_id=1, source_target_pairs={{0,4},{2,6},{4,0},{6,2},{8,12},{10,14},{12,8},{14,10},{16,20},{18,... | collective-permute-start | bytes 98312 | tf_op jit(solution)/shard_map/ppermute | solution.py:431
  35.7 12.9 %copy-start.4 = (f32[2048]{0:T(1024)S(1)}, f32[2048]{0:T(1024)}, u32[]{:S(2)}) copy-start(f32[2048]{0:T(1024)} %param.21) | copy-start | bytes 24580
  35.8 6.6 %collective-permute-start.3 = (bf16[256,2048]{1,0:T(8,128)(2,1)}, bf16[256,2048]{1,0:T(8,128)(2,1)}, u32[]{:S(2)}, u32[]{:S(2)}) collective-permute-start(bf16[256,2048]{1,0:T(8,128)(2,1)} %spread.1.own), channel_id=1, source_target_pairs={{0,1},{1,0},{2,3},{3,2},{4,5},{5,4},{6,7},{7,6},{8,9},{9,8},{10,11... | collective-permute-start | bytes 3145736 | tf_op jit(solution)/shard_map/ppermute | solution.py:443
  37.4 3.7 %collective-permute-start.2 = (bf16[4,32,256]{2,1,0:T(8,128)(2,1)S(1)}, bf16[4,32,256]{2,1,0:T(8,128)(2,1)S(1)}, u32[]{:S(2)}, u32[]{:S(2)}) collective-permute-start(bf16[4,32,256]{2,1,0:T(8,128)(2,1)S(1)} %pad_maximum_fusion.1), channel_id=1, source_target_pairs={{0,2},{2,0},{4,6},{6,4},{8,10},{10,8},{12,14},{14,12},{16,18},{18,... | collective-permute-start | bytes 196616 | tf_op jit(solution)/shard_map/ppermute | solution.py:431
  42.4 15.0 %all-to-all-start.1 = ((bf16[8,32,384]{2,1,0:T(8,128)(2,1)}), bf16[8,32,384]{2,1,0:T(8,128)(2,1)S(1)}, u32[]{:S(2)}, u32[]{:S(2)}) async-start(bf16[8,32,384]{2,1,0:T(8,128)(2,1)} %remote_pieces.1), calls=%async_computation.1 | async-start | bytes 393216 | tf_op jit(solution)/shard_map/all_to_all | solution.py:447
  60.0 5.8 %collective-permute-start.4 = (f32[8,2048]{1,0:T(8,128)S(1)}, f32[8,2048]{1,0:T(8,128)S(1)}, u32[]{:S(2)}, u32[]{:S(2)}) collective-permute-start(f32[8,2048]{1,0:T(8,128)S(1)} %join.1.own), channel_id=1, source_target_pairs={{0,1},{1,0},{2,3},{3,2},{4,5},{5,4},{6,7},{7,6},{8,9},{9,8},{10,11... | collective-permute-start | bytes 196616 | tf_op jit(solution)/shard_map/ppermute | solution.py:450

commit v4 on v3

--- a/solution.py
+++ b/solution.py
@@ -56,16 +56,15 @@
 
 
 def project_kernel(
-    length, accepted, x, draft, gain, wq, wkv, qk_gain, cosine, sine, table,
-    queries, prompt_kv, sent, draft_kv, own_count, verify_kv,
+    meta, x, draft, gain, wq, wkv, qk_gain, cosine, sine, table,
+    queries, prompt_kv, near_kv, sent, draft_kv, own_count, verify_kv,
     weights, normed, wide, rows_q, sems,
 ):
     rows, drafted = x.shape[0], draft.shape[1]
     copies = []
-    for h in range(QH + 2):
-        part = wq if h < QH else wkv
-        col = (h if h < QH else h - QH) * HEAD
-        copy = pltpu.make_async_copy(part.at[:, col : col + HEAD], weights.at[h], sems.at[h])
+    for h in range(3):
+        part = wq.at[:, h * 2 * HEAD : (h + 1) * 2 * HEAD] if h < 2 else wkv
+        copy = pltpu.make_async_copy(part, weights.at[h], sems.at[h])
         copy.start()
         copies.append(copy)
 
@@ -82,7 +81,7 @@
     def tally(lanes, first, step):
         lane = iota((slots, lanes), 1)
         named = page == first + (lane >> 4) * step
-        valid = base + (lane & (PAGE - 1)) < length[0]
+        valid = base + (lane & (PAGE - 1)) < meta[0]
         return jnp.sum(jnp.where(named & valid, 1.0, 0.0), axis=0, keepdims=True)
 
     own = own_count.shape[1]
@@ -97,36 +96,41 @@
         return jnp.concatenate([a * cos - b * sin, b * cos + a * sin], axis=-1)
 
     row = iota((PAD, HEAD), 0)
-    for h in range(QH):
-        copies[h].wait()
-        query = rotated(unit(dot_n(normed[...], weights[h])) * qk_gain[0:1, :])
-        queries[h] = query[:rows].astype(bf16)
-        mine = query[rows : rows + PAD]
-        mine = jnp.where(row == drafted, far[h], mine)
-        mine = jnp.where(row == drafted + 1, far[h + QH], mine)
-        rows_q[h * PAD : (h + 1) * PAD, :] = mine
+    keep = iota((PAD, HEAD), 0) < meta[1]
+
+    for pair in range(3):
+        copies[pair].wait()
+        both = dot_n(normed[...], weights[pair])
+        for j in range(2):
+            h = 2 * pair + j
+            value = unit(both[:, j * HEAD : (j + 1) * HEAD])
+            if h < QH:
+                query = rotated(value * qk_gain[0:1, :])
+                queries[h] = query[:rows].astype(bf16)
+                mine = query[rows : rows + PAD]
+                mine = jnp.where(row == drafted, far[h], mine)
+                mine = jnp.where(row == drafted + 1, far[h + QH], mine)
+                rows_q[h * PAD : (h + 1) * PAD, :] = mine
+                continue
+            if h == QH:
+                value = rotated(value * qk_gain[1:2, :])
+            cols = slice(j * HEAD, (j + 1) * HEAD)
+            prompt_kv[:, cols] = value[:rows].astype(bf16)
+            near_kv[:, cols] = value[:rows].astype(bf16)
+            mine = value[rows : rows + PAD]
+            draft_kv[:, cols] = mine
+            verify_kv[0, :, cols] = jnp.where(keep, mine, 0.0)[:drafted].astype(bf16)
     sent[...] = rows_q[...].astype(bf16)
 
-    keep = iota((PAD, HEAD), 0) < accepted[0]
-    for part in range(2):
-        copies[QH + part].wait()
-        value = unit(dot_n(normed[...], weights[QH + part]))
-        if part == 0:
-            value = rotated(value * qk_gain[1:2, :])
-        cols = slice(part * HEAD, (part + 1) * HEAD)
-        prompt_kv[:, cols] = value[:rows].astype(bf16)
-        mine = value[rows : rows + PAD]
-        draft_kv[:, cols] = mine
-        verify_kv[0, :, cols] = jnp.where(keep, mine, 0.0)[:drafted].astype(bf16)
-
-
-def project(length, accepted, x, draft, gain, wq, wkv, qk_gain, cosine, sine, table, own):
+
+def project(meta, x, draft, gain, wq, wkv, qk_gain, cosine, sine, table, own):
     rows, width = x.shape
     drafted = draft.shape[1]
     total = rows + 16
     shapes = [
         jax.ShapeDtypeStruct((QH, rows, HEAD), bf16),
         jax.ShapeDtypeStruct((rows, 2 * HEAD), bf16),
+        jax.ShapeDtypeStruct((rows, 2 * HEAD), bf16),
         jax.ShapeDtypeStruct((QH * PAD, HEAD), bf16),
         jax.ShapeDtypeStruct((PAD, 2 * HEAD), f32),
         jax.ShapeDtypeStruct((1, own), f32),
@@ -134,22 +138,22 @@
     ]
     return pl.pallas_call(
         project_kernel,
-        in_specs=[SMEM, SMEM, VMEM, VMEM, VMEM, HBM, HBM, VMEM, VMEM, VMEM, VMEM],
+        in_specs=[SMEM, VMEM, VMEM, VMEM, HBM, HBM, VMEM, VMEM, VMEM, VMEM],
         out_specs=[VMEM] * len(shapes),
         out_shape=shapes,
         scratch_shapes=[
-            pltpu.VMEM((QH + 2, width, HEAD), bf16),
+            pltpu.VMEM((3, width, 2 * HEAD), bf16),
             pltpu.VMEM((total, width), bf16),
             pltpu.VMEM((16, width), f32),
             pltpu.VMEM((QH * PAD, HEAD), f32),
-            pltpu.SemaphoreType.DMA((QH + 2,)),
+            pltpu.SemaphoreType.DMA((3,)),
         ],
         compiler_params=pltpu.CompilerParams(vmem_limit_bytes=BIG),
         cost_estimate=pl.CostEstimate(
             flops=2 * total * width * 6 * HEAD, transcendentals=0, bytes_accessed=9 << 20
         ),
         name="project",
-    )(length, accepted, x, draft, gain, wq, wkv, qk_gain, cosine, sine, table)
+    )(meta, x, draft, gain, wq, wkv, qk_gain, cosine, sine, table)
 
 
 def prompt_kernel(lengths, q, kv, query, draft_kv, pool, count, attn, local):
@@ -205,19 +209,8 @@
     )(lengths, q, kv, query, draft_kv, pool, count)
 
 
-def spread_kernel(attn, w_out, out, weights, sems):
-    parts = sems.shape[0]
-    cols = out.shape[1] // parts
-    copies = []
-    for i in range(parts):
-        part = slice(i * cols, (i + 1) * cols)
-        copy = pltpu.make_async_copy(w_out.at[:, part], weights.at[:, part], sems.at[i])
-        copy.start()
-        copies.append(copy)
-    for i in range(parts):
-        copies[i].wait()
-        part = slice(i * cols, (i + 1) * cols)
-        out[:, part] = dot_n(attn[...], weights[:, part]).astype(bf16)
+def spread_kernel(attn, w_out, out):
+    out[...] = dot_n(attn[...], w_out[...]).astype(bf16)
 
 
 def spread(attn, w_out):
@@ -225,11 +218,10 @@
     depth, width = w_out.shape
     return pl.pallas_call(
         spread_kernel,
-        in_specs=[VMEM, HBM],
+        in_specs=[VMEM, VMEM],
         out_specs=VMEM,
         out_shape=jax.ShapeDtypeStruct((rows, width), bf16),
-        scratch_shapes=[pltpu.VMEM((depth, width), bf16), pltpu.SemaphoreType.DMA((4,))],
-        compiler_params=pltpu.CompilerParams(vmem_limit_bytes=BIG),
+        compiler_params=pltpu.CompilerParams(vmem_limit_bytes=12 << 20),
         cost_estimate=pl.CostEstimate(
             flops=2 * rows * depth * width, transcendentals=0, bytes_accessed=6 << 20
         ),
@@ -255,14 +247,26 @@
     parts = jnp.where(count > 0.0, jnp.exp(score - peak) * count, 0.0)
     denom = jnp.sum(parts, axis=-1, keepdims=True)
     high = denom.astype(bf16).astype(f32)
-    lane = iota((groups * rows, 128), 1)
-    stats = jnp.where(lane < 32, peak, jnp.where(lane < 64, high, denom - high)).astype(bf16)
+
+    shape = (groups * rows // PAD, PAD, 128)
+    token, lane = iota(shape, 1), iota(shape, 2)
+
+    def along(values):
+        wide = jnp.broadcast_to(values, (groups * rows, 128)).reshape(shape)
+        wide = jnp.sum(jnp.where(token == lane, wide, 0.0), axis=1, keepdims=True)
+        return jnp.broadcast_to(wide, shape)
+
+    stats = jnp.where(
+        token == 5, along(peak), jnp.where(token == 6, along(high), along(denom - high))
+    ).reshape(groups * rows, 128)
+    spare = (iota((rows, 128), 0) & (PAD - 1)) >= 5
     parts = parts.astype(bf16)
     for e in range(groups):
         own = slice(e * rows, (e + 1) * rows)
         held = pages[:, asked[e], :, HEAD:].reshape(HEAD, HEAD)
-        out[asked[e], :, :HEAD] = dot_n(parts[own], held).astype(bf16)
-        out[asked[e], :, HEAD:] = stats[own]
+        total = dot_n(parts[own], held)
+        out[asked[e], :, :128] = jnp.where(spare, stats[own], total[:, :128]).astype(bf16)
+        out[asked[e], :, 128:] = total[:, 128:].astype(bf16)
 
 
 ORDER = (0, 4, 2, 6, 1, 5, 3, 7)
@@ -274,7 +278,7 @@
         remote_kernel,
         in_specs=[SMEM, VMEM, VMEM],
         out_specs=VMEM,
-        out_shape=jax.ShapeDtypeStruct((groups, rows, HEAD + 128), bf16),
+        out_shape=jax.ShapeDtypeStruct((groups, rows, HEAD), bf16),
         compiler_params=pltpu.CompilerParams(vmem_limit_bytes=12 << 20),
         cost_estimate=pl.CostEstimate(flops=1 << 26, transcendentals=1 << 16, bytes_accessed=3 << 20),
         name="remote_pieces",
@@ -291,20 +295,24 @@
         copy = pltpu.make_async_copy(w_out.at[:, part], weights.at[:, part], sems.at[i])
         copy.start()
         copies.append(copy)
-    groups = pieces.shape[0]
-    peaks = [pieces[z, :, HEAD : HEAD + 1].astype(f32) for z in range(groups)]
+    groups, rows = pieces.shape[0], pieces.shape[1]
+    shape = (groups * rows // PAD, PAD, 128)
+    token, lane = iota(shape, 1), iota(shape, 2)
+    spare = pieces[:, :, :128].astype(f32).reshape(shape)
+
+    def upright(which):
+        row = jnp.sum(jnp.where(token == which, spare, 0.0), axis=1, keepdims=True)
+        row = jnp.where(token == lane, jnp.broadcast_to(row, shape), 0.0)
+        return jnp.sum(row, axis=2, keepdims=True).reshape(groups, rows, 1)
+
+    peaks = upright(5)
+    sums = upright(6) + upright(7)
     own = local[:, HEAD : HEAD + 1]
-    top = functools.reduce(jnp.maximum, peaks, own)
-    scale = jnp.exp(own - top)
-    total = local[:, :HEAD] * scale
-    denom = local[:, HEAD + 128 : HEAD + 129] * scale
-    for z in range(groups):
-        scale = jnp.exp(peaks[z] - top)
-        total += pieces[z, :, :HEAD].astype(f32) * scale
-        denom += scale * (
-            pieces[z, :, HEAD + 32 : HEAD + 33].astype(f32)
-            + pieces[z, :, HEAD + 64 : HEAD + 65].astype(f32)
-        )
+    top = jnp.maximum(jnp.max(peaks, axis=0), own)
+    scale = jnp.exp(peaks - top[None])
+    near = jnp.exp(own - top)
+    total = local[:, :HEAD] * near + jnp.sum(pieces[...].astype(f32) * scale, axis=0)
+    denom = local[:, HEAD + 128 : HEAD + 129] * near + jnp.sum(sums * scale, axis=0)
     attn[...] = total / denom
     heads = [attn[h * PAD : (h + 1) * PAD, :].astype(bf16) for h in range(QH)]
     for i in range(parts):
@@ -417,8 +425,9 @@
     inv_freq = rope_base ** (-(jnp.arange(HEAD // 2, dtype=f32) * 2.0) / HEAD)
     angles = position[:, None] * inv_freq[None, :]
 
-    queries, prefill_kv, sent, draft_kv, own_count, verify_kv = project(
-        cache_len, accepted, prefill_x, verify_x, attn_gain[None], w_query, w_keyval,
+    meta = jnp.where(jnp.arange(8, dtype=i32) == 0, cache_len[0], accepted[0])
+    queries, prefill_kv, near_kv, sent, draft_kv, own_count, verify_kv = project(
+        meta, prefill_x, verify_x, attn_gain[None], w_query, w_keyval,
         qk_gain, jnp.cos(angles), jnp.sin(angles), page_table, pool_pages * PAGE,
     )
 
@@ -432,7 +441,7 @@
 
     asked = beside(sent[None], 4)
     attn, own = prompts(
-        prompt_len, queries, prefill_kv, sent, draft_kv,
+        prompt_len, queries, near_kv, sent, draft_kv,
         page_pool.reshape(pool_pages * PAGE, -1), own_count,
     )
     asked, attn = lax.optimization_barrier((asked, attn))

time: 66.8 us -> 66 us (0.988)
  Pallas kernels: 23.1 us -> 19.9 us
  starting transfers between devices: 29.6 us -> 32 us
    pallas_call x2, Pallas kernels: 11 us -> 8.03 us  [the longest x1 6.79 us: project(): pl.pallas_call(project_kernel, in_specs=[SMEM, VMEM, VMEM, VMEM, HBM, HBM...]
    all_to_all x1, waiting for transfers between devices: 6.08 us -> 4.23 us  [on_device(): lax.all_to_all(pieces, 'req', 0, 0, tiled=True, axis_index_groups=column)]
    all_to_all x1, starting transfers between devices: 6.25 us -> 8.1 us  [on_device(): lax.all_to_all(pieces, 'req', 0, 0, tiled=True, axis_index_groups=column)]
    ppermute x3, waiting for transfers between devices: 2.84 us -> 4.4 us  [beside(): return jnp.concatenate([values, lax.ppermute(values, 'req', pairs)], axis=0)]
    ppermute x2, starting transfers between devices: 6.47 us -> 7.15 us  [on_device(): other = lax.ppermute(partial, 'head', swap)]
  transfers between devices with their start and end apart: 7 -> 7, of which waited for: 3 -> 4; matrix products, arithmetic and copies ran while one was open for 1% -> 1% of each run, Pallas kernels for 26% -> 21%
where the time goes in v4:
time: 66 us; the launch traced here: 65.6 us
  starting transfers between devices  32 us (48%)
  Pallas kernels  19.9 us (30%)
  waiting for transfers between devices  9.53 us (14%)
  between operations  2.11 us (3%)
  local copies, waits for them, and re-layouts  1.26 us (2%)
  other arithmetic  0.84 us (1%)
    ppermute x3, starting transfers between devices, beside(): return jnp.concatenate([values, lax.ppermute(values, 'req', pairs)], axis=0)  9.03 us
    all_to_all x1, starting transfers between devices, on_device(): lax.all_to_all(pieces, 'req', 0, 0, tiled=True, axis_index_groups=column)  8.1 us
    all_to_all x1, starting transfers between devices, on_device(): lax.all_to_all(outgoing, 'req', 0, 0, tiled=True, axis_index_groups=plane)  7.73 us
    ppermute x2, starting transfers between devices, on_device(): other = lax.ppermute(partial, 'head', swap)  7.15 us
    pallas_call x1, Pallas kernels, project(): pl.pallas_call(project_kernel, in_specs=[SMEM, VMEM, VMEM, VMEM, HBM, HBM...  6.79 us
    ppermute x3, waiting for transfers between devices, beside(): return jnp.concatenate([values, lax.ppermute(values, 'req', pairs)], axis=0)  4.4 us
    all_to_all x1, waiting for transfers between devices, on_device(): lax.all_to_all(pieces, 'req', 0, 0, tiled=True, axis_index_groups=column)  4.23 us
    pallas_call x2, Pallas kernels, finish(): pl.pallas_call(finish_kernel, grid_spec=pltpu.PrefetchScalarGridSpec(num_...  3.18 us
  transfers between devices with their start and end apart: 7, of which 4 were waited for; matrix products, arithmetic and copies ran while one was open for 1% of the time, Pallas kernels for 21%

profile of v4, /device:TPU:1, one launch (start us, length us, event | category | flops | bytes accessed | tf_op | source)
XLA Modules:
  0.0 65.6 jit_solution(2457909649032876482)
XLA Ops:
  0.6 2.8 %pick_pages.1 = bf16[128,16,512]{2,1,0:T(8,128)(2,1)} custom-call(s32[1,128]{1,0:T(1,128)} %index.1, bf16[64,16,512]{2,1,0:T(8,128)(2,1)} %pool.1), custom_call_target="tpu_custom_call" | custom-call | bytes 4194304 | tf_op jit(solution)/shard_map/pick_pages/pallas_call | solution.py:48
  3.5 0.0 copy-start.7
  3.5 7.7 %all-to-all-start = ((bf16[128,16,512]{2,1,0:T(8,128)(2,1)}), bf16[128,16,512]{2,1,0:T(8,128)(2,1)S(1)}, u32[]{:S(2)}, u32[]{:S(2)}) async-start(bf16[128,16,512]{2,1,0:T(8,128)(2,1)} %pick_pages.1), calls=%async_computation | async-start | bytes 4194304 | tf_op jit(solution)/shard_map/all_to_all | solution.py:415
  12.5 0.1 select_reduce_fusion.1
  12.7 0.1 select_reduce_fusion
  12.8 0.6 multiply_sine_fusion
  13.4 6.8 %project.1 = (bf16[4,256,256]{2,1,0:T(8,128)(2,1)S(1)}, bf16[256,512]{1,0:T(8,128)(2,1)}, bf16[256,512]{1,0:T(8,128)(2,1)S(1)}, bf16[32,256]{1,0:T(8,128)(2,1)S(...) custom-call(s32[8]{0:T(128)S(1)} %compare_select_fusion.meta, bf16[256,2048]{1,0:T(8,128)(2,1)} %x.2, ...), custom_call_target="tpu_custom_call" | custom-call | flops 1711276032 | bytes 9437184 | tf_op jit(solution)/shard_map/project/pallas_call | solution.py:139
  20.2 7.0 %collective-permute-start = (bf16[1,32,256]{2,1,0:T(8,128)(2,1)S(1)}, bf16[1,32,256]{2,1,0:T(8,128)(2,1)S(1)}, u32[]{:S(2)}, u32[]{:S(2)}) collective-permute-start(bf16[1,32,256]{2,1,0:T(8,128)(2,1)S(1)} %bitcast.15), channel_id=1, source_target_pairs={{0,8},{2,10},{4,12},{6,14},{8,0},{10,2},{12,4},{14,6},{16,24},{18,... | collective-permute-start | bytes 49160 | tf_op jit(solution)/shard_map/ppermute | solution.py:440
  27.2 2.0 %prompts.1 = (bf16[256,1024]{1,0:T(8,128)(2,1)S(1)}, f32[32,512]{1,0:T(8,128)S(1)}) custom-call(s32[1,4]{1,0:T(1,128)S(1)} %copy-done.8, bf16[4,256,256]{2,1,0:T(8,128)(2,1)S(1)} %get-tuple-element.25.q, bf16[256,512]{1,0:T(8,128)(2,1)S(1)} %get-tuple-element.26.kv, bf16[32,256]{1,0:T(8,128)(2,1)S(1)} %get-tuple-element.24.query, ...), custom_call_target="tpu_custom_call" | custom-call | flops 268435456 | bytes 4194304 | tf_op jit(solution)/shard_map/prompts/pallas_call | solution.py:196
  29.3 1.3 %collective-permute-start.1 = (bf16[2,32,256]{2,1,0:T(8,128)(2,1)S(1)}, bf16[2,32,256]{2,1,0:T(8,128)(2,1)S(1)}, u32[]{:S(2)}, u32[]{:S(2)}) collective-permute-start(bf16[2,32,256]{2,1,0:T(8,128)(2,1)S(1)} %pad_maximum_fusion.2), channel_id=1, source_target_pairs={{0,4},{2,6},{4,0},{6,2},{8,12},{10,14},{12,8},{14,10},{16,20},{18,... | collective-permute-start | bytes 98312 | tf_op jit(solution)/shard_map/ppermute | solution.py:440
  30.5 1.2 %spread.1.own = bf16[256,2048]{1,0:T(8,128)(2,1)S(1)} custom-call(bf16[256,1024]{1,0:T(8,128)(2,1)S(1)} %get-tuple-element.31.attn, bf16[1024,2048]{1,0:T(8,128)(2,1)S(1)} %copy-done), custom_call_target="tpu_custom_call" | custom-call | flops 1073741824 | bytes 6291456 | tf_op jit(solution)/shard_map/spread/pallas_call | solution.py:219
  31.8 1.5 %collective-permute-done.1 = bf16[2,32,256]{2,1,0:T(8,128)(2,1)S(1)} collective-permute-done((bf16[2,32,256]{2,1,0:T(8,128)(2,1)S(1)}, bf16[2,32,256]{2,1,0:T(8,128)(2,1)S(1)}, u32[]{:S(2)}, u32[]{:S(2)}) %collective-permute-start.1) | collective-permute-done | bytes 32800 | tf_op jit(solution)/shard_map/ppermute | solution.py:440
  33.3 2.2 %collective-permute-start.3 = (bf16[256,2048]{1,0:T(8,128)(2,1)S(1)}, bf16[256,2048]{1,0:T(8,128)(2,1)}, u32[]{:S(2)}, u32[]{:S(2)}) collective-permute-start(bf16[256,2048]{1,0:T(8,128)(2,1)S(1)} %spread.1.own), channel_id=1, source_target_pairs={{0,1},{1,0},{2,3},{3,2},{4,5},{5,4},{6,7},{7,6},{8,9},{9,8},{10,11... | collective-permute-start | bytes 3145736 | tf_op jit(solution)/shard_map/ppermute | solution.py:452
  35.5 0.8 %collective-permute-start.2 = (bf16[4,32,256]{2,1,0:T(8,128)(2,1)S(1)}, bf16[4,32,256]{2,1,0:T(8,128)(2,1)S(1)}, u32[]{:S(2)}, u32[]{:S(2)}) collective-permute-start(bf16[4,32,256]{2,1,0:T(8,128)(2,1)S(1)} %pad_maximum_fusion.1), channel_id=1, source_target_pairs={{0,2},{2,0},{4,6},{6,4},{8,10},{10,8},{12,14},{14,12},{16,18},{18,... | collective-permute-start | bytes 196616 | tf_op jit(solution)/shard_map/ppermute | solution.py:440
  36.3 2.9 %collective-permute-done.2 = bf16[4,32,256]{2,1,0:T(8,128)(2,1)S(1)} collective-permute-done((bf16[4,32,256]{2,1,0:T(8,128)(2,1)S(1)}, bf16[4,32,256]{2,1,0:T(8,128)(2,1)S(1)}, u32[]{:S(2)}, u32[]{:S(2)}) %collective-permute-start.2) | collective-permute-done | bytes 65568 | tf_op jit(solution)/shard_map/ppermute | solution.py:440
  39.2 1.3 %remote_pieces.1 = bf16[8,32,256]{2,1,0:T(8,128)(2,1)} custom-call(s32[1]{0:T(128)} %bitcast.1.where, bf16[8,32,256]{2,1,0:T(8,128)(2,1)S(1)} %pad_maximum_fusion.queries, bf16[16,8,16,512]{3,2,1,0:T(8,128)(2,1)S(1)} %bitcast.13), custom_call_target="tpu_custom_call" | custom-call | flops 67108864 | bytes 3145728 | tf_op jit(solution)/shard_map/remote_pieces/pallas_call | solution.py:277
  40.5 8.1 %all-to-all-start.1 = ((bf16[8,32,256]{2,1,0:T(8,128)(2,1)}), bf16[8,32,256]{2,1,0:T(8,128)(2,1)S(1)}, u32[]{:S(2)}, u32[]{:S(2)}) async-start(bf16[8,32,256]{2,1,0:T(8,128)(2,1)} %remote_pieces.1), calls=%async_computation.1 | async-start | bytes 262144 | tf_op jit(solution)/shard_map/all_to_all | solution.py:456
  48.7 1.2 %copy-done.2 = bf16[256,2048]{1,0:T(8,128)(2,1)S(1)} copy-done((bf16[256,2048]{1,0:T(8,128)(2,1)S(1)}, bf16[256,2048]{1,0:T(8,128)(2,1)}, u32[]{:S(2)}) %copy-start.2) | copy-done | bytes 1048600
  49.9 2.5 %finish_prompts.1 = bf16[256,1024]{1,0:T(8,128)(2,1)} custom-call(s32[1]{0:T(128)} %bitcast.side, bf16[256,2048]{1,0:T(8,128)(2,1)S(1)} %spread.1.own, bf16[256,2048]{1,0:T(8,128)(2,1)} %collective-permute-done.3.other, bf16[256,2048]{1,0:T(8,128)(2,1)S(1)} %copy-done.2, f32[1,2048]{1,0:T(1,128)S(1)} %bitcast.17), custom_call_target="tpu_custom_call" | custom-call | flops 4194304 | bytes 3145728 | tf_op jit(solution)/shard_map/finish_prompts/pallas_call | solution.py:368
  52.3 4.2 %all-to-all-done.1.pieces = bf16[8,32,256]{2,1,0:T(8,128)(2,1)S(1)} async-done(((bf16[8,32,256]{2,1,0:T(8,128)(2,1)}), bf16[8,32,256]{2,1,0:T(8,128)(2,1)S(1)}, u32[]{:S(2)}, u32[]{:S(2)}) %all-to-all-start.1) | async-done | bytes 131104 | tf_op jit(solution)/shard_map/all_to_all | solution.py:456
  56.6 2.5 %join.1.own = f32[8,2048]{1,0:T(8,128)S(1)} custom-call(bf16[8,32,256]{2,1,0:T(8,128)(2,1)S(1)} %all-to-all-done.1.pieces, f32[32,512]{1,0:T(8,128)S(1)} %get-tuple-element.38.local, bf16[1024,2048]{1,0:T(8,128)(2,1)} %w_out.3), custom_call_target="tpu_custom_call" | custom-call | flops 33554432 | bytes 4194304 | tf_op jit(solution)/shard_map/join/pallas_call | solution.py:329
  59.1 5.0 %collective-permute-start.4 = (f32[8,2048]{1,0:T(8,128)S(1)}, f32[8,2048]{1,0:T(8,128)S(1)}, u32[]{:S(2)}, u32[]{:S(2)}) collective-permute-start(f32[8,2048]{1,0:T(8,128)S(1)} %join.1.own), channel_id=1, source_target_pairs={{0,1},{1,0},{2,3},{3,2},{4,5},{5,4},{6,7},{7,6},{8,9},{9,8},{10,11... | collective-permute-start | bytes 196616 | tf_op jit(solution)/shard_map/ppermute | solution.py:459
  64.0 0.9 %collective-permute-done.4.other = f32[8,2048]{1,0:T(8,128)S(1)} collective-permute-done((f32[8,2048]{1,0:T(8,128)S(1)}, f32[8,2048]{1,0:T(8,128)S(1)}, u32[]{:S(2)}, u32[]{:S(2)}) %collective-permute-start.4) | collective-permute-done | bytes 65568 | tf_op jit(solution)/shard_map/ppermute | solution.py:459
  64.9 0.7 %finish_drafts.1 = bf16[1,5,1024]{2,1,0:T(8,128)(2,1)} custom-call(s32[1]{0:T(128)} %bitcast.side, f32[8,2048]{1,0:T(8,128)S(1)} %join.1.own, f32[8,2048]{1,0:T(8,128)S(1)} %collective-permute-done.4.other, bf16[1,5,2048]{2,1,0:T(8,128)(2,1)S(1)} %copy-done.3, f32[1,2048]{1,0:T(1,128)S(1)} %bitcast.18), custom_call_target="tpu_custom_call" | custom-call | flops 131072 | bytes 98304 | tf_op jit(solution)/shard_map/finish_drafts/pallas_call | solution.py:368
  (27 shorter events, 0.1 us)
Async XLA Ops:
  3.5 9.1 %copy-start.8 = (s32[1,4]{1,0:T(1,128)S(1)}, s32[1,4]{1,0:T(1,128)}, u32[]{:S(2)}) copy-start(s32[1,4]{1,0:T(1,128)} %lengths.1) | copy-start | bytes 52
  3.5 9.9 %copy-start.3 = (bf16[1,5,2048]{2,1,0:T(8,128)(2,1)S(1)}, bf16[1,5,2048]{2,1,0:T(8,128)(2,1)}, u32[]{:S(2)}) copy-start(bf16[1,5,2048]{2,1,0:T(8,128)(2,1)} %x.3) | copy-start | bytes 61444
  3.5 9.9 %copy-start.5 = (f32[2048]{0:T(1024)S(1)}, f32[2048]{0:T(1024)}, u32[]{:S(2)}) copy-start(f32[2048]{0:T(1024)} %param.16) | copy-start | bytes 24580
  3.5 9.9 %copy-start.6 = (f32[2,256]{1,0:T(2,128)S(1)}, f32[2,256]{1,0:T(2,128)}, u32[]{:S(2)}) copy-start(f32[2,256]{1,0:T(2,128)} %qk_gain.1) | copy-start | bytes 6148
  3.5 9.9 %copy-start.7 = (s32[1,64]{1,0:T(1,128)S(1)}, s32[1,64]{1,0:T(1,128)}, u32[]{:S(2)}) copy-start(s32[1,64]{1,0:T(1,128)} %table.1) | copy-start | bytes 772
  3.5 35.7 %all-to-all-start = ((bf16[128,16,512]{2,1,0:T(8,128)(2,1)}), bf16[128,16,512]{2,1,0:T(8,128)(2,1)S(1)}, u32[]{:S(2)}, u32[]{:S(2)}) async-start(bf16[128,16,512]{2,1,0:T(8,128)(2,1)} %pick_pages.1), calls=%async_computation | async-start | bytes 4194304 | tf_op jit(solution)/shard_map/all_to_all | solution.py:415
  13.4 13.8 %copy-start.1 = (bf16[64,16,512]{2,1,0:T(8,128)(2,1)S(1)}, bf16[64,16,512]{2,1,0:T(8,128)(2,1)}, u32[]{:S(2)}) copy-start(bf16[64,16,512]{2,1,0:T(8,128)(2,1)} %pool.1) | copy-start | bytes 3145732
  13.4 17.1 %copy-start = (bf16[1024,2048]{1,0:T(8,128)(2,1)S(1)}, bf16[1024,2048]{1,0:T(8,128)(2,1)}, u32[]{:S(2)}) copy-start(bf16[1024,2048]{1,0:T(8,128)(2,1)} %w_out.3) | copy-start | bytes 12582916
  20.2 9.0 %collective-permute-start = (bf16[1,32,256]{2,1,0:T(8,128)(2,1)S(1)}, bf16[1,32,256]{2,1,0:T(8,128)(2,1)S(1)}, u32[]{:S(2)}, u32[]{:S(2)}) collective-permute-start(bf16[1,32,256]{2,1,0:T(8,128)(2,1)S(1)} %bitcast.15), channel_id=1, source_target_pairs={{0,8},{2,10},{4,12},{6,14},{8,0},{10,2},{12,4},{14,6},{16,24},{18,... | collective-permute-start | bytes 49160 | tf_op jit(solution)/shard_map/ppermute | solution.py:440
  29.3 4.0 %collective-permute-start.1 = (bf16[2,32,256]{2,1,0:T(8,128)(2,1)S(1)}, bf16[2,32,256]{2,1,0:T(8,128)(2,1)S(1)}, u32[]{:S(2)}, u32[]{:S(2)}) collective-permute-start(bf16[2,32,256]{2,1,0:T(8,128)(2,1)S(1)} %pad_maximum_fusion.2), channel_id=1, source_target_pairs={{0,4},{2,6},{4,0},{6,2},{8,12},{10,14},{12,8},{14,10},{16,20},{18,... | collective-permute-start | bytes 98312 | tf_op jit(solution)/shard_map/ppermute | solution.py:440
  31.8 16.8 %copy-start.4 = (f32[2048]{0:T(1024)S(1)}, f32[2048]{0:T(1024)}, u32[]{:S(2)}) copy-start(f32[2048]{0:T(1024)} %param.21) | copy-start | bytes 24580
  33.3 7.2 %collective-permute-start.3 = (bf16[256,2048]{1,0:T(8,128)(2,1)S(1)}, bf16[256,2048]{1,0:T(8,128)(2,1)}, u32[]{:S(2)}, u32[]{:S(2)}) collective-permute-start(bf16[256,2048]{1,0:T(8,128)(2,1)S(1)} %spread.1.own), channel_id=1, source_target_pairs={{0,1},{1,0},{2,3},{3,2},{4,5},{5,4},{6,7},{7,6},{8,9},{9,8},{10,11... | collective-permute-start | bytes 3145736 | tf_op jit(solution)/shard_map/ppermute | solution.py:452
  35.5 3.7 %collective-permute-start.2 = (bf16[4,32,256]{2,1,0:T(8,128)(2,1)S(1)}, bf16[4,32,256]{2,1,0:T(8,128)(2,1)S(1)}, u32[]{:S(2)}, u32[]{:S(2)}) collective-permute-start(bf16[4,32,256]{2,1,0:T(8,128)(2,1)S(1)} %pad_maximum_fusion.1), channel_id=1, source_target_pairs={{0,2},{2,0},{4,6},{6,4},{8,10},{10,8},{12,14},{14,12},{16,18},{18,... | collective-permute-start | bytes 196616 | tf_op jit(solution)/shard_map/ppermute | solution.py:440
  40.5 16.0 %all-to-all-start.1 = ((bf16[8,32,256]{2,1,0:T(8,128)(2,1)}), bf16[8,32,256]{2,1,0:T(8,128)(2,1)S(1)}, u32[]{:S(2)}, u32[]{:S(2)}) async-start(bf16[8,32,256]{2,1,0:T(8,128)(2,1)} %remote_pieces.1), calls=%async_computation.1 | async-start | bytes 262144 | tf_op jit(solution)/shard_map/all_to_all | solution.py:456
  48.6 1.2 %copy-start.2 = (bf16[256,2048]{1,0:T(8,128)(2,1)S(1)}, bf16[256,2048]{1,0:T(8,128)(2,1)}, u32[]{:S(2)}) copy-start(bf16[256,2048]{1,0:T(8,128)(2,1)} %x.2) | copy-start | bytes 3145732
  59.1 5.9 %collective-permute-start.4 = (f32[8,2048]{1,0:T(8,128)S(1)}, f32[8,2048]{1,0:T(8,128)S(1)}, u32[]{:S(2)}, u32[]{:S(2)}) collective-permute-start(f32[8,2048]{1,0:T(8,128)S(1)} %join.1.own), channel_id=1, source_target_pairs={{0,1},{1,0},{2,3},{3,2},{4,5},{5,4},{6,7},{7,6},{8,9},{9,8},{10,11... | collective-permute-start | bytes 196616 | tf_op jit(solution)/shard_map/ppermute | solution.py:459

commit v5 on v4

--- a/solution.py
+++ b/solution.py
@@ -38,6 +38,17 @@
     return values * lax.rsqrt(jnp.mean(values * values, axis=-1, keepdims=True) + eps_norm)
 
 
+def tally(table, length, lanes, first, step):
+    slots = table.shape[1]
+    eye = iota((slots, slots), 0) == iota((slots, slots), 1)
+    page = jnp.sum(jnp.where(eye, table, 0), axis=1, keepdims=True)
+    base = iota((slots, 1), 0) * PAGE
+    lane = iota((slots, lanes), 1)
+    named = page == first + (lane >> 4) * step
+    valid = base + (lane & (PAGE - 1)) < length
+    return jnp.sum(jnp.where(named & valid, 1.0, 0.0), axis=0, keepdims=True)
+
+
 def pick_kernel(index, pool, out):
     for i in range(out.shape[0]):
         out[i] = pool[jnp.clip(index[0, i], 0, pool.shape[0] - 1)]
@@ -73,20 +84,7 @@
     wide[:drafted] = unit(draft[0].astype(f32)) * gain[...]
     normed[rows:] = wide[...].astype(bf16)
 
-    slots = table.shape[1]
-    eye = iota((slots, slots), 0) == iota((slots, slots), 1)
-    page = jnp.sum(jnp.where(eye, table[...], 0), axis=1, keepdims=True)
-    base = iota((slots, 1), 0) * PAGE
-
-    def tally(lanes, first, step):
-        lane = iota((slots, lanes), 1)
-        named = page == first + (lane >> 4) * step
-        valid = base + (lane & (PAGE - 1)) < meta[0]
-        return jnp.sum(jnp.where(named & valid, 1.0, 0.0), axis=0, keepdims=True)
-
-    own = own_count.shape[1]
-    own_count[...] = tally(own, 0, 1)
-    far = [tally(HEAD, own // PAGE + z, DEEP) for z in range(DEEP)]
+    own_count[...] = tally(table[...], meta[0], own_count.shape[1], 0, 1)
 
     half = HEAD // 2
     cos, sin = cosine[...], sine[...]
@@ -95,7 +93,6 @@
         a, b = values[:, :half], values[:, half:]
         return jnp.concatenate([a * cos - b * sin, b * cos + a * sin], axis=-1)
 
-    row = iota((PAD, HEAD), 0)
     keep = iota((PAD, HEAD), 0) < meta[1]
 
     for pair in range(3):
@@ -108,8 +105,6 @@
                 query = rotated(value * qk_gain[0:1, :])
                 queries[h] = query[:rows].astype(bf16)
                 mine = query[rows : rows + PAD]
-                mine = jnp.where(row == drafted, far[h], mine)
-                mine = jnp.where(row == drafted + 1, far[h + QH], mine)
                 rows_q[h * PAD : (h + 1) * PAD, :] = mine
                 continue
             if h == QH:
@@ -154,6 +149,83 @@
         ),
         name="project",
     )(meta, x, draft, gain, wq, wkv, qk_gain, cosine, sine, table)
+
+
+def pack_kernel(meta, draft, table, out, wide):
+    drafted, slots = draft.shape[1], table.shape[1]
+    wide[...] = jnp.zeros_like(wide)
+    wide[:drafted] = draft[0].astype(f32)
+    lane = iota((1, 128), 1)
+    size = jnp.where(lane == slots, meta[0] >> 3, jnp.where(lane == slots + 1, meta[0] & 7, 0))
+    wide[5:6, :128] = size.astype(f32)
+    wide[5:6, :slots] = table[...].astype(f32)
+    out[0] = wide[...].astype(bf16)
+
+
+def pack(meta, draft, table):
+    width = draft.shape[2]
+    return pl.pallas_call(
+        pack_kernel,
+        in_specs=[SMEM, VMEM, VMEM],
+        out_specs=VMEM,
+        out_shape=jax.ShapeDtypeStruct((1, PAD, width), bf16),
+        scratch_shapes=[pltpu.VMEM((PAD, width), f32)],
+        compiler_params=pltpu.CompilerParams(vmem_limit_bytes=4 << 20),
+        cost_estimate=pl.CostEstimate(flops=0, transcendentals=0, bytes_accessed=1 << 17),
+        name="pack",
+    )(meta, draft, table)
+
+
+def ask_kernel(where, x, gain, wq, qk_gain, cosine, sine, out, weights, sems):
+    groups = x.shape[0]
+    copies = []
+    for i in range(2):
+        cols = slice(i * 2 * HEAD, (i + 1) * 2 * HEAD)
+        copy = pltpu.make_async_copy(wq.at[:, cols], weights.at[i], sems.at[i])
+        copy.start()
+        copies.append(copy)
+    rows = x[...].astype(f32).reshape(groups * PAD, -1)
+    normed = (unit(rows) * gain[...]).astype(bf16)
+    counts = []
+    for e in range(groups):
+        note = x[e][5:6, :128].astype(f32).astype(i32)
+        size = jnp.sum(jnp.where(iota((1, 128), 1) == 64, note * 8, 0), keepdims=True)
+        size += jnp.sum(jnp.where(iota((1, 128), 1) == 65, note, 0), keepdims=True)
+        counts.append(tally(note[:, :64], size, HEAD, 64 + where[0], DEEP))
+    count = jnp.concatenate(counts, axis=0).reshape(groups, 1, HEAD)
+    half = HEAD // 2
+    cos, sin = cosine[...], sine[...]
+    mark = iota((groups, PAD, HEAD), 1) == 5
+    heads = []
+    for i in range(2):
+        copies[i].wait()
+        both = dot_n(normed, weights[i])
+        for j in range(2):
+            value = unit(both[:, j * HEAD : (j + 1) * HEAD]) * qk_gain[0:1, :]
+            a, b = value[:, :half], value[:, half:]
+            value = jnp.concatenate([a * cos - b * sin, b * cos + a * sin], axis=-1)
+            value = value.reshape(groups, PAD, HEAD)
+            heads.append(jnp.where(mark, count, value) if not heads else value)
+    out[...] = jnp.concatenate(heads, axis=1).astype(bf16)
+
+
+def ask(where, x, gain, wq, qk_gain, cosine, sine):
+    groups, _, width = x.shape
+    return pl.pallas_call(
+        ask_kernel,
+        in_specs=[SMEM, VMEM, VMEM, HBM, VMEM, VMEM, VMEM],
+        out_specs=VMEM,
+        out_shape=jax.ShapeDtypeStruct((groups, QH * PAD, HEAD), bf16),
+        scratch_shapes=[
+            pltpu.VMEM((2, width, 2 * HEAD), bf16),
+            pltpu.SemaphoreType.DMA((2,)),
+        ],
+        compiler_params=pltpu.CompilerParams(vmem_limit_bytes=BIG),
+        cost_estimate=pl.CostEstimate(
+            flops=2 * groups * PAD * width * QH * HEAD, transcendentals=0, bytes_accessed=5 << 20
+        ),
+        name="ask",
+    )(where, x, gain, wq, qk_gain, cosine, sine)
 
 
 def prompt_kernel(lengths, q, kv, query, draft_kv, pool, count, attn, local):
@@ -232,12 +304,11 @@
 def remote_kernel(where, queries, pages, out):
     here = where[0]
     groups, rows = queries.shape[0], queries.shape[1]
-    pick = iota((rows, HEAD), 0) == (here % QH) * PAD + 5 + here // QH
     asked = [here ^ mask for mask in ORDER]
     scores, counts = [], []
     for e in range(groups):
         query = queries[e]
-        count = jnp.sum(jnp.where(pick, query.astype(f32), 0.0), axis=0, keepdims=True)
+        count = query.astype(f32)[5:6, :]
         held = pages[:, asked[e], :, :HEAD].reshape(HEAD, HEAD)
         scores.append(jnp.where(count > 0.0, dot_t(query, held), neg_large))
         counts.append(jnp.broadcast_to(count, (rows, HEAD)))
@@ -411,9 +482,22 @@
     column = [list(range(i, i + DEEP)) for i in range(0, devices, DEEP)]
 
     outgoing = pick_pages(outbound, page_pool)
-    outgoing, prefill_x = lax.optimization_barrier((outgoing, prefill_x))
+    outgoing, prefill_x, cache_len = lax.optimization_barrier((outgoing, prefill_x, cache_len))
     arrived = lax.all_to_all(outgoing, "req", 0, 0, tiled=True, axis_index_groups=plane)
 
+    meta = jnp.where(jnp.arange(8, dtype=i32) == 0, cache_len[0], accepted[0])
+    meta, verify_x = lax.optimization_barrier((meta, verify_x))
+    side = lax.axis_index("head").reshape(1)
+    where = (lax.axis_index("req") & (DEEP - 1)).reshape(1)
+    swap = [(0, 1), (1, 0)]
+
+    def beside(values, mask):
+        pairs = [(i, i ^ mask) for i in range(devices)]
+        return jnp.concatenate([values, lax.ppermute(values, "req", pairs)], axis=0)
+
+    asked = beside(pack(meta, verify_x, page_table), 4)
+
+    inv_freq = rope_base ** (-(jnp.arange(HEAD // 2, dtype=f32) * 2.0) / HEAD)
     lengths = prompt_len[0]
     order = jnp.arange(3, dtype=i32)[:, None] >= jnp.arange(4, dtype=i32)[None, :]
     ends = jnp.sum(jnp.where(order, lengths[None, :], 0), axis=1)
@@ -422,35 +506,32 @@
     position = jnp.concatenate(
         [row - start, cache_len[0] + jnp.arange(16, dtype=i32)]
     ).astype(f32)
-    inv_freq = rope_base ** (-(jnp.arange(HEAD // 2, dtype=f32) * 2.0) / HEAD)
     angles = position[:, None] * inv_freq[None, :]
 
-    meta = jnp.where(jnp.arange(8, dtype=i32) == 0, cache_len[0], accepted[0])
     queries, prefill_kv, near_kv, sent, draft_kv, own_count, verify_kv = project(
         meta, prefill_x, verify_x, attn_gain[None], w_query, w_keyval,
         qk_gain, jnp.cos(angles), jnp.sin(angles), page_table, pool_pages * PAGE,
     )
-
-    side = lax.axis_index("head").reshape(1)
-    where = (lax.axis_index("req") & (DEEP - 1)).reshape(1)
-    swap = [(0, 1), (1, 0)]
-
-    def beside(values, mask):
-        pairs = [(i, i ^ mask) for i in range(devices)]
-        return jnp.concatenate([values, lax.ppermute(values, "req", pairs)], axis=0)
-
-    asked = beside(sent[None], 4)
+    asked, queries = lax.optimization_barrier((asked, queries))
+    asked = beside(asked, 2)
     attn, own = prompts(
         prompt_len, queries, near_kv, sent, draft_kv,
         page_pool.reshape(pool_pages * PAGE, -1), own_count,
     )
-    asked, attn = lax.optimization_barrier((asked, attn))
-    asked = beside(asked, 2)
     partial = spread(attn, w_out)
     asked, partial = lax.optimization_barrier((asked, partial))
     asked = beside(asked, 1)
     other = lax.ppermute(partial, "head", swap)
-    pieces = remote_pieces(where, asked, arrived.reshape(planes, DEEP, PAGE, -1))
+
+    slots = page_table.shape[1]
+    size = asked[:, 5, slots : slots + 2].astype(f32)
+    position = (size[:, 0] * 8.0 + size[:, 1])[:, None] + jnp.arange(PAD, dtype=f32)[None, :]
+    angles = position.reshape(-1)[:, None] * inv_freq[None, :]
+    queries = ask(
+        where, asked, attn_gain[None], w_query, qk_gain, jnp.cos(angles), jnp.sin(angles)
+    )
+    arrived, queries = lax.optimization_barrier((arrived, queries))
+    pieces = remote_pieces(where, queries, arrived.reshape(planes, DEEP, PAGE, -1))
     pieces, other = lax.optimization_barrier((pieces, other))
     prefill_out = finish(side, partial, other, prefill_x, post_gain[None], "finish_prompts")
     pieces = lax.all_to_all(pieces, "req", 0, 0, tiled=True, axis_index_groups=column)

time: 66 us -> 66.4 us (level)
  starting transfers between devices: 32 us -> 26.4 us
  local copies, waits for them, and re-layouts: 1.26 us -> 5.5 us
  Pallas kernels: 19.9 us -> 23 us
  waiting for transfers between devices: 9.53 us -> 6.71 us
  other arithmetic: 0.84 us -> 1.94 us
    all_to_all x1, starting transfers between devices: 8.1 us -> 3.5 us  [on_device(): lax.all_to_all(pieces, 'req', 0, 0, tiled=True, axis_index_groups=column)]
    unnamed x18 -> x29, local copies, waits for them, and re-layouts: 1.26 us -> 5.32 us
    pallas_call x0 -> x2, Pallas kernels: none -> 3.66 us  [the longest x1 3.1 us: ask(): pl.pallas_call(ask_kernel, in_specs=[SMEM, VMEM, VMEM, HBM, VMEM, VMEM, V...]
    ppermute x3, waiting for transfers between devices: 4.4 us -> 1.57 us  [beside(): return jnp.concatenate([values, lax.ppermute(values, 'req', pairs)], axis=0)]
    ppermute x2, starting transfers between devices: 7.15 us -> 6.2 us  [on_device(): other = lax.ppermute(partial, 'head', swap)]
    concatenate x3 -> x2, other arithmetic: 0.04 us -> 0.78 us  [beside(): return jnp.concatenate([values, lax.ppermute(values, 'req', pairs)], axis=0)]
  transfers between devices with their start and end apart: 7 -> 7, of which waited for: 4 -> 3; matrix products, arithmetic and copies ran while one was open for 1% -> 3% of each run, Pallas kernels for 21% -> 26%
where the time goes in v5:
time: 66.4 us; the launch traced here: 65.8 us
  starting transfers between devices  26.4 us (40%)
  Pallas kernels  23 us (35%)
  waiting for transfers between devices  6.71 us (10%)
  local copies, waits for them, and re-layouts  5.5 us (8%)
  between operations  2.16 us (3%)
  other arithmetic  1.94 us (3%)
    ppermute x3, starting transfers between devices, beside(): return jnp.concatenate([values, lax.ppermute(values, 'req', pairs)], axis=0)  9.01 us
    all_to_all x1, starting transfers between devices, on_device(): lax.all_to_all(outgoing, 'req', 0, 0, tiled=True, axis_index_groups=plane)  7.73 us
    pallas_call x1, Pallas kernels, project(): pl.pallas_call(project_kernel, in_specs=[SMEM, VMEM, VMEM, VMEM, HBM, HBM...  6.26 us
    ppermute x2, starting transfers between devices, on_device(): other = lax.ppermute(partial, 'head', swap)  6.2 us
    unnamed x29, local copies, waits for them, and re-layouts  5.32 us
    all_to_all x1, waiting for transfers between devices, on_device(): lax.all_to_all(pieces, 'req', 0, 0, tiled=True, axis_index_groups=column)  4.23 us
    all_to_all x1, starting transfers between devices, on_device(): lax.all_to_all(pieces, 'req', 0, 0, tiled=True, axis_index_groups=column)  3.5 us
    pallas_call x2, Pallas kernels, finish(): pl.pallas_call(finish_kernel, grid_spec=pltpu.PrefetchScalarGridSpec(num_...  3.19 us
  transfers between devices with their start and end apart: 7, of which 3 were waited for; matrix products, arithmetic and copies ran while one was open for 3% of the time, Pallas kernels for 26%

profile of v5, /device:TPU:1, one launch (start us, length us, event | category | flops | bytes accessed | tf_op | source)
XLA Modules:
  0.0 65.8 jit_solution(17283351768167047613)
XLA Ops:
  0.6 2.8 %pick_pages.1 = bf16[128,16,512]{2,1,0:T(8,128)(2,1)} custom-call(s32[1,128]{1,0:T(1,128)} %index.1, bf16[64,16,512]{2,1,0:T(8,128)(2,1)} %pool.1), custom_call_target="tpu_custom_call" | custom-call | bytes 4194304 | tf_op jit(solution)/shard_map/pick_pages/pallas_call | solution.py:59
  3.5 7.7 %all-to-all-start = ((bf16[128,16,512]{2,1,0:T(8,128)(2,1)}), bf16[128,16,512]{2,1,0:T(8,128)(2,1)S(1)}, u32[]{:S(2)}, u32[]{:S(2)}) async-start(bf16[128,16,512]{2,1,0:T(8,128)(2,1)} %pick_pages.1), calls=%async_computation | async-start | bytes 4194304 | tf_op jit(solution)/shard_map/all_to_all | solution.py:486
  13.1 7.0 %collective-permute-start = (bf16[1,8,2048]{2,1,0:T(8,128)(2,1)S(1)}, bf16[1,8,2048]{2,1,0:T(8,128)(2,1)}, u32[]{:S(2)}, u32[]{:S(2)}) collective-permute-start(bf16[1,8,2048]{2,1,0:T(8,128)(2,1)S(1)} %pack.1), channel_id=1, source_target_pairs={{0,8},{2,10},{4,12},{6,14},{8,0},{10,2},{12,4},{14,6},{16,24},{18,... | collective-permute-start | bytes 98312 | tf_op jit(solution)/shard_map/ppermute | solution.py:496
  21.0 6.3 %project.1 = (bf16[4,256,256]{2,1,0:T(8,128)(2,1)S(1)}, bf16[256,512]{1,0:T(8,128)(2,1)}, bf16[256,512]{1,0:T(8,128)(2,1)S(1)}, bf16[32,256]{1,0:T(8,128)(2,1)S(...) custom-call(s32[8]{0:T(128)S(1)} %compare_select_fusion.meta, bf16[256,2048]{1,0:T(8,128)(2,1)} %x.1, ...), custom_call_target="tpu_custom_call" | custom-call | flops 1711276032 | bytes 9437184 | tf_op jit(solution)/shard_map/project/pallas_call | solution.py:134
  27.2 0.8 %copy-done.3 = bf16[4,256,256]{2,1,0:T(8,128)(2,1)} copy-done((bf16[4,256,256]{2,1,0:T(8,128)(2,1)}, bf16[4,256,256]{2,1,0:T(8,128)(2,1)S(1)}, u32[]{:S(2)}) %copy-start.3) | copy-done | bytes 524312
  28.0 0.8 %pad_maximum_fusion.1 = bf16[2,8,2048]{2,1,0:T(8,128)(2,1)S(1)} fusion(bf16[1,8,2048]{2,1,0:T(8,128)(2,1)} %collective-permute-done, bf16[1,8,2048]{2,1,0:T(8,128)(2,1)S(1)} %pack.1), kind=kLoop, calls=%fused_computation.3 | loop fusion | flops 32768 | bytes 131072 | tf_op jit(solution)/shard_map/concatenate | solution.py:496
  28.8 1.2 %collective-permute-start.1 = (bf16[2,8,2048]{2,1,0:T(8,128)(2,1)S(1)}, bf16[2,8,2048]{2,1,0:T(8,128)(2,1)S(1)}, u32[]{:S(2)}, u32[]{:S(2)}) collective-permute-start(bf16[2,8,2048]{2,1,0:T(8,128)(2,1)S(1)} %pad_maximum_fusion.1), channel_id=1, source_target_pairs={{0,4},{2,6},{4,0},{6,2},{8,12},{10,14},{12,8},{14,10},{16,20},{18,... | collective-permute-start | bytes 196616 | tf_op jit(solution)/shard_map/ppermute | solution.py:496
  30.0 1.0 %copy-done.4 = bf16[4,256,256]{2,1,0:T(8,128)(2,1)S(1)} copy-done((bf16[4,256,256]{2,1,0:T(8,128)(2,1)S(1)}, bf16[4,256,256]{2,1,0:T(8,128)(2,1)}, u32[]{:S(2)}) %copy-start.4) | copy-done | bytes 524312
  31.0 2.0 %prompts.1 = (bf16[256,1024]{1,0:T(8,128)(2,1)S(1)}, f32[32,512]{1,0:T(8,128)S(1)}) custom-call(s32[1,4]{1,0:T(1,128)S(1)} %copy-done.13, bf16[4,256,256]{2,1,0:T(8,128)(2,1)S(1)} %copy-done.4, bf16[256,512]{1,0:T(8,128)(2,1)S(1)} %get-tuple-element.36.kv, bf16[32,256]{1,0:T(8,128)(2,1)S(1)} %get-tuple-element.37.query, ...), custom_call_target="tpu_custom_call" | custom-call | flops 268435456 | bytes 4194304 | tf_op jit(solution)/shard_map/prompts/pallas_call | solution.py:268
  33.1 2.2 %copy-done = bf16[1024,2048]{1,0:T(8,128)(2,1)S(1)} copy-done((bf16[1024,2048]{1,0:T(8,128)(2,1)S(1)}, bf16[1024,2048]{1,0:T(8,128)(2,1)}, u32[]{:S(2)}) %copy-start) | copy-done | bytes 4194328
  35.3 1.2 %spread.1.own = bf16[256,2048]{1,0:T(8,128)(2,1)S(1)} custom-call(bf16[256,1024]{1,0:T(8,128)(2,1)S(1)} %get-tuple-element.40.attn, bf16[1024,2048]{1,0:T(8,128)(2,1)S(1)} %copy-done), custom_call_target="tpu_custom_call" | custom-call | flops 1073741824 | bytes 6291456 | tf_op jit(solution)/shard_map/spread/pallas_call | solution.py:291
  36.6 0.8 %collective-permute-start.2 = (bf16[4,8,2048]{2,1,0:T(8,128)(2,1)S(1)}, bf16[4,8,2048]{2,1,0:T(8,128)(2,1)S(1)}, u32[]{:S(2)}, u32[]{:S(2)}) collective-permute-start(bf16[4,8,2048]{2,1,0:T(8,128)(2,1)S(1)} %pad_maximum_fusion), channel_id=1, source_target_pairs={{0,2},{2,0},{4,6},{6,4},{8,10},{10,8},{12,14},{14,12},{16,18},{18,... | collective-permute-start | bytes 393224 | tf_op jit(solution)/shard_map/ppermute | solution.py:496
  37.4 1.8 %collective-permute-start.3 = (bf16[256,2048]{1,0:T(8,128)(2,1)S(1)}, bf16[256,2048]{1,0:T(8,128)(2,1)}, u32[]{:S(2)}, u32[]{:S(2)}) collective-permute-start(bf16[256,2048]{1,0:T(8,128)(2,1)S(1)} %spread.1.own), channel_id=1, source_target_pairs={{0,1},{1,0},{2,3},{3,2},{4,5},{5,4},{6,7},{7,6},{8,9},{9,8},{10,11... | collective-permute-start | bytes 3145736 | tf_op jit(solution)/shard_map/ppermute | solution.py:524
  39.2 1.6 %collective-permute-done.2 = bf16[4,8,2048]{2,1,0:T(8,128)(2,1)S(1)} collective-permute-done((bf16[4,8,2048]{2,1,0:T(8,128)(2,1)S(1)}, bf16[4,8,2048]{2,1,0:T(8,128)(2,1)S(1)}, u32[]{:S(2)}, u32[]{:S(2)}) %collective-permute-start.2) | collective-permute-done | bytes 131104 | tf_op jit(solution)/shard_map/ppermute | solution.py:496
  41.3 3.1 %ask.1.queries = bf16[8,32,256]{2,1,0:T(8,128)(2,1)S(1)} custom-call(s32[1]{0:T(128)} %bitcast.1.where, bf16[8,8,2048]{2,1,0:T(8,128)(2,1)S(1)} %constant_dynamic-update-slice_fusion.x, f32[1,2048]{1,0:T(1,128)S(1)} %bitcast.20, bf16[2048,1024]{1,0:T(8,128)(2,1)} %wq.3, f32[2,256]{1,0:T(2,128)S(1)} %copy-done.11, f32[64,128]{1,0:T(8,128)S(1)} %get-tuple-element.55.cosine, ...), custom_call_target="tpu_custom_call" | custom-call | flops 268435456 | bytes 5242880 | tf_op jit(solution)/shard_map/ask/pallas_call | solution.py:214
  44.5 1.3 %remote_pieces.1 = bf16[8,32,256]{2,1,0:T(8,128)(2,1)} custom-call(s32[1]{0:T(128)} %bitcast.1.where, bf16[8,32,256]{2,1,0:T(8,128)(2,1)S(1)} %ask.1.queries, bf16[16,8,16,512]{3,2,1,0:T(8,128)(2,1)S(1)} %bitcast.15), custom_call_target="tpu_custom_call" | custom-call | flops 67108864 | bytes 3145728 | tf_op jit(solution)/shard_map/remote_pieces/pallas_call | solution.py:348
  45.8 3.5 %all-to-all-start.1 = ((bf16[8,32,256]{2,1,0:T(8,128)(2,1)}), bf16[8,32,256]{2,1,0:T(8,128)(2,1)S(1)}, u32[]{:S(2)}, u32[]{:S(2)}) async-start(bf16[8,32,256]{2,1,0:T(8,128)(2,1)} %remote_pieces.1), calls=%async_computation.1 | async-start | bytes 262144 | tf_op jit(solution)/shard_map/all_to_all | solution.py:537
  49.3 1.2 %copy-done.2 = bf16[256,2048]{1,0:T(8,128)(2,1)S(1)} copy-done((bf16[256,2048]{1,0:T(8,128)(2,1)S(1)}, bf16[256,2048]{1,0:T(8,128)(2,1)}, u32[]{:S(2)}) %copy-start.2) | copy-done | bytes 1048600
  50.5 2.5 %finish_prompts.1 = bf16[256,1024]{1,0:T(8,128)(2,1)} custom-call(s32[1]{0:T(128)} %bitcast.side, bf16[256,2048]{1,0:T(8,128)(2,1)S(1)} %spread.1.own, bf16[256,2048]{1,0:T(8,128)(2,1)} %collective-permute-done.3.other, bf16[256,2048]{1,0:T(8,128)(2,1)S(1)} %copy-done.2, f32[1,2048]{1,0:T(1,128)S(1)} %bitcast.17), custom_call_target="tpu_custom_call" | custom-call | flops 4194304 | bytes 3145728 | tf_op jit(solution)/shard_map/finish_prompts/pallas_call | solution.py:439
  53.0 4.2 %all-to-all-done.1.pieces = bf16[8,32,256]{2,1,0:T(8,128)(2,1)S(1)} async-done(((bf16[8,32,256]{2,1,0:T(8,128)(2,1)}), bf16[8,32,256]{2,1,0:T(8,128)(2,1)S(1)}, u32[]{:S(2)}, u32[]{:S(2)}) %all-to-all-start.1) | async-done | bytes 131104 | tf_op jit(solution)/shard_map/all_to_all | solution.py:537
  57.3 2.5 %join.1.own = f32[8,2048]{1,0:T(8,128)S(1)} custom-call(bf16[8,32,256]{2,1,0:T(8,128)(2,1)S(1)} %all-to-all-done.1.pieces, f32[32,512]{1,0:T(8,128)S(1)} %copy-done.8, bf16[1024,2048]{1,0:T(8,128)(2,1)} %w_out.3), custom_call_target="tpu_custom_call" | custom-call | flops 33554432 | bytes 4194304 | tf_op jit(solution)/shard_map/join/pallas_call | solution.py:400
  59.8 4.4 %collective-permute-start.4 = (f32[8,2048]{1,0:T(8,128)S(1)}, f32[8,2048]{1,0:T(8,128)S(1)}, u32[]{:S(2)}, u32[]{:S(2)}) collective-permute-start(f32[8,2048]{1,0:T(8,128)S(1)} %join.1.own), channel_id=1, source_target_pairs={{0,1},{1,0},{2,3},{3,2},{4,5},{5,4},{6,7},{7,6},{8,9},{9,8},{10,11... | collective-permute-start | bytes 196616 | tf_op jit(solution)/shard_map/ppermute | solution.py:540
  64.2 0.9 %collective-permute-done.4.other = f32[8,2048]{1,0:T(8,128)S(1)} collective-permute-done((f32[8,2048]{1,0:T(8,128)S(1)}, f32[8,2048]{1,0:T(8,128)S(1)}, u32[]{:S(2)}, u32[]{:S(2)}) %collective-permute-start.4) | collective-permute-done | bytes 65568 | tf_op jit(solution)/shard_map/ppermute | solution.py:540
  65.1 0.7 %finish_drafts.1 = bf16[1,5,1024]{2,1,0:T(8,128)(2,1)} custom-call(s32[1]{0:T(128)} %bitcast.side, f32[8,2048]{1,0:T(8,128)S(1)} %join.1.own, f32[8,2048]{1,0:T(8,128)S(1)} %collective-permute-done.4.other, bf16[1,5,2048]{2,1,0:T(8,128)(2,1)S(1)} %copy-done.6, f32[1,2048]{1,0:T(1,128)S(1)} %bitcast.18), custom_call_target="tpu_custom_call" | custom-call | flops 131072 | bytes 98304 | tf_op jit(solution)/shard_map/finish_drafts/pallas_call | solution.py:439
  (46 shorter events, 2.0 us)
Async XLA Ops:
  3.5 9.1 %copy-start.5 = (bf16[1,5,2048]{2,1,0:T(8,128)(2,1)S(1)}, bf16[1,5,2048]{2,1,0:T(8,128)(2,1)}, u32[]{:S(2)}) copy-start(bf16[1,5,2048]{2,1,0:T(8,128)(2,1)} %x.2) | copy-start | bytes 61444
  3.5 9.1 %copy-start.12 = (s32[1,64]{1,0:T(1,128)S(1)}, s32[1,64]{1,0:T(1,128)}, u32[]{:S(2)}) copy-start(s32[1,64]{1,0:T(1,128)} %table.3) | copy-start | bytes 772
  3.5 16.7 %copy-start.13 = (s32[1,4]{1,0:T(1,128)S(1)}, s32[1,4]{1,0:T(1,128)}, u32[]{:S(2)}) copy-start(s32[1,4]{1,0:T(1,128)} %lengths.1) | copy-start | bytes 52
  3.5 17.5 %copy-start.10 = (f32[2048]{0:T(1024)S(1)}, f32[2048]{0:T(1024)}, u32[]{:S(2)}) copy-start(f32[2048]{0:T(1024)} %param.16) | copy-start | bytes 24580
  3.5 17.5 %copy-start.11 = (f32[2,256]{1,0:T(2,128)S(1)}, f32[2,256]{1,0:T(2,128)}, u32[]{:S(2)}) copy-start(f32[2,256]{1,0:T(2,128)} %qk_gain.3) | copy-start | bytes 6148
  3.5 41.0 %all-to-all-start = ((bf16[128,16,512]{2,1,0:T(8,128)(2,1)}), bf16[128,16,512]{2,1,0:T(8,128)(2,1)S(1)}, u32[]{:S(2)}, u32[]{:S(2)}) async-start(bf16[128,16,512]{2,1,0:T(8,128)(2,1)} %pick_pages.1), calls=%async_computation | async-start | bytes 4194304 | tf_op jit(solution)/shard_map/all_to_all | solution.py:486
  13.1 14.9 %collective-permute-start = (bf16[1,8,2048]{2,1,0:T(8,128)(2,1)S(1)}, bf16[1,8,2048]{2,1,0:T(8,128)(2,1)}, u32[]{:S(2)}, u32[]{:S(2)}) collective-permute-start(bf16[1,8,2048]{2,1,0:T(8,128)(2,1)S(1)} %pack.1), channel_id=1, source_target_pairs={{0,8},{2,10},{4,12},{6,14},{8,0},{10,2},{12,4},{14,6},{16,24},{18,... | collective-permute-start | bytes 98312 | tf_op jit(solution)/shard_map/ppermute | solution.py:496
  20.9 9.0 %copy-start.1 = (bf16[64,16,512]{2,1,0:T(8,128)(2,1)S(1)}, bf16[64,16,512]{2,1,0:T(8,128)(2,1)}, u32[]{:S(2)}) copy-start(bf16[64,16,512]{2,1,0:T(8,128)(2,1)} %pool.1) | copy-start | bytes 3145732
  27.2 0.8 %copy-start.3 = (bf16[4,256,256]{2,1,0:T(8,128)(2,1)}, bf16[4,256,256]{2,1,0:T(8,128)(2,1)S(1)}, u32[]{:S(2)}) copy-start(bf16[4,256,256]{2,1,0:T(8,128)(2,1)S(1)} %get-tuple-element.35.q) | copy-start | bytes 1572868
  28.8 7.8 %collective-permute-start.1 = (bf16[2,8,2048]{2,1,0:T(8,128)(2,1)S(1)}, bf16[2,8,2048]{2,1,0:T(8,128)(2,1)S(1)}, u32[]{:S(2)}, u32[]{:S(2)}) collective-permute-start(bf16[2,8,2048]{2,1,0:T(8,128)(2,1)S(1)} %pad_maximum_fusion.1), channel_id=1, source_target_pairs={{0,4},{2,6},{4,0},{6,2},{8,12},{10,14},{12,8},{14,10},{16,20},{18,... | collective-permute-start | bytes 196616 | tf_op jit(solution)/shard_map/ppermute | solution.py:496
  30.0 1.0 %copy-start.4 = (bf16[4,256,256]{2,1,0:T(8,128)(2,1)S(1)}, bf16[4,256,256]{2,1,0:T(8,128)(2,1)}, u32[]{:S(2)}) copy-start(bf16[4,256,256]{2,1,0:T(8,128)(2,1)} %copy-done.3) | copy-start | bytes 1572868
  33.1 3.5 %copy-start.7 = (f32[32,512]{1,0:T(8,128)}, f32[32,512]{1,0:T(8,128)S(1)}, u32[]{:S(2)}) copy-start(f32[32,512]{1,0:T(8,128)S(1)} %get-tuple-element.48.local) | copy-start | bytes 196612
  33.1 2.2 %copy-start = (bf16[1024,2048]{1,0:T(8,128)(2,1)S(1)}, bf16[1024,2048]{1,0:T(8,128)(2,1)}, u32[]{:S(2)}) copy-start(bf16[1024,2048]{1,0:T(8,128)(2,1)} %w_out.3) | copy-start | bytes 12582916
  36.6 4.2 %collective-permute-start.2 = (bf16[4,8,2048]{2,1,0:T(8,128)(2,1)S(1)}, bf16[4,8,2048]{2,1,0:T(8,128)(2,1)S(1)}, u32[]{:S(2)}, u32[]{:S(2)}) collective-permute-start(bf16[4,8,2048]{2,1,0:T(8,128)(2,1)S(1)} %pad_maximum_fusion), channel_id=1, source_target_pairs={{0,2},{2,0},{4,6},{6,4},{8,10},{10,8},{12,14},{14,12},{16,18},{18,... | collective-permute-start | bytes 393224 | tf_op jit(solution)/shard_map/ppermute | solution.py:496
  37.4 8.4 %collective-permute-start.3 = (bf16[256,2048]{1,0:T(8,128)(2,1)S(1)}, bf16[256,2048]{1,0:T(8,128)(2,1)}, u32[]{:S(2)}, u32[]{:S(2)}) collective-permute-start(bf16[256,2048]{1,0:T(8,128)(2,1)S(1)} %spread.1.own), channel_id=1, source_target_pairs={{0,1},{1,0},{2,3},{3,2},{4,5},{5,4},{6,7},{7,6},{8,9},{9,8},{10,11... | collective-permute-start | bytes 3145736 | tf_op jit(solution)/shard_map/ppermute | solution.py:524
  44.4 4.9 %copy-start.9 = (f32[2048]{0:T(1024)S(1)}, f32[2048]{0:T(1024)}, u32[]{:S(2)}) copy-start(f32[2048]{0:T(1024)} %param.21) | copy-start | bytes 24580
  45.8 11.5 %copy-start.8 = (f32[32,512]{1,0:T(8,128)S(1)}, f32[32,512]{1,0:T(8,128)}, u32[]{:S(2)}) copy-start(f32[32,512]{1,0:T(8,128)} %copy-done.7) | copy-start | bytes 196612
  45.8 11.4 %all-to-all-start.1 = ((bf16[8,32,256]{2,1,0:T(8,128)(2,1)}), bf16[8,32,256]{2,1,0:T(8,128)(2,1)S(1)}, u32[]{:S(2)}, u32[]{:S(2)}) async-start(bf16[8,32,256]{2,1,0:T(8,128)(2,1)} %remote_pieces.1), calls=%async_computation.1 | async-start | bytes 262144 | tf_op jit(solution)/shard_map/all_to_all | solution.py:537
  49.3 1.2 %copy-start.2 = (bf16[256,2048]{1,0:T(8,128)(2,1)S(1)}, bf16[256,2048]{1,0:T(8,128)(2,1)}, u32[]{:S(2)}) copy-start(bf16[256,2048]{1,0:T(8,128)(2,1)} %x.1) | copy-start | bytes 3145732
  57.3 7.8 %copy-start.6 = (bf16[1,5,2048]{2,1,0:T(8,128)(2,1)S(1)}, bf16[1,5,2048]{2,1,0:T(8,128)(2,1)}, u32[]{:S(2)}) copy-start(bf16[1,5,2048]{2,1,0:T(8,128)(2,1)} %x.2) | copy-start | bytes 61444
  59.8 5.3 %collective-permute-start.4 = (f32[8,2048]{1,0:T(8,128)S(1)}, f32[8,2048]{1,0:T(8,128)S(1)}, u32[]{:S(2)}, u32[]{:S(2)}) collective-permute-start(f32[8,2048]{1,0:T(8,128)S(1)} %join.1.own), channel_id=1, source_target_pairs={{0,1},{1,0},{2,3},{3,2},{4,5},{5,4},{6,7},{7,6},{8,9},{9,8},{10,11... | collective-permute-start | bytes 196616 | tf_op jit(solution)/shard_map/ppermute | solution.py:540

commit v6 on v5

--- a/solution.py
+++ b/solution.py
@@ -15,10 +15,10 @@
 eps_norm = 1e-06
 rope_base = 1000000.0
 neg_large = -1e30
-BIG = 52 << 20
 bf16, f32, i32 = jnp.bfloat16, jnp.float32, jnp.int32
 HBM = pl.BlockSpec(memory_space=pltpu.MemorySpace.HBM)
 VMEM = pl.BlockSpec(memory_space=pltpu.MemorySpace.VMEM)
+TOKEN = jax.ShapeDtypeStruct((8, 128), f32)
 SMEM = pl.BlockSpec(memory_space=pltpu.MemorySpace.SMEM)
 
 
@@ -49,7 +49,8 @@
     return jnp.sum(jnp.where(named & valid, 1.0, 0.0), axis=0, keepdims=True)
 
 
-def pick_kernel(index, pool, out):
+def pick_kernel(index, pool, out, token):
+    token[...] = jnp.zeros_like(token)
     for i in range(out.shape[0]):
         out[i] = pool[jnp.clip(index[0, i], 0, pool.shape[0] - 1)]
 
@@ -59,8 +60,8 @@
     return pl.pallas_call(
         pick_kernel,
         in_specs=[SMEM, VMEM],
-        out_specs=VMEM,
-        out_shape=jax.ShapeDtypeStruct((count,) + pool.shape[1:], pool.dtype),
+        out_specs=[VMEM, VMEM],
+        out_shape=[jax.ShapeDtypeStruct((count,) + pool.shape[1:], pool.dtype), TOKEN],
         cost_estimate=pl.CostEstimate(flops=0, transcendentals=0, bytes_accessed=4 << 20),
         name="pick_pages",
     )(index, pool)
@@ -143,7 +144,7 @@
             pltpu.VMEM((QH * PAD, HEAD), f32),
             pltpu.SemaphoreType.DMA((3,)),
         ],
-        compiler_params=pltpu.CompilerParams(vmem_limit_bytes=BIG),
+        compiler_params=pltpu.CompilerParams(vmem_limit_bytes=55 << 20),
         cost_estimate=pl.CostEstimate(
             flops=2 * total * width * 6 * HEAD, transcendentals=0, bytes_accessed=9 << 20
         ),
@@ -151,7 +152,7 @@
     )(meta, x, draft, gain, wq, wkv, qk_gain, cosine, sine, table)
 
 
-def pack_kernel(meta, draft, table, out, wide):
+def pack_kernel(meta, draft, table, after, out, wide):
     drafted, slots = draft.shape[1], table.shape[1]
     wide[...] = jnp.zeros_like(wide)
     wide[:drafted] = draft[0].astype(f32)
@@ -162,18 +163,18 @@
     out[0] = wide[...].astype(bf16)
 
 
-def pack(meta, draft, table):
+def pack(meta, draft, table, after):
     width = draft.shape[2]
     return pl.pallas_call(
         pack_kernel,
-        in_specs=[SMEM, VMEM, VMEM],
+        in_specs=[SMEM, VMEM, VMEM, VMEM],
         out_specs=VMEM,
         out_shape=jax.ShapeDtypeStruct((1, PAD, width), bf16),
         scratch_shapes=[pltpu.VMEM((PAD, width), f32)],
         compiler_params=pltpu.CompilerParams(vmem_limit_bytes=4 << 20),
         cost_estimate=pl.CostEstimate(flops=0, transcendentals=0, bytes_accessed=1 << 17),
         name="pack",
-    )(meta, draft, table)
+    )(meta, draft, table, after)
 
 
 def ask_kernel(where, x, gain, wq, qk_gain, cosine, sine, out, weights, sems):
@@ -220,7 +221,7 @@
             pltpu.VMEM((2, width, 2 * HEAD), bf16),
             pltpu.SemaphoreType.DMA((2,)),
         ],
-        compiler_params=pltpu.CompilerParams(vmem_limit_bytes=BIG),
+        compiler_params=pltpu.CompilerParams(vmem_limit_bytes=50 << 20),
         cost_estimate=pl.CostEstimate(
             flops=2 * groups * PAD * width * QH * HEAD, transcendentals=0, bytes_accessed=5 << 20
         ),
@@ -228,7 +229,17 @@
     )(where, x, gain, wq, qk_gain, cosine, sine)
 
 
-def prompt_kernel(lengths, q, kv, query, draft_kv, pool, count, attn, local):
+def prompt_kernel(
+    lengths, q, kv, query, draft_kv, pool, count, w_out, out, local, attn, weights, sems
+):
+    split = sems.shape[0]
+    cols = out.shape[1] // split
+    copies = []
+    for i in range(split):
+        part = slice(i * cols, (i + 1) * cols)
+        copy = pltpu.make_async_copy(w_out.at[:, part], weights.at[:, part], sems.at[i])
+        copy.start()
+        copies.append(copy)
     rows = attn.shape[0]
     row, col = iota((rows, rows), 0), iota((rows, rows), 1)
     start = jnp.zeros((rows, rows), i32)
@@ -262,46 +273,37 @@
     local[:, HEAD : HEAD + 128] = jnp.broadcast_to(peak, (QH * PAD, 128))
     local[:, HEAD + 128 :] = jnp.broadcast_to(denom, (QH * PAD, 128))
 
-
-def prompts(lengths, q, kv, query, draft_kv, pool, count):
+    for i in range(split):
+        copies[i].wait()
+        part = slice(i * cols, (i + 1) * cols)
+        out[:, part] = dot_n(attn[...], weights[:, part]).astype(bf16)
+
+
+def prompts(lengths, q, kv, query, draft_kv, pool, count, w_out):
     rows = kv.shape[0]
+    depth, width = w_out.shape
     return pl.pallas_call(
         prompt_kernel,
-        in_specs=[SMEM] + [VMEM] * 6,
+        in_specs=[SMEM] + [VMEM] * 6 + [HBM],
         out_specs=[VMEM, VMEM],
         out_shape=[
-            jax.ShapeDtypeStruct((rows, QH * HEAD), bf16),
+            jax.ShapeDtypeStruct((rows, width), bf16),
             jax.ShapeDtypeStruct((QH * PAD, 2 * HEAD), f32),
         ],
-        compiler_params=pltpu.CompilerParams(vmem_limit_bytes=16 << 20),
+        scratch_shapes=[
+            pltpu.VMEM((rows, depth), bf16),
+            pltpu.VMEM((depth, width), bf16),
+            pltpu.SemaphoreType.DMA((4,)),
+        ],
+        compiler_params=pltpu.CompilerParams(vmem_limit_bytes=54 << 20),
         cost_estimate=pl.CostEstimate(
             flops=16 * rows * rows * HEAD, transcendentals=4 * rows * rows, bytes_accessed=4 << 20
         ),
         name="prompts",
-    )(lengths, q, kv, query, draft_kv, pool, count)
-
-
-def spread_kernel(attn, w_out, out):
-    out[...] = dot_n(attn[...], w_out[...]).astype(bf16)
-
-
-def spread(attn, w_out):
-    rows = attn.shape[0]
-    depth, width = w_out.shape
-    return pl.pallas_call(
-        spread_kernel,
-        in_specs=[VMEM, VMEM],
-        out_specs=VMEM,
-        out_shape=jax.ShapeDtypeStruct((rows, width), bf16),
-        compiler_params=pltpu.CompilerParams(vmem_limit_bytes=12 << 20),
-        cost_estimate=pl.CostEstimate(
-            flops=2 * rows * depth * width, transcendentals=0, bytes_accessed=6 << 20
-        ),
-        name="spread",
-    )(attn, w_out)
-
-
-def remote_kernel(where, queries, pages, out):
+    )(lengths, q, kv, query, draft_kv, pool, count, w_out)
+
+
+def remote_kernel(where, queries, pages, after, out):
     here = where[0]
     groups, rows = queries.shape[0], queries.shape[1]
     asked = [here ^ mask for mask in ORDER]
@@ -343,17 +345,17 @@
 ORDER = (0, 4, 2, 6, 1, 5, 3, 7)
 
 
-def remote_pieces(where, queries, pages):
+def remote_pieces(where, queries, pages, after):
     groups, rows, _ = queries.shape
     return pl.pallas_call(
         remote_kernel,
-        in_specs=[SMEM, VMEM, VMEM],
+        in_specs=[SMEM, VMEM, VMEM, VMEM],
         out_specs=VMEM,
         out_shape=jax.ShapeDtypeStruct((groups, rows, HEAD), bf16),
         compiler_params=pltpu.CompilerParams(vmem_limit_bytes=12 << 20),
         cost_estimate=pl.CostEstimate(flops=1 << 26, transcendentals=1 << 16, bytes_accessed=3 << 20),
         name="remote_pieces",
-    )(where, queries, pages)
+    )(where, queries, pages, after)
 
 
 def join_kernel(pieces, local, w_out, out, attn, weights, sems):
@@ -407,13 +409,14 @@
             pltpu.VMEM((depth, width), bf16),
             pltpu.SemaphoreType.DMA((4,)),
         ],
-        compiler_params=pltpu.CompilerParams(vmem_limit_bytes=BIG),
+        compiler_params=pltpu.CompilerParams(vmem_limit_bytes=50 << 20),
         cost_estimate=pl.CostEstimate(flops=1 << 25, transcendentals=0, bytes_accessed=4 << 20),
         name="join",
     )(pieces, local, w_out)
 
 
-def finish_kernel(side, own, other, x, gain, out):
+def finish_kernel(side, own, other, x, gain, out, token):
+    token[...] = jnp.zeros_like(token)
     half = out.shape[-1]
     total = own[...].astype(f32) + other[...].astype(f32)
     scale = lax.rsqrt(jnp.mean(total * total, axis=-1, keepdims=True) + eps_norm)
@@ -447,9 +450,9 @@
                 x_spec,
                 pl.BlockSpec((1, half), lambda i, s: (0, s[0])),
             ],
-            out_specs=o_spec,
+            out_specs=[o_spec, pl.BlockSpec(TOKEN.shape, lambda i, s: (0, 0))],
         ),
-        out_shape=jax.ShapeDtypeStruct(shape, bf16),
+        out_shape=[jax.ShapeDtypeStruct(shape, bf16), TOKEN],
         compiler_params=pltpu.CompilerParams(vmem_limit_bytes=12 << 20),
         cost_estimate=pl.CostEstimate(
             flops=8 * rows * width, transcendentals=0, bytes_accessed=6 * rows * width
@@ -481,7 +484,7 @@
     planes = len(plane[0])
     column = [list(range(i, i + DEEP)) for i in range(0, devices, DEEP)]
 
-    outgoing = pick_pages(outbound, page_pool)
+    outgoing, picked = pick_pages(outbound, page_pool)
     outgoing, prefill_x, cache_len = lax.optimization_barrier((outgoing, prefill_x, cache_len))
     arrived = lax.all_to_all(outgoing, "req", 0, 0, tiled=True, axis_index_groups=plane)
 
@@ -495,7 +498,7 @@
         pairs = [(i, i ^ mask) for i in range(devices)]
         return jnp.concatenate([values, lax.ppermute(values, "req", pairs)], axis=0)
 
-    asked = beside(pack(meta, verify_x, page_table), 4)
+    asked = beside(pack(meta, verify_x, page_table, picked), 4)
 
     inv_freq = rope_base ** (-(jnp.arange(HEAD // 2, dtype=f32) * 2.0) / HEAD)
     lengths = prompt_len[0]
@@ -514,14 +517,14 @@
     )
     asked, queries = lax.optimization_barrier((asked, queries))
     asked = beside(asked, 2)
-    attn, own = prompts(
+    partial, own = prompts(
         prompt_len, queries, near_kv, sent, draft_kv,
-        page_pool.reshape(pool_pages * PAGE, -1), own_count,
-    )
-    partial = spread(attn, w_out)
+        page_pool.reshape(pool_pages * PAGE, -1), own_count, w_out,
+    )
     asked, partial = lax.optimization_barrier((asked, partial))
     asked = beside(asked, 1)
     other = lax.ppermute(partial, "head", swap)
+    prefill_out, done = finish(side, partial, other, prefill_x, post_gain[None], "finish_prompts")
 
     slots = page_table.shape[1]
     size = asked[:, 5, slots : slots + 2].astype(f32)
@@ -530,15 +533,13 @@
     queries = ask(
         where, asked, attn_gain[None], w_query, qk_gain, jnp.cos(angles), jnp.sin(angles)
     )
-    arrived, queries = lax.optimization_barrier((arrived, queries))
-    pieces = remote_pieces(where, queries, arrived.reshape(planes, DEEP, PAGE, -1))
-    pieces, other = lax.optimization_barrier((pieces, other))
-    prefill_out = finish(side, partial, other, prefill_x, post_gain[None], "finish_prompts")
+    pieces = remote_pieces(
+        where, queries, arrived.reshape(planes, DEEP, PAGE, -1), done
+    )
     pieces = lax.all_to_all(pieces, "req", 0, 0, tiled=True, axis_index_groups=column)
-    pieces, prefill_out = lax.optimization_barrier((pieces, prefill_out))
     partial = join(pieces, own, w_out)
     other = lax.ppermute(partial, "head", swap)
-    verify_out = finish(side, partial, other, verify_x, post_gain[None], "finish_drafts")
+    verify_out, _ = finish(side, partial, other, verify_x, post_gain[None], "finish_drafts")
     return (verify_out, prefill_out, verify_kv, prefill_kv)
 
 

time: 66.4 us -> 65.3 us (0.983)
  blocking collectives: 0 us -> 10.6 us
  local copies, waits for them, and re-layouts: 5.5 us -> 0.91 us
  waiting for transfers between devices: 6.71 us -> 2.48 us
  starting transfers between devices: 26.4 us -> 22.5 us
  Pallas kernels: 23 us -> 24.4 us
    all_to_all x0 -> x1, blocking collectives: none -> 10.6 us  [on_device(): lax.all_to_all(pieces, 'req', 0, 0, tiled=True, axis_index_groups=column)]
    unnamed x29 -> x25, local copies, waits for them, and re-layouts: 5.32 us -> 0.73 us
    all_to_all x1 -> x0, waiting for transfers between devices: 4.23 us -> none  [on_device(): lax.all_to_all(pieces, 'req', 0, 0, tiled=True, axis_index_groups=column)]
    all_to_all x1 -> x0, starting transfers between devices: 3.5 us -> none  [on_device(): lax.all_to_all(pieces, 'req', 0, 0, tiled=True, axis_index_groups=column)]
    pallas_call x5 -> x4, Pallas kernels: 8 us -> 10 us  [the longest x1 5.97 us: prompts(): pl.pallas_call(prompt_kernel, in_specs=[SMEM] + [VMEM] * 6 + [HBM], out_s...]
    pallas_call x2, Pallas kernels: 3.19 us -> 2.22 us  [finish(): pl.pallas_call(finish_kernel, grid_spec=pltpu.PrefetchScalarGridSpec(num_...]
    concatenate x2, other arithmetic: 0.78 us -> 0.02 us  [beside(): return jnp.concatenate([values, lax.ppermute(values, 'req', pairs)], axis=0)]
    sin x2, other arithmetic: 0.76 us -> 1.49 us  [on_device(): jnp.sin(angles)]
  transfers between devices with their start and end apart: 7 -> 6, of which waited for: 3 -> 2; matrix products, arithmetic and copies ran while one was open for 3% -> 3% of each run, Pallas kernels for 26% -> 27%
where the time goes in v6:
time: 65.3 us; the launch traced here: 64.9 us
  Pallas kernels  24.4 us (37%)
  starting transfers between devices  22.5 us (34%)
  blocking collectives  10.6 us (16%)
  waiting for transfers between devices  2.48 us (4%)
  between operations  2.15 us (3%)
  other arithmetic  1.91 us (3%)
  local copies, waits for them, and re-layouts  0.91 us (1%)
    all_to_all x1, blocking collectives, on_device(): lax.all_to_all(pieces, 'req', 0, 0, tiled=True, axis_index_groups=column)  10.6 us
    ppermute x3, starting transfers between devices, beside(): return jnp.concatenate([values, lax.ppermute(values, 'req', pairs)], axis=0)  9.1 us
    all_to_all x1, starting transfers between devices, on_device(): lax.all_to_all(outgoing, 'req', 0, 0, tiled=True, axis_index_groups=plane)  7.73 us
    pallas_call x1, Pallas kernels, project(): pl.pallas_call(project_kernel, in_specs=[SMEM, VMEM, VMEM, VMEM, HBM, HBM...  6.38 us
    pallas_call x1, Pallas kernels, prompts(): pl.pallas_call(prompt_kernel, in_specs=[SMEM] + [VMEM] * 6 + [HBM], out_s...  5.97 us
    ppermute x2, starting transfers between devices, on_device(): other = lax.ppermute(partial, 'head', swap)  5.68 us
    pallas_call x1, Pallas kernels, ask(): pl.pallas_call(ask_kernel, in_specs=[SMEM, VMEM, VMEM, HBM, VMEM, VMEM, V...  3.22 us
    pallas_call x1, Pallas kernels, pick_pages(): pl.pallas_call(pick_kernel, in_specs=[SMEM, VMEM], out_specs=[VMEM, VMEM]...  2.83 us
  transfers between devices with their start and end apart: 6, of which 2 were waited for; matrix products, arithmetic and copies ran while one was open for 3% of the time, Pallas kernels for 27%

profile of v6, /device:TPU:1, one launch (start us, length us, event | category | flops | bytes accessed | tf_op | source)
XLA Modules:
  0.0 64.9 jit_solution(6254185412114415111)
XLA Ops:
  0.6 2.8 %pick_pages.1 = (bf16[128,16,512]{2,1,0:T(8,128)(2,1)}, f32[8,128]{1,0:T(8,128)}) custom-call(s32[1,128]{1,0:T(1,128)} %index.1, bf16[64,16,512]{2,1,0:T(8,128)(2,1)} %pool.1), custom_call_target="tpu_custom_call" | custom-call | bytes 4194304 | tf_op jit(solution)/shard_map/pick_pages/pallas_call | solution.py:60
  3.5 7.7 %all-to-all-start = ((bf16[128,16,512]{2,1,0:T(8,128)(2,1)}), bf16[128,16,512]{2,1,0:T(8,128)(2,1)S(1)}, u32[]{:S(2)}, u32[]{:S(2)}) async-start(bf16[128,16,512]{2,1,0:T(8,128)(2,1)} %get-tuple-element.42), calls=%async_computation | async-start | bytes 4194304 | tf_op jit(solution)/shard_map/all_to_all | solution.py:489
  12.6 0.6 pack.1
  13.1 7.0 %collective-permute-start = (bf16[1,8,2048]{2,1,0:T(8,128)(2,1)S(1)}, bf16[1,8,2048]{2,1,0:T(8,128)(2,1)S(1)}, u32[]{:S(2)}, u32[]{:S(2)}) collective-permute-start(bf16[1,8,2048]{2,1,0:T(8,128)(2,1)S(1)} %pack.1), channel_id=1, source_target_pairs={{0,8},{2,10},{4,12},{6,14},{8,0},{10,2},{12,4},{14,6},{16,24},{18,... | collective-permute-start | bytes 98312 | tf_op jit(solution)/shard_map/ppermute | solution.py:499
  20.1 0.1 select_reduce_fusion.1
  20.3 0.1 select_reduce_fusion
  20.4 1.3 %multiply_sine_fusion = (f32[272,128]{1,0:T(8,128)}, f32[272,128]{1,0:T(8,128)}) fusion(f32[128]{0:T(128)S(1)} %multiply_power_fusion, f32[272]{0:T(512)S(1)} %add_convert_fusion), kind=kLoop, calls=%fused_computation | loop fusion | flops 34816 | bytes 280128 | tf_op jit(solution)/shard_map/sin | solution.py:516
  21.7 6.4 %project.1 = (bf16[4,256,256]{2,1,0:T(8,128)(2,1)}, bf16[256,512]{1,0:T(8,128)(2,1)}, bf16[256,512]{1,0:T(8,128)(2,1)}, bf16[32,256]{1,0:T(8,128)(2,1)}, f32[8,5...) custom-call(s32[8]{0:T(128)} %copy-done.10, bf16[256,2048]{1,0:T(8,128)(2,1)} %x.1, ...), custom_call_target="tpu_custom_call" | custom-call | flops 1711276032 | bytes 9437184 | tf_op jit(solution)/shard_map/project/pallas_call | solution.py:135
  28.1 1.3 %collective-permute-start.1 = (bf16[2,8,2048]{2,1,0:T(8,128)(2,1)S(1)}, bf16[2,8,2048]{2,1,0:T(8,128)(2,1)S(1)}, u32[]{:S(2)}, u32[]{:S(2)}) collective-permute-start(bf16[2,8,2048]{2,1,0:T(8,128)(2,1)S(1)} %pad_maximum_fusion.1), channel_id=1, source_target_pairs={{0,4},{2,6},{4,0},{6,2},{8,12},{10,14},{12,8},{14,10},{16,20},{18,... | collective-permute-start | bytes 196616 | tf_op jit(solution)/shard_map/ppermute | solution.py:499
  29.4 6.0 %prompts.1 = (bf16[256,2048]{1,0:T(8,128)(2,1)}, f32[32,512]{1,0:T(8,128)}) custom-call(s32[1,4]{1,0:T(1,128)} %lengths.1, bf16[4,256,256]{2,1,0:T(8,128)(2,1)} %get-tuple-element.35.q, bf16[256,512]{1,0:T(8,128)(2,1)} %get-tuple-element.36.kv, bf16[32,256]{1,0:T(8,128)(2,1)} %get-tuple-element.37.query, f32[8,512]{1,0:T(8,128)} %get-tuple-element.38.draft_kv, ...), custom_call_target="tpu_custom_call" | custom-call | flops 268435456 | bytes 4194304 | tf_op jit(solution)/shard_map/prompts/pallas_call | solution.py:285
  35.4 0.8 %collective-permute-start.2 = (bf16[4,8,2048]{2,1,0:T(8,128)(2,1)S(1)}, bf16[4,8,2048]{2,1,0:T(8,128)(2,1)S(1)}, u32[]{:S(2)}, u32[]{:S(2)}) collective-permute-start(bf16[4,8,2048]{2,1,0:T(8,128)(2,1)S(1)} %pad_maximum_fusion), channel_id=1, source_target_pairs={{0,2},{2,0},{4,6},{6,4},{8,10},{10,8},{12,14},{14,12},{16,18},{18,... | collective-permute-start | bytes 393224 | tf_op jit(solution)/shard_map/ppermute | solution.py:499
  36.2 1.8 %collective-permute-start.3 = (bf16[256,2048]{1,0:T(8,128)(2,1)}, bf16[256,2048]{1,0:T(8,128)(2,1)S(1)}, u32[]{:S(2)}, u32[]{:S(2)}) collective-permute-start(bf16[256,2048]{1,0:T(8,128)(2,1)} %get-tuple-element.43.own), channel_id=1, source_target_pairs={{0,1},{1,0},{2,3},{3,2},{4,5},{5,4},{6,7},{7,6},{8,9},{9,8},{10,11... | collective-permute-start | bytes 3145736 | tf_op jit(solution)/shard_map/ppermute | solution.py:526
  38.0 1.6 %collective-permute-done.2 = bf16[4,8,2048]{2,1,0:T(8,128)(2,1)S(1)} collective-permute-done((bf16[4,8,2048]{2,1,0:T(8,128)(2,1)S(1)}, bf16[4,8,2048]{2,1,0:T(8,128)(2,1)S(1)}, u32[]{:S(2)}, u32[]{:S(2)}) %collective-permute-start.2) | collective-permute-done | bytes 131104 | tf_op jit(solution)/shard_map/ppermute | solution.py:499
  39.7 0.1 copy.20
  39.9 0.2 multiply_sine_fusion.1
  40.2 0.7 %copy-done.7 = f32[2,256]{1,0:T(2,128)S(1)} copy-done((f32[2,256]{1,0:T(2,128)S(1)}, f32[2,256]{1,0:T(2,128)}, u32[]{:S(2)}) %copy-start.7) | copy-done | bytes 2072
  40.8 3.2 %ask.1.queries = bf16[8,32,256]{2,1,0:T(8,128)(2,1)S(1)} custom-call(s32[1]{0:T(128)} %bitcast.1.where, bf16[8,8,2048]{2,1,0:T(8,128)(2,1)S(1)} %constant_dynamic-update-slice_fusion.x, f32[1,2048]{1,0:T(1,128)S(1)} %bitcast.19, bf16[2048,1024]{1,0:T(8,128)(2,1)} %wq.3, f32[2,256]{1,0:T(2,128)S(1)} %copy-done.7, f32[64,128]{1,0:T(8,128)S(1)} %get-tuple-element.53.cosine, ...), custom_call_target="tpu_custom_call" | custom-call | flops 268435456 | bytes 5242880 | tf_op jit(solution)/shard_map/ask/pallas_call | solution.py:215
  44.1 1.5 %finish_prompts.1 = (bf16[256,1024]{1,0:T(8,128)(2,1)}, f32[8,128]{1,0:T(8,128)S(1)}) custom-call(s32[1]{0:T(128)} %bitcast.side, bf16[256,2048]{1,0:T(8,128)(2,1)S(1)} %copy-done.1, bf16[256,2048]{1,0:T(8,128)(2,1)S(1)} %collective-permute-done.3.other, bf16[256,2048]{1,0:T(8,128)(2,1)S(1)} %copy-done, f32[1,2048]{1,0:T(1,128)S(1)} %bitcast.16), custom_call_target="tpu_custom_call" | custom-call | flops 4194304 | bytes 3145728 | tf_op jit(solution)/shard_map/finish_prompts/pallas_call | solution.py:442
  45.6 0.7 %remote_pieces.1 = bf16[8,32,256]{2,1,0:T(8,128)(2,1)S(1)} custom-call(s32[1]{0:T(128)} %bitcast.1.where, bf16[8,32,256]{2,1,0:T(8,128)(2,1)S(1)} %ask.1.queries, bf16[16,8,16,512]{3,2,1,0:T(8,128)(2,1)S(1)} %bitcast.15, f32[8,128]{1,0:T(8,128)S(1)} %get-tuple-element.44.after), custom_call_target="tpu_custom_call" | custom-call | flops 67108864 | bytes 3145728 | tf_op jit(solution)/shard_map/remote_pieces/pallas_call | solution.py:350
  46.3 10.6 %all_to_all.10.pieces = bf16[8,32,256]{2,1,0:T(8,128)(2,1)S(1)} all-to-all(bf16[8,32,256]{2,1,0:T(8,128)(2,1)S(1)} %remote_pieces.1), channel_id=1, replica_groups={{0,2,4,6,8,10,12,14},{16,18,20,22,24,26,28,30},{32,34,36,38,40,42,44,46..., dimensions={0} | all-to-all | bytes 262144 | tf_op jit(solution)/shard_map/all_to_all | solution.py:539
  56.9 2.5 %join.1.own = f32[8,2048]{1,0:T(8,128)S(1)} custom-call(bf16[8,32,256]{2,1,0:T(8,128)(2,1)S(1)} %all_to_all.10.pieces, f32[32,512]{1,0:T(8,128)S(1)} %copy-done.4, bf16[1024,2048]{1,0:T(8,128)(2,1)} %w_out.3), custom_call_target="tpu_custom_call" | custom-call | flops 33554432 | bytes 4194304 | tf_op jit(solution)/shard_map/join/pallas_call | solution.py:402
  59.4 3.9 %collective-permute-start.4 = (f32[8,2048]{1,0:T(8,128)S(1)}, f32[8,2048]{1,0:T(8,128)S(1)}, u32[]{:S(2)}, u32[]{:S(2)}) collective-permute-start(f32[8,2048]{1,0:T(8,128)S(1)} %join.1.own), channel_id=1, source_target_pairs={{0,1},{1,0},{2,3},{3,2},{4,5},{5,4},{6,7},{7,6},{8,9},{9,8},{10,11... | collective-permute-start | bytes 196616 | tf_op jit(solution)/shard_map/ppermute | solution.py:541
  63.3 0.9 %collective-permute-done.4.other = f32[8,2048]{1,0:T(8,128)S(1)} collective-permute-done((f32[8,2048]{1,0:T(8,128)S(1)}, f32[8,2048]{1,0:T(8,128)S(1)}, u32[]{:S(2)}, u32[]{:S(2)}) %collective-permute-start.4) | collective-permute-done | bytes 65568 | tf_op jit(solution)/shard_map/ppermute | solution.py:541
  64.2 0.7 %finish_drafts.1 = (bf16[1,5,1024]{2,1,0:T(8,128)(2,1)}, f32[8,128]{1,0:T(8,128)}) custom-call(s32[1]{0:T(128)} %bitcast.side, f32[8,2048]{1,0:T(8,128)S(1)} %join.1.own, f32[8,2048]{1,0:T(8,128)S(1)} %collective-permute-done.4.other, bf16[1,5,2048]{2,1,0:T(8,128)(2,1)S(1)} %copy-done.3, f32[1,2048]{1,0:T(1,128)S(1)} %bitcast.17), custom_call_target="tpu_custom_call" | custom-call | flops 131072 | bytes 98304 | tf_op jit(solution)/shard_map/finish_drafts/pallas_call | solution.py:442
  (40 shorter events, 0.4 us)
Async XLA Ops:
  3.5 9.1 %copy-start.2 = (bf16[1,5,2048]{2,1,0:T(8,128)(2,1)S(1)}, bf16[1,5,2048]{2,1,0:T(8,128)(2,1)}, u32[]{:S(2)}) copy-start(bf16[1,5,2048]{2,1,0:T(8,128)(2,1)} %x.2) | copy-start | bytes 61444
  3.5 9.1 %copy-start.8 = (f32[8,128]{1,0:T(8,128)S(1)}, f32[8,128]{1,0:T(8,128)}, u32[]{:S(2)}) copy-start(f32[8,128]{1,0:T(8,128)} %get-tuple-element.31.after) | copy-start | bytes 12292
  3.5 9.1 %copy-start.9 = (s32[1,64]{1,0:T(1,128)S(1)}, s32[1,64]{1,0:T(1,128)}, u32[]{:S(2)}) copy-start(s32[1,64]{1,0:T(1,128)} %table.3) | copy-start | bytes 772
  3.5 16.7 %copy-start.11 = (s32[1,4]{1,0:T(1,128)S(1)}, s32[1,4]{1,0:T(1,128)}, u32[]{:S(2)}) copy-start(s32[1,4]{1,0:T(1,128)} %lengths.1) | copy-start | bytes 52
  3.5 42.1 %all-to-all-start = ((bf16[128,16,512]{2,1,0:T(8,128)(2,1)}), bf16[128,16,512]{2,1,0:T(8,128)(2,1)S(1)}, u32[]{:S(2)}, u32[]{:S(2)}) async-start(bf16[128,16,512]{2,1,0:T(8,128)(2,1)} %get-tuple-element.42), calls=%async_computation | async-start | bytes 4194304 | tf_op jit(solution)/shard_map/all_to_all | solution.py:489
  12.5 9.1 %copy-start.10 = (s32[8]{0:T(128)}, s32[8]{0:T(128)S(1)}, u32[]{:S(2)}) copy-start(s32[8]{0:T(128)S(1)} %compare_select_fusion.meta) | copy-start | bytes 100
  13.1 14.9 %collective-permute-start = (bf16[1,8,2048]{2,1,0:T(8,128)(2,1)S(1)}, bf16[1,8,2048]{2,1,0:T(8,128)(2,1)S(1)}, u32[]{:S(2)}, u32[]{:S(2)}) collective-permute-start(bf16[1,8,2048]{2,1,0:T(8,128)(2,1)S(1)} %pack.1), channel_id=1, source_target_pairs={{0,8},{2,10},{4,12},{6,14},{8,0},{10,2},{12,4},{14,6},{16,24},{18,... | collective-permute-start | bytes 98312 | tf_op jit(solution)/shard_map/ppermute | solution.py:499
  28.1 7.3 %collective-permute-start.1 = (bf16[2,8,2048]{2,1,0:T(8,128)(2,1)S(1)}, bf16[2,8,2048]{2,1,0:T(8,128)(2,1)S(1)}, u32[]{:S(2)}, u32[]{:S(2)}) collective-permute-start(bf16[2,8,2048]{2,1,0:T(8,128)(2,1)S(1)} %pad_maximum_fusion.1), channel_id=1, source_target_pairs={{0,4},{2,6},{4,0},{6,2},{8,12},{10,14},{12,8},{14,10},{16,20},{18,... | collective-permute-start | bytes 196616 | tf_op jit(solution)/shard_map/ppermute | solution.py:499
  29.4 10.8 %copy-start.6 = (f32[2048]{0:T(1024)S(1)}, f32[2048]{0:T(1024)}, u32[]{:S(2)}) copy-start(f32[2048]{0:T(1024)} %param.16) | copy-start | bytes 24580
  35.4 4.2 %collective-permute-start.2 = (bf16[4,8,2048]{2,1,0:T(8,128)(2,1)S(1)}, bf16[4,8,2048]{2,1,0:T(8,128)(2,1)S(1)}, u32[]{:S(2)}, u32[]{:S(2)}) collective-permute-start(bf16[4,8,2048]{2,1,0:T(8,128)(2,1)S(1)} %pad_maximum_fusion), channel_id=1, source_target_pairs={{0,2},{2,0},{4,6},{6,4},{8,10},{10,8},{12,14},{14,12},{16,18},{18,... | collective-permute-start | bytes 393224 | tf_op jit(solution)/shard_map/ppermute | solution.py:499
  36.2 7.9 %collective-permute-start.3 = (bf16[256,2048]{1,0:T(8,128)(2,1)}, bf16[256,2048]{1,0:T(8,128)(2,1)S(1)}, u32[]{:S(2)}, u32[]{:S(2)}) collective-permute-start(bf16[256,2048]{1,0:T(8,128)(2,1)} %get-tuple-element.43.own), channel_id=1, source_target_pairs={{0,1},{1,0},{2,3},{3,2},{4,5},{5,4},{6,7},{7,6},{8,9},{9,8},{10,11... | collective-permute-start | bytes 3145736 | tf_op jit(solution)/shard_map/ppermute | solution.py:526
  40.1 0.7 %copy-start.7 = (f32[2,256]{1,0:T(2,128)S(1)}, f32[2,256]{1,0:T(2,128)}, u32[]{:S(2)}) copy-start(f32[2,256]{1,0:T(2,128)} %qk_gain.3) | copy-start | bytes 6148
  40.8 3.2 %copy-start = (bf16[256,2048]{1,0:T(8,128)(2,1)S(1)}, bf16[256,2048]{1,0:T(8,128)(2,1)}, u32[]{:S(2)}) copy-start(bf16[256,2048]{1,0:T(8,128)(2,1)} %x.1) | copy-start | bytes 3145732
  40.8 3.3 %copy-start.1 = (bf16[256,2048]{1,0:T(8,128)(2,1)S(1)}, bf16[256,2048]{1,0:T(8,128)(2,1)}, u32[]{:S(2)}) copy-start(bf16[256,2048]{1,0:T(8,128)(2,1)} %get-tuple-element.43.own) | copy-start | bytes 3145732
  40.8 3.3 %copy-start.5 = (f32[2048]{0:T(1024)S(1)}, f32[2048]{0:T(1024)}, u32[]{:S(2)}) copy-start(f32[2048]{0:T(1024)} %param.21) | copy-start | bytes 24580
  45.6 11.3 %copy-start.4 = (f32[32,512]{1,0:T(8,128)S(1)}, f32[32,512]{1,0:T(8,128)}, u32[]{:S(2)}) copy-start(f32[32,512]{1,0:T(8,128)} %get-tuple-element.45.local) | copy-start | bytes 196612
  56.9 7.3 %copy-start.3 = (bf16[1,5,2048]{2,1,0:T(8,128)(2,1)S(1)}, bf16[1,5,2048]{2,1,0:T(8,128)(2,1)}, u32[]{:S(2)}) copy-start(bf16[1,5,2048]{2,1,0:T(8,128)(2,1)} %x.2) | copy-start | bytes 61444
  59.4 4.8 %collective-permute-start.4 = (f32[8,2048]{1,0:T(8,128)S(1)}, f32[8,2048]{1,0:T(8,128)S(1)}, u32[]{:S(2)}, u32[]{:S(2)}) collective-permute-start(f32[8,2048]{1,0:T(8,128)S(1)} %join.1.own), channel_id=1, source_target_pairs={{0,1},{1,0},{2,3},{3,2},{4,5},{5,4},{6,7},{7,6},{8,9},{9,8},{10,11... | collective-permute-start | bytes 196616 | tf_op jit(solution)/shard_map/ppermute | solution.py:541

commit v7 on v6

--- a/solution.py
+++ b/solution.py
@@ -2,6 +2,7 @@
 
 import jax
 import jax.numpy as jnp
+import numpy as np
 from jax import lax
 from jax.experimental import pallas as pl
 from jax.experimental.pallas import tpu as pltpu
@@ -68,7 +69,7 @@
 
 
 def project_kernel(
-    meta, x, draft, gain, wq, wkv, qk_gain, cosine, sine, table,
+    meta, lengths, x, draft, gain, wq, wkv, qk_gain, freq, table,
     queries, prompt_kv, near_kv, sent, draft_kv, own_count, verify_kv,
     weights, normed, wide, rows_q, sems,
 ):
@@ -88,7 +89,15 @@
     own_count[...] = tally(table[...], meta[0], own_count.shape[1], 0, 1)
 
     half = HEAD // 2
-    cos, sin = cosine[...], sine[...]
+    row = iota((normed.shape[0], half), 0)
+    start = jnp.zeros_like(row)
+    end = jnp.int32(0)
+    for i in range(3):
+        end = end + lengths[0, i]
+        start = jnp.where(row >= end, end, start)
+    position = jnp.where(row < rows, row - start, row - rows + meta[0])
+    angles = position.astype(f32) * freq[...]
+    cos, sin = jnp.cos(angles), jnp.sin(angles)
 
     def rotated(values):
         a, b = values[:, :half], values[:, half:]
@@ -119,7 +128,7 @@
     sent[...] = rows_q[...].astype(bf16)
 
 
-def project(meta, x, draft, gain, wq, wkv, qk_gain, cosine, sine, table, own):
+def project(meta, lengths, x, draft, gain, wq, wkv, qk_gain, freq, table, own):
     rows, width = x.shape
     drafted = draft.shape[1]
     total = rows + 16
@@ -134,7 +143,7 @@
     ]
     return pl.pallas_call(
         project_kernel,
-        in_specs=[SMEM, VMEM, VMEM, VMEM, HBM, HBM, VMEM, VMEM, VMEM, VMEM],
+        in_specs=[SMEM, SMEM, VMEM, VMEM, VMEM, HBM, HBM, VMEM, VMEM, VMEM],
         out_specs=[VMEM] * len(shapes),
         out_shape=shapes,
         scratch_shapes=[
@@ -149,7 +158,7 @@
             flops=2 * total * width * 6 * HEAD, transcendentals=0, bytes_accessed=9 << 20
         ),
         name="project",
-    )(meta, x, draft, gain, wq, wkv, qk_gain, cosine, sine, table)
+    )(meta, lengths, x, draft, gain, wq, wkv, qk_gain, freq, table)
 
 
 def pack_kernel(meta, draft, table, after, out, wide):
@@ -177,7 +186,7 @@
     )(meta, draft, table, after)
 
 
-def ask_kernel(where, x, gain, wq, qk_gain, cosine, sine, out, weights, sems):
+def ask_kernel(where, x, gain, wq, qk_gain, freq, out, weights, sems):
     groups = x.shape[0]
     copies = []
     for i in range(2):
@@ -187,15 +196,18 @@
         copies.append(copy)
     rows = x[...].astype(f32).reshape(groups * PAD, -1)
     normed = (unit(rows) * gain[...]).astype(bf16)
-    counts = []
+    half = HEAD // 2
+    counts, starts = [], []
     for e in range(groups):
         note = x[e][5:6, :128].astype(f32).astype(i32)
         size = jnp.sum(jnp.where(iota((1, 128), 1) == 64, note * 8, 0), keepdims=True)
         size += jnp.sum(jnp.where(iota((1, 128), 1) == 65, note, 0), keepdims=True)
+        starts.append(jnp.broadcast_to(size, (PAD, half)))
         counts.append(tally(note[:, :64], size, HEAD, 64 + where[0], DEEP))
     count = jnp.concatenate(counts, axis=0).reshape(groups, 1, HEAD)
-    half = HEAD // 2
-    cos, sin = cosine[...], sine[...]
+    position = jnp.concatenate(starts, axis=0) + (iota((groups * PAD, half), 0) & (PAD - 1))
+    angles = position.astype(f32) * freq[...]
+    cos, sin = jnp.cos(angles), jnp.sin(angles)
     mark = iota((groups, PAD, HEAD), 1) == 5
     heads = []
     for i in range(2):
@@ -210,11 +222,11 @@
     out[...] = jnp.concatenate(heads, axis=1).astype(bf16)
 
 
-def ask(where, x, gain, wq, qk_gain, cosine, sine):
+def ask(where, x, gain, wq, qk_gain, freq):
     groups, _, width = x.shape
     return pl.pallas_call(
         ask_kernel,
-        in_specs=[SMEM, VMEM, VMEM, HBM, VMEM, VMEM, VMEM],
+        in_specs=[SMEM, VMEM, VMEM, HBM, VMEM, VMEM],
         out_specs=VMEM,
         out_shape=jax.ShapeDtypeStruct((groups, QH * PAD, HEAD), bf16),
         scratch_shapes=[
@@ -226,12 +238,14 @@
             flops=2 * groups * PAD * width * QH * HEAD, transcendentals=0, bytes_accessed=5 << 20
         ),
         name="ask",
-    )(where, x, gain, wq, qk_gain, cosine, sine)
+    )(where, x, gain, wq, qk_gain, freq)
 
 
 def prompt_kernel(
-    lengths, q, kv, query, draft_kv, pool, count, w_out, out, local, attn, weights, sems
+    lengths, q, kv, query, draft_kv, pages, count, w_out, out, local, attn, weights, pool, sems, pool_sem
 ):
+    fetch = pltpu.make_async_copy(pages, pool, pool_sem)
+    fetch.start()
     split = sems.shape[0]
     cols = out.shape[1] // split
     copies = []
@@ -255,6 +269,7 @@
         probs = (parts / jnp.sum(parts, axis=-1, keepdims=True)).astype(bf16)
         attn[:, h * HEAD : (h + 1) * HEAD] = dot_n(probs, value).astype(bf16)
 
+    fetch.wait()
     mine = query[...]
     times = count[...]
     scores = jnp.where(times > 0.0, dot_t(mine, pool[:, :HEAD]), neg_large)
@@ -284,7 +299,7 @@
     depth, width = w_out.shape
     return pl.pallas_call(
         prompt_kernel,
-        in_specs=[SMEM] + [VMEM] * 6 + [HBM],
+        in_specs=[SMEM] + [VMEM] * 4 + [HBM, VMEM, HBM],
         out_specs=[VMEM, VMEM],
         out_shape=[
             jax.ShapeDtypeStruct((rows, width), bf16),
@@ -293,7 +308,9 @@
         scratch_shapes=[
             pltpu.VMEM((rows, depth), bf16),
             pltpu.VMEM((depth, width), bf16),
+            pltpu.VMEM(pool.shape, bf16),
             pltpu.SemaphoreType.DMA((4,)),
+            pltpu.SemaphoreType.DMA,
         ],
         compiler_params=pltpu.CompilerParams(vmem_limit_bytes=54 << 20),
         cost_estimate=pl.CostEstimate(
@@ -488,8 +505,7 @@
     outgoing, prefill_x, cache_len = lax.optimization_barrier((outgoing, prefill_x, cache_len))
     arrived = lax.all_to_all(outgoing, "req", 0, 0, tiled=True, axis_index_groups=plane)
 
-    meta = jnp.where(jnp.arange(8, dtype=i32) == 0, cache_len[0], accepted[0])
-    meta, verify_x = lax.optimization_barrier((meta, verify_x))
+    meta = jnp.where(jnp.arange(8, dtype=i32) == 0, cache_len, accepted)
     side = lax.axis_index("head").reshape(1)
     where = (lax.axis_index("req") & (DEEP - 1)).reshape(1)
     swap = [(0, 1), (1, 0)]
@@ -500,20 +516,11 @@
 
     asked = beside(pack(meta, verify_x, page_table, picked), 4)
 
-    inv_freq = rope_base ** (-(jnp.arange(HEAD // 2, dtype=f32) * 2.0) / HEAD)
-    lengths = prompt_len[0]
-    order = jnp.arange(3, dtype=i32)[:, None] >= jnp.arange(4, dtype=i32)[None, :]
-    ends = jnp.sum(jnp.where(order, lengths[None, :], 0), axis=1)
-    row = jnp.arange(rows, dtype=i32)
-    start = jnp.max(jnp.where(row[:, None] >= ends[None, :], ends[None, :], 0), axis=1)
-    position = jnp.concatenate(
-        [row - start, cache_len[0] + jnp.arange(16, dtype=i32)]
-    ).astype(f32)
-    angles = position[:, None] * inv_freq[None, :]
-
+    power = -(np.arange(HEAD // 2, dtype=np.float64) * 2.0) / HEAD
+    freq = jnp.asarray((rope_base**power)[None], f32)
     queries, prefill_kv, near_kv, sent, draft_kv, own_count, verify_kv = project(
-        meta, prefill_x, verify_x, attn_gain[None], w_query, w_keyval,
-        qk_gain, jnp.cos(angles), jnp.sin(angles), page_table, pool_pages * PAGE,
+        meta, prompt_len, prefill_x, verify_x, attn_gain[None], w_query, w_keyval,
+        qk_gain, freq, page_table, pool_pages * PAGE,
     )
     asked, queries = lax.optimization_barrier((asked, queries))
     asked = beside(asked, 2)
@@ -526,13 +533,7 @@
     other = lax.ppermute(partial, "head", swap)
     prefill_out, done = finish(side, partial, other, prefill_x, post_gain[None], "finish_prompts")
 
-    slots = page_table.shape[1]
-    size = asked[:, 5, slots : slots + 2].astype(f32)
-    position = (size[:, 0] * 8.0 + size[:, 1])[:, None] + jnp.arange(PAD, dtype=f32)[None, :]
-    angles = position.reshape(-1)[:, None] * inv_freq[None, :]
-    queries = ask(
-        where, asked, attn_gain[None], w_query, qk_gain, jnp.cos(angles), jnp.sin(angles)
-    )
+    queries = ask(where, asked, attn_gain[None], w_query, qk_gain, freq)
     pieces = remote_pieces(
         where, queries, arrived.reshape(planes, DEEP, PAGE, -1), done
     )

time: 65.3 us -> 65.1 us (level)
  waiting for transfers between devices: 2.48 us -> 5.21 us
  other arithmetic: 1.91 us -> 0.05 us
  starting transfers between devices: 22.5 us -> 21.3 us
  Pallas kernels: 24.4 us -> 25.3 us
  local copies, waits for them, and re-layouts: 0.91 us -> 0.05 us
    ppermute x3, waiting for transfers between devices: 1.57 us -> 4.3 us  [beside(): return jnp.concatenate([values, lax.ppermute(values, 'req', pairs)], axis=0)]
    sin x2 -> x0, other arithmetic: 1.49 us -> none  [on_device(): jnp.sin(angles)]
    ppermute x2, starting transfers between devices: 5.68 us -> 4.55 us  [on_device(): other = lax.ppermute(partial, 'head', swap)]
    pallas_call x3, Pallas kernels: 15.6 us -> 16.6 us  [the longest x1 6.85 us: prompts(): pl.pallas_call(prompt_kernel, in_specs=[SMEM] + [VMEM] * 4 + [HBM, VMEM,...]
    unnamed x25 -> x24, local copies, waits for them, and re-layouts: 0.73 us -> 0.05 us
  transfers between devices with their start and end apart: 6 -> 6, of which waited for: 2 -> 2; matrix products, arithmetic and copies ran while one was open for 3% -> 0% of each run, Pallas kernels for 27% -> 29%
where the time goes in v7:
time: 65.1 us; the launch traced here: 64.8 us
  Pallas kernels  25.3 us (39%)
  starting transfers between devices  21.3 us (33%)
  blocking collectives  10.7 us (16%)
  waiting for transfers between devices  5.21 us (8%)
  between operations  2.14 us (3%)
    all_to_all x1, blocking collectives, on_device(): lax.all_to_all(pieces, 'req', 0, 0, tiled=True, axis_index_groups=column)  10.7 us
    ppermute x3, starting transfers between devices, beside(): return jnp.concatenate([values, lax.ppermute(values, 'req', pairs)], axis=0)  9.04 us
    all_to_all x1, starting transfers between devices, on_device(): lax.all_to_all(outgoing, 'req', 0, 0, tiled=True, axis_index_groups=plane)  7.73 us
    pallas_call x1, Pallas kernels, prompts(): pl.pallas_call(prompt_kernel, in_specs=[SMEM] + [VMEM] * 4 + [HBM, VMEM,...  6.85 us
    pallas_call x1, Pallas kernels, project(): pl.pallas_call(project_kernel, in_specs=[SMEM, SMEM, VMEM, VMEM, VMEM, HB...  6.29 us
    ppermute x2, starting transfers between devices, on_device(): other = lax.ppermute(partial, 'head', swap)  4.55 us
    ppermute x3, waiting for transfers between devices, beside(): return jnp.concatenate([values, lax.ppermute(values, 'req', pairs)], axis=0)  4.3 us
    pallas_call x1, Pallas kernels, ask(): pl.pallas_call(ask_kernel, in_specs=[SMEM, VMEM, VMEM, HBM, VMEM, VMEM],...  3.44 us
  transfers between devices with their start and end apart: 6, of which 2 were waited for; matrix products, arithmetic and copies ran while one was open for 0% of the time, Pallas kernels for 29%

profile of v7, /device:TPU:1, one launch (start us, length us, event | category | flops | bytes accessed | tf_op | source)
XLA Modules:
  0.0 64.8 jit_solution(9781178005921423905)
XLA Ops:
  0.6 2.8 %pick_pages.1 = (bf16[128,16,512]{2,1,0:T(8,128)(2,1)}, f32[8,128]{1,0:T(8,128)}) custom-call(s32[1,128]{1,0:T(1,128)} %index.1, bf16[64,16,512]{2,1,0:T(8,128)(2,1)} %pool.1), custom_call_target="tpu_custom_call" | custom-call | bytes 4194304 | tf_op jit(solution)/shard_map/pick_pages/pallas_call | solution.py:61
  3.5 7.7 %all-to-all-start = ((bf16[128,16,512]{2,1,0:T(8,128)(2,1)}), bf16[128,16,512]{2,1,0:T(8,128)(2,1)S(1)}, u32[]{:S(2)}, u32[]{:S(2)}) async-start(bf16[128,16,512]{2,1,0:T(8,128)(2,1)} %get-tuple-element.38), calls=%async_computation | async-start | bytes 4194304 | tf_op jit(solution)/shard_map/all_to_all | solution.py:506
  12.5 0.6 pack.1
  13.1 7.0 %collective-permute-start = (bf16[1,8,2048]{2,1,0:T(8,128)(2,1)S(1)}, bf16[1,8,2048]{2,1,0:T(8,128)(2,1)S(1)}, u32[]{:S(2)}, u32[]{:S(2)}) collective-permute-start(bf16[1,8,2048]{2,1,0:T(8,128)(2,1)S(1)} %pack.1), channel_id=1, source_target_pairs={{0,8},{2,10},{4,12},{6,14},{8,0},{10,2},{12,4},{14,6},{16,24},{18,... | collective-permute-start | bytes 98312 | tf_op jit(solution)/shard_map/ppermute | solution.py:515
  20.1 6.3 %project.1 = (bf16[4,256,256]{2,1,0:T(8,128)(2,1)}, bf16[256,512]{1,0:T(8,128)(2,1)}, bf16[256,512]{1,0:T(8,128)(2,1)}, bf16[32,256]{1,0:T(8,128)(2,1)}, f32[8,5...) custom-call(s32[8]{0:T(128)} %copy-done.11, s32[1,4]{1,0:T(1,128)} %lengths.3, bf16[256,2048]{1,0:T(8,128)(2,1)} %x.2, ...), custom_call_target="tpu_custom_call" | custom-call | flops 1711276032 | bytes 9437184 | tf_op jit(solution)/shard_map/project/pallas_call | solution.py:144
  26.4 0.0 collective-permute-done
  26.4 1.3 %collective-permute-start.1 = (bf16[2,8,2048]{2,1,0:T(8,128)(2,1)S(1)}, bf16[2,8,2048]{2,1,0:T(8,128)(2,1)S(1)}, u32[]{:S(2)}, u32[]{:S(2)}) collective-permute-start(bf16[2,8,2048]{2,1,0:T(8,128)(2,1)S(1)} %pad_maximum_fusion.2), channel_id=1, source_target_pairs={{0,4},{2,6},{4,0},{6,2},{8,12},{10,14},{12,8},{14,10},{16,20},{18,... | collective-permute-start | bytes 196616 | tf_op jit(solution)/shard_map/ppermute | solution.py:515
  27.7 6.9 %prompts.1 = (bf16[256,2048]{1,0:T(8,128)(2,1)}, f32[32,512]{1,0:T(8,128)}) custom-call(s32[1,4]{1,0:T(1,128)} %lengths.3, bf16[4,256,256]{2,1,0:T(8,128)(2,1)} %get-tuple-element.31.q, bf16[256,512]{1,0:T(8,128)(2,1)} %get-tuple-element.32.kv, bf16[32,256]{1,0:T(8,128)(2,1)} %get-tuple-element.33.query, f32[8,512]{1,0:T(8,128)} %get-tuple-element.34.draft_kv, ...), custom_call_target="tpu_custom_call" | custom-call | flops 268435456 | bytes 4194304 | tf_op jit(solution)/shard_map/prompts/pallas_call | solution.py:300
  34.6 0.0 collective-permute-done.1
  34.6 1.6 %collective-permute-start.3 = (bf16[256,2048]{1,0:T(8,128)(2,1)}, bf16[256,2048]{1,0:T(8,128)(2,1)S(1)}, u32[]{:S(2)}, u32[]{:S(2)}) collective-permute-start(bf16[256,2048]{1,0:T(8,128)(2,1)} %get-tuple-element.39.own), channel_id=1, source_target_pairs={{0,1},{1,0},{2,3},{3,2},{4,5},{5,4},{6,7},{7,6},{8,9},{9,8},{10,11... | collective-permute-start | bytes 3145736 | tf_op jit(solution)/shard_map/ppermute | solution.py:533
  36.2 0.8 %collective-permute-start.2 = (bf16[4,8,2048]{2,1,0:T(8,128)(2,1)S(1)}, bf16[4,8,2048]{2,1,0:T(8,128)(2,1)S(1)}, u32[]{:S(2)}, u32[]{:S(2)}) collective-permute-start(bf16[4,8,2048]{2,1,0:T(8,128)(2,1)S(1)} %pad_maximum_fusion.1), channel_id=1, source_target_pairs={{0,2},{2,0},{4,6},{6,4},{8,10},{10,8},{12,14},{14,12},{16,18},{18,... | collective-permute-start | bytes 393224 | tf_op jit(solution)/shard_map/ppermute | solution.py:515
  37.0 4.3 %collective-permute-done.2 = bf16[4,8,2048]{2,1,0:T(8,128)(2,1)S(1)} collective-permute-done((bf16[4,8,2048]{2,1,0:T(8,128)(2,1)S(1)}, bf16[4,8,2048]{2,1,0:T(8,128)(2,1)S(1)}, u32[]{:S(2)}, u32[]{:S(2)}) %collective-permute-start.2) | collective-permute-done | bytes 131104 | tf_op jit(solution)/shard_map/ppermute | solution.py:515
  41.3 0.0 copy-start
  41.4 0.0 copy-start.5
  41.4 3.4 %ask.1.queries = bf16[8,32,256]{2,1,0:T(8,128)(2,1)S(1)} custom-call(s32[1]{0:T(128)} %bitcast.1.where, bf16[8,8,2048]{2,1,0:T(8,128)(2,1)S(1)} %pad_maximum_fusion.x, f32[1,2048]{1,0:T(1,128)S(1)} %bitcast.14, bf16[2048,1024]{1,0:T(8,128)(2,1)} %wq.3, f32[2,256]{1,0:T(2,128)S(1)} %copy-done.7, f32[1,128]{1,0:T(1,128)S(1)} %copy-done.10), custom_call_target="tpu_custom_call" | custom-call | flops 268435456 | bytes 5242880 | tf_op jit(solution)/shard_map/ask/pallas_call | solution.py:227
  44.8 0.0 collective-permute-done.3.other
  44.8 1.5 %finish_prompts.1 = (bf16[256,1024]{1,0:T(8,128)(2,1)}, f32[8,128]{1,0:T(8,128)S(1)}) custom-call(s32[1]{0:T(128)} %bitcast.side, bf16[256,2048]{1,0:T(8,128)(2,1)S(1)} %copy-done.1, bf16[256,2048]{1,0:T(8,128)(2,1)S(1)} %collective-permute-done.3.other, bf16[256,2048]{1,0:T(8,128)(2,1)S(1)} %copy-done, f32[1,2048]{1,0:T(1,128)S(1)} %bitcast.11), custom_call_target="tpu_custom_call" | custom-call | flops 4194304 | bytes 3145728 | tf_op jit(solution)/shard_map/finish_prompts/pallas_call | solution.py:459
  46.4 0.0 all-to-all-done
  46.4 0.7 %remote_pieces.1 = bf16[8,32,256]{2,1,0:T(8,128)(2,1)S(1)} custom-call(s32[1]{0:T(128)} %bitcast.1.where, bf16[8,32,256]{2,1,0:T(8,128)(2,1)S(1)} %ask.1.queries, bf16[16,8,16,512]{3,2,1,0:T(8,128)(2,1)S(1)} %bitcast.10, f32[8,128]{1,0:T(8,128)S(1)} %get-tuple-element.40.after), custom_call_target="tpu_custom_call" | custom-call | flops 67108864 | bytes 3145728 | tf_op jit(solution)/shard_map/remote_pieces/pallas_call | solution.py:367
  47.0 10.7 %all_to_all.10.pieces = bf16[8,32,256]{2,1,0:T(8,128)(2,1)S(1)} all-to-all(bf16[8,32,256]{2,1,0:T(8,128)(2,1)S(1)} %remote_pieces.1), channel_id=1, replica_groups={{0,2,4,6,8,10,12,14},{16,18,20,22,24,26,28,30},{32,34,36,38,40,42,44,46..., dimensions={0} | all-to-all | bytes 262144 | tf_op jit(solution)/shard_map/all_to_all | solution.py:540
  57.7 2.5 %join.1.own = f32[8,2048]{1,0:T(8,128)S(1)} custom-call(bf16[8,32,256]{2,1,0:T(8,128)(2,1)S(1)} %all_to_all.10.pieces, f32[32,512]{1,0:T(8,128)S(1)} %copy-done.4, bf16[1024,2048]{1,0:T(8,128)(2,1)} %w_out.3), custom_call_target="tpu_custom_call" | custom-call | flops 33554432 | bytes 4194304 | tf_op jit(solution)/shard_map/join/pallas_call | solution.py:419
  60.2 2.9 %collective-permute-start.4 = (f32[8,2048]{1,0:T(8,128)S(1)}, f32[8,2048]{1,0:T(8,128)S(1)}, u32[]{:S(2)}, u32[]{:S(2)}) collective-permute-start(f32[8,2048]{1,0:T(8,128)S(1)} %join.1.own), channel_id=1, source_target_pairs={{0,1},{1,0},{2,3},{3,2},{4,5},{5,4},{6,7},{7,6},{8,9},{9,8},{10,11... | collective-permute-start | bytes 196616 | tf_op jit(solution)/shard_map/ppermute | solution.py:542
  63.1 0.9 %collective-permute-done.4.other = f32[8,2048]{1,0:T(8,128)S(1)} collective-permute-done((f32[8,2048]{1,0:T(8,128)S(1)}, f32[8,2048]{1,0:T(8,128)S(1)}, u32[]{:S(2)}, u32[]{:S(2)}) %collective-permute-start.4) | collective-permute-done | bytes 65568 | tf_op jit(solution)/shard_map/ppermute | solution.py:542
  64.0 0.7 %finish_drafts.1 = (bf16[1,5,1024]{2,1,0:T(8,128)(2,1)}, f32[8,128]{1,0:T(8,128)}) custom-call(s32[1]{0:T(128)} %bitcast.side, f32[8,2048]{1,0:T(8,128)S(1)} %join.1.own, f32[8,2048]{1,0:T(8,128)S(1)} %collective-permute-done.4.other, bf16[1,5,2048]{2,1,0:T(8,128)(2,1)S(1)} %copy-done.3, f32[1,2048]{1,0:T(1,128)S(1)} %bitcast.12), custom_call_target="tpu_custom_call" | custom-call | flops 131072 | bytes 98304 | tf_op jit(solution)/shard_map/finish_drafts/pallas_call | solution.py:459
  (26 shorter events, 0.1 us)
Async XLA Ops:
  3.5 9.1 %copy-start.2 = (bf16[1,5,2048]{2,1,0:T(8,128)(2,1)S(1)}, bf16[1,5,2048]{2,1,0:T(8,128)(2,1)}, u32[]{:S(2)}) copy-start(bf16[1,5,2048]{2,1,0:T(8,128)(2,1)} %x.3) | copy-start | bytes 61444
  3.5 9.1 %copy-start.8 = (f32[8,128]{1,0:T(8,128)S(1)}, f32[8,128]{1,0:T(8,128)}, u32[]{:S(2)}) copy-start(f32[8,128]{1,0:T(8,128)} %get-tuple-element.27.after) | copy-start | bytes 12292
  3.5 9.1 %copy-start.9 = (s32[1,64]{1,0:T(1,128)S(1)}, s32[1,64]{1,0:T(1,128)}, u32[]{:S(2)}) copy-start(s32[1,64]{1,0:T(1,128)} %table.3) | copy-start | bytes 772
  3.5 42.9 %all-to-all-start = ((bf16[128,16,512]{2,1,0:T(8,128)(2,1)}), bf16[128,16,512]{2,1,0:T(8,128)(2,1)S(1)}, u32[]{:S(2)}, u32[]{:S(2)}) async-start(bf16[128,16,512]{2,1,0:T(8,128)(2,1)} %get-tuple-element.38), calls=%async_computation | async-start | bytes 4194304 | tf_op jit(solution)/shard_map/all_to_all | solution.py:506
  12.5 7.6 %copy-start.11 = (s32[8]{0:T(128)}, s32[8]{0:T(128)S(1)}, u32[]{:S(2)}) copy-start(s32[8]{0:T(128)S(1)} %compare_select_fusion.meta) | copy-start | bytes 100
  13.1 13.3 %collective-permute-start = (bf16[1,8,2048]{2,1,0:T(8,128)(2,1)S(1)}, bf16[1,8,2048]{2,1,0:T(8,128)(2,1)S(1)}, u32[]{:S(2)}, u32[]{:S(2)}) collective-permute-start(bf16[1,8,2048]{2,1,0:T(8,128)(2,1)S(1)} %pack.1), channel_id=1, source_target_pairs={{0,8},{2,10},{4,12},{6,14},{8,0},{10,2},{12,4},{14,6},{16,24},{18,... | collective-permute-start | bytes 98312 | tf_op jit(solution)/shard_map/ppermute | solution.py:515
  26.4 8.2 %collective-permute-start.1 = (bf16[2,8,2048]{2,1,0:T(8,128)(2,1)S(1)}, bf16[2,8,2048]{2,1,0:T(8,128)(2,1)S(1)}, u32[]{:S(2)}, u32[]{:S(2)}) collective-permute-start(bf16[2,8,2048]{2,1,0:T(8,128)(2,1)S(1)} %pad_maximum_fusion.2), channel_id=1, source_target_pairs={{0,4},{2,6},{4,0},{6,2},{8,12},{10,14},{12,8},{14,10},{16,20},{18,... | collective-permute-start | bytes 196616 | tf_op jit(solution)/shard_map/ppermute | solution.py:515
  27.7 13.6 %copy-start.6 = (f32[2048]{0:T(1024)S(1)}, f32[2048]{0:T(1024)}, u32[]{:S(2)}) copy-start(f32[2048]{0:T(1024)} %param.17) | copy-start | bytes 24580
  27.7 13.6 %copy-start.7 = (f32[2,256]{1,0:T(2,128)S(1)}, f32[2,256]{1,0:T(2,128)}, u32[]{:S(2)}) copy-start(f32[2,256]{1,0:T(2,128)} %qk_gain.3) | copy-start | bytes 6148
  27.7 13.6 %copy-start.10 = (f32[1,128]{1,0:T(1,128)S(1)}, f32[1,128]{1,0:T(1,128)}, u32[]{:S(2)}) copy-start(f32[1,128]{1,0:T(1,128)} %constant.14.clone.freq) | copy-start | bytes 1540
  34.6 10.2 %collective-permute-start.3 = (bf16[256,2048]{1,0:T(8,128)(2,1)}, bf16[256,2048]{1,0:T(8,128)(2,1)S(1)}, u32[]{:S(2)}, u32[]{:S(2)}) collective-permute-start(bf16[256,2048]{1,0:T(8,128)(2,1)} %get-tuple-element.39.own), channel_id=1, source_target_pairs={{0,1},{1,0},{2,3},{3,2},{4,5},{5,4},{6,7},{7,6},{8,9},{9,8},{10,11... | collective-permute-start | bytes 3145736 | tf_op jit(solution)/shard_map/ppermute | solution.py:533
  36.2 5.1 %collective-permute-start.2 = (bf16[4,8,2048]{2,1,0:T(8,128)(2,1)S(1)}, bf16[4,8,2048]{2,1,0:T(8,128)(2,1)S(1)}, u32[]{:S(2)}, u32[]{:S(2)}) collective-permute-start(bf16[4,8,2048]{2,1,0:T(8,128)(2,1)S(1)} %pad_maximum_fusion.1), channel_id=1, source_target_pairs={{0,2},{2,0},{4,6},{6,4},{8,10},{10,8},{12,14},{14,12},{16,18},{18,... | collective-permute-start | bytes 393224 | tf_op jit(solution)/shard_map/ppermute | solution.py:515
  41.3 3.5 %copy-start = (bf16[256,2048]{1,0:T(8,128)(2,1)S(1)}, bf16[256,2048]{1,0:T(8,128)(2,1)}, u32[]{:S(2)}) copy-start(bf16[256,2048]{1,0:T(8,128)(2,1)} %x.2) | copy-start | bytes 3145732
  41.3 3.5 %copy-start.1 = (bf16[256,2048]{1,0:T(8,128)(2,1)S(1)}, bf16[256,2048]{1,0:T(8,128)(2,1)}, u32[]{:S(2)}) copy-start(bf16[256,2048]{1,0:T(8,128)(2,1)} %get-tuple-element.39.own) | copy-start | bytes 3145732
  41.4 3.5 %copy-start.5 = (f32[2048]{0:T(1024)S(1)}, f32[2048]{0:T(1024)}, u32[]{:S(2)}) copy-start(f32[2048]{0:T(1024)} %param.22) | copy-start | bytes 24580
  46.4 11.3 %copy-start.4 = (f32[32,512]{1,0:T(8,128)S(1)}, f32[32,512]{1,0:T(8,128)}, u32[]{:S(2)}) copy-start(f32[32,512]{1,0:T(8,128)} %get-tuple-element.41.local) | copy-start | bytes 196612
  57.7 6.4 %copy-start.3 = (bf16[1,5,2048]{2,1,0:T(8,128)(2,1)S(1)}, bf16[1,5,2048]{2,1,0:T(8,128)(2,1)}, u32[]{:S(2)}) copy-start(bf16[1,5,2048]{2,1,0:T(8,128)(2,1)} %x.3) | copy-start | bytes 61444
  60.2 3.9 %collective-permute-start.4 = (f32[8,2048]{1,0:T(8,128)S(1)}, f32[8,2048]{1,0:T(8,128)S(1)}, u32[]{:S(2)}, u32[]{:S(2)}) collective-permute-start(f32[8,2048]{1,0:T(8,128)S(1)} %join.1.own), channel_id=1, source_target_pairs={{0,1},{1,0},{2,3},{3,2},{4,5},{5,4},{6,7},{7,6},{8,9},{9,8},{10,11... | collective-permute-start | bytes 196616 | tf_op jit(solution)/shard_map/ppermute | solution.py:542

commit v8 on v7

--- a/solution.py
+++ b/solution.py
@@ -242,10 +242,8 @@
 
 
 def prompt_kernel(
-    lengths, q, kv, query, draft_kv, pages, count, w_out, out, local, attn, weights, pool, sems, pool_sem
+    lengths, q, kv, query, draft_kv, pool, count, w_out, out, local, attn, weights, sems
 ):
-    fetch = pltpu.make_async_copy(pages, pool, pool_sem)
-    fetch.start()
     split = sems.shape[0]
     cols = out.shape[1] // split
     copies = []
@@ -269,7 +267,6 @@
         probs = (parts / jnp.sum(parts, axis=-1, keepdims=True)).astype(bf16)
         attn[:, h * HEAD : (h + 1) * HEAD] = dot_n(probs, value).astype(bf16)
 
-    fetch.wait()
     mine = query[...]
     times = count[...]
     scores = jnp.where(times > 0.0, dot_t(mine, pool[:, :HEAD]), neg_large)
@@ -299,7 +296,7 @@
     depth, width = w_out.shape
     return pl.pallas_call(
         prompt_kernel,
-        in_specs=[SMEM] + [VMEM] * 4 + [HBM, VMEM, HBM],
+        in_specs=[SMEM] + [VMEM] * 6 + [HBM],
         out_specs=[VMEM, VMEM],
         out_shape=[
             jax.ShapeDtypeStruct((rows, width), bf16),
@@ -308,9 +305,7 @@
         scratch_shapes=[
             pltpu.VMEM((rows, depth), bf16),
             pltpu.VMEM((depth, width), bf16),
-            pltpu.VMEM(pool.shape, bf16),
             pltpu.SemaphoreType.DMA((4,)),
-            pltpu.SemaphoreType.DMA,
         ],
         compiler_params=pltpu.CompilerParams(vmem_limit_bytes=54 << 20),
         cost_estimate=pl.CostEstimate(
@@ -510,9 +505,12 @@
     where = (lax.axis_index("req") & (DEEP - 1)).reshape(1)
     swap = [(0, 1), (1, 0)]
 
-    def beside(values, mask):
-        pairs = [(i, i ^ mask) for i in range(devices)]
-        return jnp.concatenate([values, lax.ppermute(values, "req", pairs)], axis=0)
+    def beside(values, *masks):
+        parts = [values]
+        for mask in masks:
+            pairs = [(i, i ^ mask) for i in range(devices)]
+            parts.append(lax.ppermute(values, "req", pairs))
+        return jnp.concatenate(parts, axis=0)
 
     asked = beside(pack(meta, verify_x, page_table, picked), 4)
 
@@ -523,13 +521,12 @@
         qk_gain, freq, page_table, pool_pages * PAGE,
     )
     asked, queries = lax.optimization_barrier((asked, queries))
-    asked = beside(asked, 2)
+    asked = beside(asked, 2, 1, 3)
     partial, own = prompts(
         prompt_len, queries, near_kv, sent, draft_kv,
         page_pool.reshape(pool_pages * PAGE, -1), own_count, w_out,
     )
     asked, partial = lax.optimization_barrier((asked, partial))
-    asked = beside(asked, 1)
     other = lax.ppermute(partial, "head", swap)
     prefill_out, done = finish(side, partial, other, prefill_x, post_gain[None], "finish_prompts")
 

time: 65.1 us -> 65.2 us (level)
  waiting for transfers between devices: 5.21 us -> 0.92 us
  starting transfers between devices: 21.3 us -> 25.1 us
  local copies, waits for them, and re-layouts: 0.05 us -> 1.37 us
  Pallas kernels: 25.3 us -> 24.5 us
    ppermute x3 -> x4, waiting for transfers between devices: 4.3 us -> 0.01 us  [beside(): parts.append(lax.ppermute(values, 'req', pairs))]
    ppermute x2, starting transfers between devices: 4.55 us -> 6.76 us  [on_device(): other = lax.ppermute(partial, 'head', swap)]
    ppermute x3 -> x4, starting transfers between devices: 9.04 us -> 10.6 us  [beside(): parts.append(lax.ppermute(values, 'req', pairs))]
    unnamed x24, local copies, waits for them, and re-layouts: 0.05 us -> 1.37 us
    pallas_call x1, Pallas kernels: 6.85 us -> 5.98 us  [prompts(): pl.pallas_call(prompt_kernel, in_specs=[SMEM] + [VMEM] * 6 + [HBM], out_s...]
  transfers between devices with their start and end apart: 6 -> 7, of which waited for: 2 -> 1; matrix products, arithmetic and copies ran while one was open for 0% -> 0% of each run, Pallas kernels for 29% -> 27%
where the time goes in v8:
time: 65.2 us; the launch traced here: 64.8 us
  starting transfers between devices  25.1 us (38%)
  Pallas kernels  24.5 us (38%)
  blocking collectives  10.7 us (16%)
  between operations  2.11 us (3%)
  local copies, waits for them, and re-layouts  1.37 us (2%)
  waiting for transfers between devices  0.92 us (1%)
    all_to_all x1, blocking collectives, on_device(): lax.all_to_all(pieces, 'req', 0, 0, tiled=True, axis_index_groups=column)  10.7 us
    ppermute x4, starting transfers between devices, beside(): parts.append(lax.ppermute(values, 'req', pairs))  10.6 us
    all_to_all x1, starting transfers between devices, on_device(): lax.all_to_all(outgoing, 'req', 0, 0, tiled=True, axis_index_groups=plane)  7.73 us
    ppermute x2, starting transfers between devices, on_device(): other = lax.ppermute(partial, 'head', swap)  6.76 us
    pallas_call x1, Pallas kernels, project(): pl.pallas_call(project_kernel, in_specs=[SMEM, SMEM, VMEM, VMEM, VMEM, HB...  6.31 us
    pallas_call x1, Pallas kernels, prompts(): pl.pallas_call(prompt_kernel, in_specs=[SMEM] + [VMEM] * 6 + [HBM], out_s...  5.98 us
    pallas_call x1, Pallas kernels, ask(): pl.pallas_call(ask_kernel, in_specs=[SMEM, VMEM, VMEM, HBM, VMEM, VMEM],...  3.41 us
    pallas_call x1, Pallas kernels, pick_pages(): pl.pallas_call(pick_kernel, in_specs=[SMEM, VMEM], out_specs=[VMEM, VMEM]...  2.83 us
  transfers between devices with their start and end apart: 7, of which 1 were waited for; matrix products, arithmetic and copies ran while one was open for 0% of the time, Pallas kernels for 27%

profile of v8, /device:TPU:1, one launch (start us, length us, event | category | flops | bytes accessed | tf_op | source)
XLA Modules:
  0.0 64.8 jit_solution(628454141341874562)
XLA Ops:
  0.6 2.8 %pick_pages.1 = (bf16[128,16,512]{2,1,0:T(8,128)(2,1)}, f32[8,128]{1,0:T(8,128)}) custom-call(s32[1,128]{1,0:T(1,128)} %index.1, bf16[64,16,512]{2,1,0:T(8,128)(2,1)} %pool.1), custom_call_target="tpu_custom_call" | custom-call | bytes 4194304 | tf_op jit(solution)/shard_map/pick_pages/pallas_call | solution.py:61
  3.5 7.7 %all-to-all-start = ((bf16[128,16,512]{2,1,0:T(8,128)(2,1)}), bf16[128,16,512]{2,1,0:T(8,128)(2,1)S(1)}, u32[]{:S(2)}, u32[]{:S(2)}) async-start(bf16[128,16,512]{2,1,0:T(8,128)(2,1)} %get-tuple-element.38), calls=%async_computation | async-start | bytes 4194304 | tf_op jit(solution)/shard_map/all_to_all | solution.py:501
  12.6 0.6 pack.1
  13.1 7.0 %collective-permute-start = (bf16[1,8,2048]{2,1,0:T(8,128)(2,1)S(1)}, bf16[1,8,2048]{2,1,0:T(8,128)(2,1)S(1)}, u32[]{:S(2)}, u32[]{:S(2)}) collective-permute-start(bf16[1,8,2048]{2,1,0:T(8,128)(2,1)S(1)} %pack.1), channel_id=1, source_target_pairs={{0,8},{2,10},{4,12},{6,14},{8,0},{10,2},{12,4},{14,6},{16,24},{18,... | collective-permute-start | bytes 98312 | tf_op jit(solution)/shard_map/ppermute | solution.py:512
  20.1 6.3 %project.1 = (bf16[4,256,256]{2,1,0:T(8,128)(2,1)}, bf16[256,512]{1,0:T(8,128)(2,1)}, bf16[256,512]{1,0:T(8,128)(2,1)}, bf16[32,256]{1,0:T(8,128)(2,1)}, f32[8,5...) custom-call(s32[8]{0:T(128)} %copy-done.11, s32[1,4]{1,0:T(1,128)} %lengths.3, bf16[256,2048]{1,0:T(8,128)(2,1)} %x.2, ...), custom_call_target="tpu_custom_call" | custom-call | flops 1711276032 | bytes 9437184 | tf_op jit(solution)/shard_map/project/pallas_call | solution.py:144
  26.4 0.0 collective-permute-done
  26.5 1.7 %collective-permute-start.3 = (bf16[2,8,2048]{2,1,0:T(8,128)(2,1)S(1)}, bf16[2,8,2048]{2,1,0:T(8,128)(2,1)S(1)}, u32[]{:S(2)}, u32[]{:S(2)}) collective-permute-start(bf16[2,8,2048]{2,1,0:T(8,128)(2,1)S(1)} %pad_maximum_fusion.1), channel_id=1, source_target_pairs={{0,6},{2,4},{4,2},{6,0},{8,14},{10,12},{12,10},{14,8},{16,22},{18,... | collective-permute-start | bytes 196616 | tf_op jit(solution)/shard_map/ppermute | solution.py:512
  28.2 0.0 collective-permute-start.2
  28.2 1.9 %collective-permute-start.1 = (bf16[2,8,2048]{2,1,0:T(8,128)(2,1)S(1)}, bf16[2,8,2048]{2,1,0:T(8,128)(2,1)S(1)}, u32[]{:S(2)}, u32[]{:S(2)}) collective-permute-start(bf16[2,8,2048]{2,1,0:T(8,128)(2,1)S(1)} %pad_maximum_fusion.1), channel_id=1, source_target_pairs={{0,4},{2,6},{4,0},{6,2},{8,12},{10,14},{12,8},{14,10},{16,20},{18,... | collective-permute-start | bytes 196616 | tf_op jit(solution)/shard_map/ppermute | solution.py:512
  30.1 6.0 %prompts.1 = (bf16[256,2048]{1,0:T(8,128)(2,1)}, f32[32,512]{1,0:T(8,128)}) custom-call(s32[1,4]{1,0:T(1,128)} %lengths.3, bf16[4,256,256]{2,1,0:T(8,128)(2,1)} %get-tuple-element.31.q, bf16[256,512]{1,0:T(8,128)(2,1)} %get-tuple-element.32.kv, bf16[32,256]{1,0:T(8,128)(2,1)} %get-tuple-element.33.query, f32[8,512]{1,0:T(8,128)} %get-tuple-element.34.draft_kv, ...), custom_call_target="tpu_custom_call" | custom-call | flops 268435456 | bytes 4194304 | tf_op jit(solution)/shard_map/prompts/pallas_call | solution.py:297
  36.1 0.0 collective-permute-done.3
  36.1 0.0 collective-permute-done.2
  36.1 0.0 collective-permute-done.1
  36.2 2.2 %collective-permute-start.4 = (bf16[256,2048]{1,0:T(8,128)(2,1)}, bf16[256,2048]{1,0:T(8,128)(2,1)S(1)}, u32[]{:S(2)}, u32[]{:S(2)}) collective-permute-start(bf16[256,2048]{1,0:T(8,128)(2,1)} %get-tuple-element.39.own), channel_id=1, source_target_pairs={{0,1},{1,0},{2,3},{3,2},{4,5},{5,4},{6,7},{7,6},{8,9},{9,8},{10,11... | collective-permute-start | bytes 3145736 | tf_op jit(solution)/shard_map/ppermute | solution.py:530
  38.3 0.7 %copy-done.7 = f32[2,256]{1,0:T(2,128)S(1)} copy-done((f32[2,256]{1,0:T(2,128)S(1)}, f32[2,256]{1,0:T(2,128)}, u32[]{:S(2)}) %copy-start.7) | copy-done | bytes 2072
  39.0 0.7 %copy-done.10 = f32[1,128]{1,0:T(1,128)S(1)} copy-done((f32[1,128]{1,0:T(1,128)S(1)}, f32[1,128]{1,0:T(1,128)}, u32[]{:S(2)}) %copy-start.10) | copy-done | bytes 536
  39.7 3.4 %ask.1.queries = bf16[8,32,256]{2,1,0:T(8,128)(2,1)S(1)} custom-call(s32[1]{0:T(128)} %bitcast.1.where, bf16[8,8,2048]{2,1,0:T(8,128)(2,1)S(1)} %pad_maximum_fusion.x, f32[1,2048]{1,0:T(1,128)S(1)} %bitcast.14, bf16[2048,1024]{1,0:T(8,128)(2,1)} %wq.3, f32[2,256]{1,0:T(2,128)S(1)} %copy-done.7, f32[1,128]{1,0:T(1,128)S(1)} %copy-done.10), custom_call_target="tpu_custom_call" | custom-call | flops 268435456 | bytes 5242880 | tf_op jit(solution)/shard_map/ask/pallas_call | solution.py:227
  43.1 1.5 %finish_prompts.1 = (bf16[256,1024]{1,0:T(8,128)(2,1)}, f32[8,128]{1,0:T(8,128)S(1)}) custom-call(s32[1]{0:T(128)} %bitcast.side, bf16[256,2048]{1,0:T(8,128)(2,1)S(1)} %copy-done.1, bf16[256,2048]{1,0:T(8,128)(2,1)S(1)} %collective-permute-done.4.other, bf16[256,2048]{1,0:T(8,128)(2,1)S(1)} %copy-done, f32[1,2048]{1,0:T(1,128)S(1)} %bitcast.11), custom_call_target="tpu_custom_call" | custom-call | flops 4194304 | bytes 3145728 | tf_op jit(solution)/shard_map/finish_prompts/pallas_call | solution.py:454
  44.7 0.7 %remote_pieces.1 = bf16[8,32,256]{2,1,0:T(8,128)(2,1)S(1)} custom-call(s32[1]{0:T(128)} %bitcast.1.where, bf16[8,32,256]{2,1,0:T(8,128)(2,1)S(1)} %ask.1.queries, bf16[16,8,16,512]{3,2,1,0:T(8,128)(2,1)S(1)} %bitcast.10, f32[8,128]{1,0:T(8,128)S(1)} %get-tuple-element.40.after), custom_call_target="tpu_custom_call" | custom-call | flops 67108864 | bytes 3145728 | tf_op jit(solution)/shard_map/remote_pieces/pallas_call | solution.py:362
  45.3 10.7 %all_to_all.10.pieces = bf16[8,32,256]{2,1,0:T(8,128)(2,1)S(1)} all-to-all(bf16[8,32,256]{2,1,0:T(8,128)(2,1)S(1)} %remote_pieces.1), channel_id=1, replica_groups={{0,2,4,6,8,10,12,14},{16,18,20,22,24,26,28,30},{32,34,36,38,40,42,44,46..., dimensions={0} | all-to-all | bytes 262144 | tf_op jit(solution)/shard_map/all_to_all | solution.py:537
  56.1 2.5 %join.1.own = f32[8,2048]{1,0:T(8,128)S(1)} custom-call(bf16[8,32,256]{2,1,0:T(8,128)(2,1)S(1)} %all_to_all.10.pieces, f32[32,512]{1,0:T(8,128)S(1)} %copy-done.4, bf16[1024,2048]{1,0:T(8,128)(2,1)} %w_out.3), custom_call_target="tpu_custom_call" | custom-call | flops 33554432 | bytes 4194304 | tf_op jit(solution)/shard_map/join/pallas_call | solution.py:414
  58.6 4.6 %collective-permute-start.5 = (f32[8,2048]{1,0:T(8,128)S(1)}, f32[8,2048]{1,0:T(8,128)S(1)}, u32[]{:S(2)}, u32[]{:S(2)}) collective-permute-start(f32[8,2048]{1,0:T(8,128)S(1)} %join.1.own), channel_id=1, source_target_pairs={{0,1},{1,0},{2,3},{3,2},{4,5},{5,4},{6,7},{7,6},{8,9},{9,8},{10,11... | collective-permute-start | bytes 196616 | tf_op jit(solution)/shard_map/ppermute | solution.py:539
  63.2 0.9 %collective-permute-done.5.other = f32[8,2048]{1,0:T(8,128)S(1)} collective-permute-done((f32[8,2048]{1,0:T(8,128)S(1)}, f32[8,2048]{1,0:T(8,128)S(1)}, u32[]{:S(2)}, u32[]{:S(2)}) %collective-permute-start.5) | collective-permute-done | bytes 65568 | tf_op jit(solution)/shard_map/ppermute | solution.py:539
  64.1 0.7 %finish_drafts.1 = (bf16[1,5,1024]{2,1,0:T(8,128)(2,1)}, f32[8,128]{1,0:T(8,128)}) custom-call(s32[1]{0:T(128)} %bitcast.side, f32[8,2048]{1,0:T(8,128)S(1)} %join.1.own, f32[8,2048]{1,0:T(8,128)S(1)} %collective-permute-done.5.other, bf16[1,5,2048]{2,1,0:T(8,128)(2,1)S(1)} %copy-done.3, f32[1,2048]{1,0:T(1,128)S(1)} %bitcast.12), custom_call_target="tpu_custom_call" | custom-call | flops 131072 | bytes 98304 | tf_op jit(solution)/shard_map/finish_drafts/pallas_call | solution.py:454
  (27 shorter events, 0.1 us)
Async XLA Ops:
  3.5 9.1 %copy-start.2 = (bf16[1,5,2048]{2,1,0:T(8,128)(2,1)S(1)}, bf16[1,5,2048]{2,1,0:T(8,128)(2,1)}, u32[]{:S(2)}) copy-start(bf16[1,5,2048]{2,1,0:T(8,128)(2,1)} %x.3) | copy-start | bytes 61444
  3.5 9.1 %copy-start.8 = (f32[8,128]{1,0:T(8,128)S(1)}, f32[8,128]{1,0:T(8,128)}, u32[]{:S(2)}) copy-start(f32[8,128]{1,0:T(8,128)} %get-tuple-element.27.after) | copy-start | bytes 12292
  3.5 9.1 %copy-start.9 = (s32[1,64]{1,0:T(1,128)S(1)}, s32[1,64]{1,0:T(1,128)}, u32[]{:S(2)}) copy-start(s32[1,64]{1,0:T(1,128)} %table.3) | copy-start | bytes 772
  3.5 41.2 %all-to-all-start = ((bf16[128,16,512]{2,1,0:T(8,128)(2,1)}), bf16[128,16,512]{2,1,0:T(8,128)(2,1)S(1)}, u32[]{:S(2)}, u32[]{:S(2)}) async-start(bf16[128,16,512]{2,1,0:T(8,128)(2,1)} %get-tuple-element.38), calls=%async_computation | async-start | bytes 4194304 | tf_op jit(solution)/shard_map/all_to_all | solution.py:501
  12.5 7.6 %copy-start.11 = (s32[8]{0:T(128)}, s32[8]{0:T(128)S(1)}, u32[]{:S(2)}) copy-start(s32[8]{0:T(128)S(1)} %compare_select_fusion.meta) | copy-start | bytes 100
  13.1 13.3 %collective-permute-start = (bf16[1,8,2048]{2,1,0:T(8,128)(2,1)S(1)}, bf16[1,8,2048]{2,1,0:T(8,128)(2,1)S(1)}, u32[]{:S(2)}, u32[]{:S(2)}) collective-permute-start(bf16[1,8,2048]{2,1,0:T(8,128)(2,1)S(1)} %pack.1), channel_id=1, source_target_pairs={{0,8},{2,10},{4,12},{6,14},{8,0},{10,2},{12,4},{14,6},{16,24},{18,... | collective-permute-start | bytes 98312 | tf_op jit(solution)/shard_map/ppermute | solution.py:512
  26.5 9.6 %collective-permute-start.3 = (bf16[2,8,2048]{2,1,0:T(8,128)(2,1)S(1)}, bf16[2,8,2048]{2,1,0:T(8,128)(2,1)S(1)}, u32[]{:S(2)}, u32[]{:S(2)}) collective-permute-start(bf16[2,8,2048]{2,1,0:T(8,128)(2,1)S(1)} %pad_maximum_fusion.1), channel_id=1, source_target_pairs={{0,6},{2,4},{4,2},{6,0},{8,14},{10,12},{12,10},{14,8},{16,22},{18,... | collective-permute-start | bytes 196616 | tf_op jit(solution)/shard_map/ppermute | solution.py:512
  28.2 7.9 %collective-permute-start.2 = (bf16[2,8,2048]{2,1,0:T(8,128)(2,1)S(1)}, bf16[2,8,2048]{2,1,0:T(8,128)(2,1)S(1)}, u32[]{:S(2)}, u32[]{:S(2)}) collective-permute-start(bf16[2,8,2048]{2,1,0:T(8,128)(2,1)S(1)} %pad_maximum_fusion.1), channel_id=1, source_target_pairs={{0,2},{2,0},{4,6},{6,4},{8,10},{10,8},{12,14},{14,12},{16,18},{18,... | collective-permute-start | bytes 196616 | tf_op jit(solution)/shard_map/ppermute | solution.py:512
  28.2 7.9 %collective-permute-start.1 = (bf16[2,8,2048]{2,1,0:T(8,128)(2,1)S(1)}, bf16[2,8,2048]{2,1,0:T(8,128)(2,1)S(1)}, u32[]{:S(2)}, u32[]{:S(2)}) collective-permute-start(bf16[2,8,2048]{2,1,0:T(8,128)(2,1)S(1)} %pad_maximum_fusion.1), channel_id=1, source_target_pairs={{0,4},{2,6},{4,0},{6,2},{8,12},{10,14},{12,8},{14,10},{16,20},{18,... | collective-permute-start | bytes 196616 | tf_op jit(solution)/shard_map/ppermute | solution.py:512
  30.1 8.2 %copy-start.6 = (f32[2048]{0:T(1024)S(1)}, f32[2048]{0:T(1024)}, u32[]{:S(2)}) copy-start(f32[2048]{0:T(1024)} %param.17) | copy-start | bytes 24580
  36.2 6.9 %collective-permute-start.4 = (bf16[256,2048]{1,0:T(8,128)(2,1)}, bf16[256,2048]{1,0:T(8,128)(2,1)S(1)}, u32[]{:S(2)}, u32[]{:S(2)}) collective-permute-start(bf16[256,2048]{1,0:T(8,128)(2,1)} %get-tuple-element.39.own), channel_id=1, source_target_pairs={{0,1},{1,0},{2,3},{3,2},{4,5},{5,4},{6,7},{7,6},{8,9},{9,8},{10,11... | collective-permute-start | bytes 3145736 | tf_op jit(solution)/shard_map/ppermute | solution.py:530
  38.3 0.7 %copy-start.7 = (f32[2,256]{1,0:T(2,128)S(1)}, f32[2,256]{1,0:T(2,128)}, u32[]{:S(2)}) copy-start(f32[2,256]{1,0:T(2,128)} %qk_gain.3) | copy-start | bytes 6148
  39.0 0.7 %copy-start.10 = (f32[1,128]{1,0:T(1,128)S(1)}, f32[1,128]{1,0:T(1,128)}, u32[]{:S(2)}) copy-start(f32[1,128]{1,0:T(1,128)} %constant.14.clone.freq) | copy-start | bytes 1540
  39.7 3.4 %copy-start = (bf16[256,2048]{1,0:T(8,128)(2,1)S(1)}, bf16[256,2048]{1,0:T(8,128)(2,1)}, u32[]{:S(2)}) copy-start(bf16[256,2048]{1,0:T(8,128)(2,1)} %x.2) | copy-start | bytes 3145732
  39.7 3.4 %copy-start.1 = (bf16[256,2048]{1,0:T(8,128)(2,1)S(1)}, bf16[256,2048]{1,0:T(8,128)(2,1)}, u32[]{:S(2)}) copy-start(bf16[256,2048]{1,0:T(8,128)(2,1)} %get-tuple-element.39.own) | copy-start | bytes 3145732
  39.7 3.4 %copy-start.5 = (f32[2048]{0:T(1024)S(1)}, f32[2048]{0:T(1024)}, u32[]{:S(2)}) copy-start(f32[2048]{0:T(1024)} %param.22) | copy-start | bytes 24580
  44.6 11.4 %copy-start.4 = (f32[32,512]{1,0:T(8,128)S(1)}, f32[32,512]{1,0:T(8,128)}, u32[]{:S(2)}) copy-start(f32[32,512]{1,0:T(8,128)} %get-tuple-element.41.local) | copy-start | bytes 196612
  56.1 8.0 %copy-start.3 = (bf16[1,5,2048]{2,1,0:T(8,128)(2,1)S(1)}, bf16[1,5,2048]{2,1,0:T(8,128)(2,1)}, u32[]{:S(2)}) copy-start(bf16[1,5,2048]{2,1,0:T(8,128)(2,1)} %x.3) | copy-start | bytes 61444
  58.6 5.5 %collective-permute-start.5 = (f32[8,2048]{1,0:T(8,128)S(1)}, f32[8,2048]{1,0:T(8,128)S(1)}, u32[]{:S(2)}, u32[]{:S(2)}) collective-permute-start(f32[8,2048]{1,0:T(8,128)S(1)} %join.1.own), channel_id=1, source_target_pairs={{0,1},{1,0},{2,3},{3,2},{4,5},{5,4},{6,7},{7,6},{8,9},{9,8},{10,11... | collective-permute-start | bytes 196616 | tf_op jit(solution)/shard_map/ppermute | solution.py:539

commit v9 on v8

--- a/solution.py
+++ b/solution.py
@@ -70,10 +70,12 @@
 
 def project_kernel(
     meta, lengths, x, draft, gain, wq, wkv, qk_gain, freq, table,
-    queries, prompt_kv, near_kv, sent, draft_kv, own_count, verify_kv,
-    weights, normed, wide, rows_q, sems,
+    queries, prompt_kv, near_kv, sent, draft_kv, own_count, verify_kv, small,
+    weights, normed, wide, rows_q, held, sems,
 ):
     rows, drafted = x.shape[0], draft.shape[1]
+    fetch = pltpu.make_async_copy(x, held, sems.at[3])
+    fetch.start()
     copies = []
     for h in range(3):
         part = wq.at[:, h * 2 * HEAD : (h + 1) * 2 * HEAD] if h < 2 else wkv
@@ -81,10 +83,12 @@
         copy.start()
         copies.append(copy)
 
-    normed[:rows] = (unit(x[...].astype(f32)) * gain[...]).astype(bf16)
     wide[...] = jnp.zeros_like(wide)
     wide[:drafted] = unit(draft[0].astype(f32)) * gain[...]
     normed[rows:] = wide[...].astype(bf16)
+    small[...] = jnp.zeros_like(small)
+    small[0:1, :] = qk_gain[0:1, :]
+    small[1:2, : HEAD // 2] = freq[...]
 
     own_count[...] = tally(table[...], meta[0], own_count.shape[1], 0, 1)
 
@@ -102,6 +106,9 @@
     def rotated(values):
         a, b = values[:, :half], values[:, half:]
         return jnp.concatenate([a * cos - b * sin, b * cos + a * sin], axis=-1)
+
+    fetch.wait()
+    normed[:rows] = (unit(held[...].astype(f32)) * gain[...]).astype(bf16)
 
     keep = iota((PAD, HEAD), 0) < meta[1]
 
@@ -140,10 +147,11 @@
         jax.ShapeDtypeStruct((PAD, 2 * HEAD), f32),
         jax.ShapeDtypeStruct((1, own), f32),
         jax.ShapeDtypeStruct((1, drafted, 2 * HEAD), bf16),
+        jax.ShapeDtypeStruct((8, HEAD), f32),
     ]
     return pl.pallas_call(
         project_kernel,
-        in_specs=[SMEM, SMEM, VMEM, VMEM, VMEM, HBM, HBM, VMEM, VMEM, VMEM],
+        in_specs=[SMEM, SMEM, HBM, VMEM, VMEM, HBM, HBM, VMEM, VMEM, VMEM],
         out_specs=[VMEM] * len(shapes),
         out_shape=shapes,
         scratch_shapes=[
@@ -151,7 +159,8 @@
             pltpu.VMEM((total, width), bf16),
             pltpu.VMEM((16, width), f32),
             pltpu.VMEM((QH * PAD, HEAD), f32),
-            pltpu.SemaphoreType.DMA((3,)),
+            pltpu.VMEM((rows, width), bf16),
+            pltpu.SemaphoreType.DMA((4,)),
         ],
         compiler_params=pltpu.CompilerParams(vmem_limit_bytes=55 << 20),
         cost_estimate=pl.CostEstimate(
@@ -161,10 +170,10 @@
     )(meta, lengths, x, draft, gain, wq, wkv, qk_gain, freq, table)
 
 
-def pack_kernel(meta, draft, table, after, out, wide):
+def pack_kernel(meta, draft, gain, table, after, out, wide):
     drafted, slots = draft.shape[1], table.shape[1]
     wide[...] = jnp.zeros_like(wide)
-    wide[:drafted] = draft[0].astype(f32)
+    wide[:drafted] = unit(draft[0].astype(f32)) * gain[...]
     lane = iota((1, 128), 1)
     size = jnp.where(lane == slots, meta[0] >> 3, jnp.where(lane == slots + 1, meta[0] & 7, 0))
     wide[5:6, :128] = size.astype(f32)
@@ -172,21 +181,21 @@
     out[0] = wide[...].astype(bf16)
 
 
-def pack(meta, draft, table, after):
+def pack(meta, draft, gain, table, after):
     width = draft.shape[2]
     return pl.pallas_call(
         pack_kernel,
-        in_specs=[SMEM, VMEM, VMEM, VMEM],
+        in_specs=[SMEM, VMEM, VMEM, VMEM, VMEM],
         out_specs=VMEM,
         out_shape=jax.ShapeDtypeStruct((1, PAD, width), bf16),
         scratch_shapes=[pltpu.VMEM((PAD, width), f32)],
         compiler_params=pltpu.CompilerParams(vmem_limit_bytes=4 << 20),
         cost_estimate=pl.CostEstimate(flops=0, transcendentals=0, bytes_accessed=1 << 17),
         name="pack",
-    )(meta, draft, table, after)
-
-
-def ask_kernel(where, x, gain, wq, qk_gain, freq, out, weights, sems):
+    )(meta, draft, gain, table, after)
+
+
+def ask_kernel(where, x, wq, small, out, weights, sems):
     groups = x.shape[0]
     copies = []
     for i in range(2):
@@ -194,8 +203,7 @@
         copy = pltpu.make_async_copy(wq.at[:, cols], weights.at[i], sems.at[i])
         copy.start()
         copies.append(copy)
-    rows = x[...].astype(f32).reshape(groups * PAD, -1)
-    normed = (unit(rows) * gain[...]).astype(bf16)
+    normed = x[...].astype(f32).reshape(groups * PAD, -1).astype(bf16)
     half = HEAD // 2
     counts, starts = [], []
     for e in range(groups):
@@ -206,7 +214,7 @@
         counts.append(tally(note[:, :64], size, HEAD, 64 + where[0], DEEP))
     count = jnp.concatenate(counts, axis=0).reshape(groups, 1, HEAD)
     position = jnp.concatenate(starts, axis=0) + (iota((groups * PAD, half), 0) & (PAD - 1))
-    angles = position.astype(f32) * freq[...]
+    angles = position.astype(f32) * small[1:2, : HEAD // 2]
     cos, sin = jnp.cos(angles), jnp.sin(angles)
     mark = iota((groups, PAD, HEAD), 1) == 5
     heads = []
@@ -214,7 +222,7 @@
         copies[i].wait()
         both = dot_n(normed, weights[i])
         for j in range(2):
-            value = unit(both[:, j * HEAD : (j + 1) * HEAD]) * qk_gain[0:1, :]
+            value = unit(both[:, j * HEAD : (j + 1) * HEAD]) * small[0:1, :]
             a, b = value[:, :half], value[:, half:]
             value = jnp.concatenate([a * cos - b * sin, b * cos + a * sin], axis=-1)
             value = value.reshape(groups, PAD, HEAD)
@@ -222,11 +230,11 @@
     out[...] = jnp.concatenate(heads, axis=1).astype(bf16)
 
 
-def ask(where, x, gain, wq, qk_gain, freq):
+def ask(where, x, wq, small):
     groups, _, width = x.shape
     return pl.pallas_call(
         ask_kernel,
-        in_specs=[SMEM, VMEM, VMEM, HBM, VMEM, VMEM],
+        in_specs=[SMEM, VMEM, HBM, VMEM],
         out_specs=VMEM,
         out_shape=jax.ShapeDtypeStruct((groups, QH * PAD, HEAD), bf16),
         scratch_shapes=[
@@ -238,7 +246,7 @@
             flops=2 * groups * PAD * width * QH * HEAD, transcendentals=0, bytes_accessed=5 << 20
         ),
         name="ask",
-    )(where, x, gain, wq, qk_gain, freq)
+    )(where, x, wq, small)
 
 
 def prompt_kernel(
@@ -512,11 +520,11 @@
             parts.append(lax.ppermute(values, "req", pairs))
         return jnp.concatenate(parts, axis=0)
 
-    asked = beside(pack(meta, verify_x, page_table, picked), 4)
+    asked = beside(pack(meta, verify_x, attn_gain[None], page_table, picked), 4)
 
     power = -(np.arange(HEAD // 2, dtype=np.float64) * 2.0) / HEAD
     freq = jnp.asarray((rope_base**power)[None], f32)
-    queries, prefill_kv, near_kv, sent, draft_kv, own_count, verify_kv = project(
+    queries, prefill_kv, near_kv, sent, draft_kv, own_count, verify_kv, small = project(
         meta, prompt_len, prefill_x, verify_x, attn_gain[None], w_query, w_keyval,
         qk_gain, freq, page_table, pool_pages * PAGE,
     )
@@ -530,7 +538,7 @@
     other = lax.ppermute(partial, "head", swap)
     prefill_out, done = finish(side, partial, other, prefill_x, post_gain[None], "finish_prompts")
 
-    queries = ask(where, asked, attn_gain[None], w_query, qk_gain, freq)
+    queries = ask(where, asked, w_query, small)
     pieces = remote_pieces(
         where, queries, arrived.reshape(planes, DEEP, PAGE, -1), done
     )

time: 65.2 us -> 65.2 us (level)
  blocking collectives: 10.7 us -> 12.2 us
  local copies, waits for them, and re-layouts: 1.37 us -> 0.04 us
    all_to_all x1, blocking collectives: 10.7 us -> 12.2 us  [on_device(): lax.all_to_all(pieces, 'req', 0, 0, tiled=True, axis_index_groups=column)]
    unnamed x24 -> x22, local copies, waits for them, and re-layouts: 1.37 us -> 0.04 us
where the time goes in v9:
time: 65.2 us; the launch traced here: 64.8 us
  starting transfers between devices  25.5 us (39%)
  Pallas kernels  24 us (37%)
  blocking collectives  12.2 us (19%)
  between operations  2.12 us (3%)
  waiting for transfers between devices  0.92 us (1%)
    all_to_all x1, blocking collectives, on_device(): lax.all_to_all(pieces, 'req', 0, 0, tiled=True, axis_index_groups=column)  12.2 us
    ppermute x4, starting transfers between devices, beside(): parts.append(lax.ppermute(values, 'req', pairs))  10.6 us
    all_to_all x1, starting transfers between devices, on_device(): lax.all_to_all(outgoing, 'req', 0, 0, tiled=True, axis_index_groups=plane)  7.73 us
    ppermute x2, starting transfers between devices, on_device(): other = lax.ppermute(partial, 'head', swap)  7.13 us
    pallas_call x1, Pallas kernels, project(): pl.pallas_call(project_kernel, in_specs=[SMEM, SMEM, HBM, VMEM, VMEM, HBM...  6.17 us
    pallas_call x1, Pallas kernels, prompts(): pl.pallas_call(prompt_kernel, in_specs=[SMEM] + [VMEM] * 6 + [HBM], out_s...  5.97 us
    pallas_call x1, Pallas kernels, ask(): pl.pallas_call(ask_kernel, in_specs=[SMEM, VMEM, HBM, VMEM], out_specs=VM...  2.99 us
    pallas_call x1, Pallas kernels, pick_pages(): pl.pallas_call(pick_kernel, in_specs=[SMEM, VMEM], out_specs=[VMEM, VMEM]...  2.82 us
  transfers between devices with their start and end apart: 7, of which 1 were waited for; matrix products, arithmetic and copies ran while one was open for 0% of the time, Pallas kernels for 27%

profile of v9, /device:TPU:1, one launch (start us, length us, event | category | flops | bytes accessed | tf_op | source)
XLA Modules:
  0.0 64.8 jit_solution(214974364300740767)
XLA Ops:
  0.6 2.8 %pick_pages.1 = (bf16[128,16,512]{2,1,0:T(8,128)(2,1)}, f32[8,128]{1,0:T(8,128)}) custom-call(s32[1,128]{1,0:T(1,128)} %index.1, bf16[64,16,512]{2,1,0:T(8,128)(2,1)} %pool.1), custom_call_target="tpu_custom_call" | custom-call | bytes 4194304 | tf_op jit(solution)/shard_map/pick_pages/pallas_call | solution.py:61
  3.5 0.0 copy-start.9
  3.5 7.7 %all-to-all-start = ((bf16[128,16,512]{2,1,0:T(8,128)(2,1)}), bf16[128,16,512]{2,1,0:T(8,128)(2,1)S(1)}, u32[]{:S(2)}, u32[]{:S(2)}) async-start(bf16[128,16,512]{2,1,0:T(8,128)(2,1)} %get-tuple-element.40), calls=%async_computation | async-start | bytes 4194304 | tf_op jit(solution)/shard_map/all_to_all | solution.py:509
  12.6 0.7 %pack.1 = bf16[1,8,2048]{2,1,0:T(8,128)(2,1)S(1)} custom-call(s32[8]{0:T(128)S(1)} %compare_select_fusion.meta, bf16[1,5,2048]{2,1,0:T(8,128)(2,1)S(1)} %copy-done.2, f32[1,2048]{1,0:T(1,128)S(1)} %bitcast.14, s32[1,64]{1,0:T(1,128)S(1)} %copy-done.9, f32[8,128]{1,0:T(8,128)S(1)} %copy-done.8), custom_call_target="tpu_custom_call" | custom-call | bytes 131072 | tf_op jit(solution)/shard_map/pack/pallas_call | solution.py:186
  13.2 7.0 %collective-permute-start = (bf16[1,8,2048]{2,1,0:T(8,128)(2,1)S(1)}, bf16[1,8,2048]{2,1,0:T(8,128)(2,1)S(1)}, u32[]{:S(2)}, u32[]{:S(2)}) collective-permute-start(bf16[1,8,2048]{2,1,0:T(8,128)(2,1)S(1)} %pack.1), channel_id=1, source_target_pairs={{0,8},{2,10},{4,12},{6,14},{8,0},{10,2},{12,4},{14,6},{16,24},{18,... | collective-permute-start | bytes 98312 | tf_op jit(solution)/shard_map/ppermute | solution.py:520
  20.2 6.2 %project.1 = (bf16[4,256,256]{2,1,0:T(8,128)(2,1)}, bf16[256,512]{1,0:T(8,128)(2,1)}, bf16[256,512]{1,0:T(8,128)(2,1)}, bf16[32,256]{1,0:T(8,128)(2,1)}, f32[8,5...) custom-call(s32[8]{0:T(128)} %copy-done.10, s32[1,4]{1,0:T(1,128)} %lengths.3, ...), custom_call_target="tpu_custom_call" | custom-call | flops 1711276032 | bytes 9437184 | tf_op jit(solution)/shard_map/project/pallas_call | solution.py:152
  26.4 0.0 collective-permute-done
  26.4 1.7 %collective-permute-start.3 = (bf16[2,8,2048]{2,1,0:T(8,128)(2,1)S(1)}, bf16[2,8,2048]{2,1,0:T(8,128)(2,1)S(1)}, u32[]{:S(2)}, u32[]{:S(2)}) collective-permute-start(bf16[2,8,2048]{2,1,0:T(8,128)(2,1)S(1)} %pad_maximum_fusion.1), channel_id=1, source_target_pairs={{0,6},{2,4},{4,2},{6,0},{8,14},{10,12},{12,10},{14,8},{16,22},{18,... | collective-permute-start | bytes 196616 | tf_op jit(solution)/shard_map/ppermute | solution.py:520
  28.2 0.0 collective-permute-start.2
  28.2 1.9 %collective-permute-start.1 = (bf16[2,8,2048]{2,1,0:T(8,128)(2,1)S(1)}, bf16[2,8,2048]{2,1,0:T(8,128)(2,1)S(1)}, u32[]{:S(2)}, u32[]{:S(2)}) collective-permute-start(bf16[2,8,2048]{2,1,0:T(8,128)(2,1)S(1)} %pad_maximum_fusion.1), channel_id=1, source_target_pairs={{0,4},{2,6},{4,0},{6,2},{8,12},{10,14},{12,8},{14,10},{16,20},{18,... | collective-permute-start | bytes 196616 | tf_op jit(solution)/shard_map/ppermute | solution.py:520
  30.1 6.0 %prompts.1 = (bf16[256,2048]{1,0:T(8,128)(2,1)}, f32[32,512]{1,0:T(8,128)}) custom-call(s32[1,4]{1,0:T(1,128)} %lengths.3, bf16[4,256,256]{2,1,0:T(8,128)(2,1)} %get-tuple-element.32.q, bf16[256,512]{1,0:T(8,128)(2,1)} %get-tuple-element.33.kv, bf16[32,256]{1,0:T(8,128)(2,1)} %get-tuple-element.34.query, f32[8,512]{1,0:T(8,128)} %get-tuple-element.35.draft_kv, ...), custom_call_target="tpu_custom_call" | custom-call | flops 268435456 | bytes 4194304 | tf_op jit(solution)/shard_map/prompts/pallas_call | solution.py:305
  36.0 0.0 collective-permute-done.2
  36.1 0.0 collective-permute-done.1
  36.1 2.2 %collective-permute-start.4 = (bf16[256,2048]{1,0:T(8,128)(2,1)}, bf16[256,2048]{1,0:T(8,128)(2,1)S(1)}, u32[]{:S(2)}, u32[]{:S(2)}) collective-permute-start(bf16[256,2048]{1,0:T(8,128)(2,1)} %get-tuple-element.41.own), channel_id=1, source_target_pairs={{0,1},{1,0},{2,3},{3,2},{4,5},{5,4},{6,7},{7,6},{8,9},{9,8},{10,11... | collective-permute-start | bytes 3145736 | tf_op jit(solution)/shard_map/ppermute | solution.py:538
  38.3 3.0 %ask.1.queries = bf16[8,32,256]{2,1,0:T(8,128)(2,1)S(1)} custom-call(s32[1]{0:T(128)} %bitcast.1.where, bf16[8,8,2048]{2,1,0:T(8,128)(2,1)S(1)} %pad_maximum_fusion.x, bf16[2048,1024]{1,0:T(8,128)(2,1)} %wq.3, f32[8,256]{1,0:T(8,128)S(1)} %copy-done.7), custom_call_target="tpu_custom_call" | custom-call | flops 268435456 | bytes 5242880 | tf_op jit(solution)/shard_map/ask/pallas_call | solution.py:235
  41.3 0.0 collective-permute-done.4.other
  41.3 1.5 %finish_prompts.1 = (bf16[256,1024]{1,0:T(8,128)(2,1)}, f32[8,128]{1,0:T(8,128)S(1)}) custom-call(s32[1]{0:T(128)} %bitcast.side, bf16[256,2048]{1,0:T(8,128)(2,1)S(1)} %copy-done.1, bf16[256,2048]{1,0:T(8,128)(2,1)S(1)} %collective-permute-done.4.other, bf16[256,2048]{1,0:T(8,128)(2,1)S(1)} %copy-done, f32[1,2048]{1,0:T(1,128)S(1)} %bitcast.11), custom_call_target="tpu_custom_call" | custom-call | flops 4194304 | bytes 3145728 | tf_op jit(solution)/shard_map/finish_prompts/pallas_call | solution.py:462
  42.8 0.0 all-to-all-done
  42.8 0.7 %remote_pieces.1 = bf16[8,32,256]{2,1,0:T(8,128)(2,1)S(1)} custom-call(s32[1]{0:T(128)} %bitcast.1.where, bf16[8,32,256]{2,1,0:T(8,128)(2,1)S(1)} %ask.1.queries, bf16[16,8,16,512]{3,2,1,0:T(8,128)(2,1)S(1)} %bitcast.10, f32[8,128]{1,0:T(8,128)S(1)} %get-tuple-element.42.after), custom_call_target="tpu_custom_call" | custom-call | flops 67108864 | bytes 3145728 | tf_op jit(solution)/shard_map/remote_pieces/pallas_call | solution.py:370
  43.5 12.2 %all_to_all.10.pieces = bf16[8,32,256]{2,1,0:T(8,128)(2,1)S(1)} all-to-all(bf16[8,32,256]{2,1,0:T(8,128)(2,1)S(1)} %remote_pieces.1), channel_id=1, replica_groups={{0,2,4,6,8,10,12,14},{16,18,20,22,24,26,28,30},{32,34,36,38,40,42,44,46..., dimensions={0} | all-to-all | bytes 262144 | tf_op jit(solution)/shard_map/all_to_all | solution.py:545
  55.7 2.5 %join.1.own = f32[8,2048]{1,0:T(8,128)S(1)} custom-call(bf16[8,32,256]{2,1,0:T(8,128)(2,1)S(1)} %all_to_all.10.pieces, f32[32,512]{1,0:T(8,128)S(1)} %copy-done.4, bf16[1024,2048]{1,0:T(8,128)(2,1)} %w_out.3), custom_call_target="tpu_custom_call" | custom-call | flops 33554432 | bytes 4194304 | tf_op jit(solution)/shard_map/join/pallas_call | solution.py:422
  58.2 5.0 %collective-permute-start.5 = (f32[8,2048]{1,0:T(8,128)S(1)}, f32[8,2048]{1,0:T(8,128)S(1)}, u32[]{:S(2)}, u32[]{:S(2)}) collective-permute-start(f32[8,2048]{1,0:T(8,128)S(1)} %join.1.own), channel_id=1, source_target_pairs={{0,1},{1,0},{2,3},{3,2},{4,5},{5,4},{6,7},{7,6},{8,9},{9,8},{10,11... | collective-permute-start | bytes 196616 | tf_op jit(solution)/shard_map/ppermute | solution.py:547
  63.2 0.9 %collective-permute-done.5.other = f32[8,2048]{1,0:T(8,128)S(1)} collective-permute-done((f32[8,2048]{1,0:T(8,128)S(1)}, f32[8,2048]{1,0:T(8,128)S(1)}, u32[]{:S(2)}, u32[]{:S(2)}) %collective-permute-start.5) | collective-permute-done | bytes 65568 | tf_op jit(solution)/shard_map/ppermute | solution.py:547
  64.1 0.7 %finish_drafts.1 = (bf16[1,5,1024]{2,1,0:T(8,128)(2,1)}, f32[8,128]{1,0:T(8,128)}) custom-call(s32[1]{0:T(128)} %bitcast.side, f32[8,2048]{1,0:T(8,128)S(1)} %join.1.own, f32[8,2048]{1,0:T(8,128)S(1)} %collective-permute-done.5.other, bf16[1,5,2048]{2,1,0:T(8,128)(2,1)S(1)} %copy-done.3, f32[1,2048]{1,0:T(1,128)S(1)} %bitcast.12), custom_call_target="tpu_custom_call" | custom-call | flops 131072 | bytes 98304 | tf_op jit(solution)/shard_map/finish_drafts/pallas_call | solution.py:462
  (25 shorter events, 0.1 us)
Async XLA Ops:
  3.5 9.1 %copy-start.2 = (bf16[1,5,2048]{2,1,0:T(8,128)(2,1)S(1)}, bf16[1,5,2048]{2,1,0:T(8,128)(2,1)}, u32[]{:S(2)}) copy-start(bf16[1,5,2048]{2,1,0:T(8,128)(2,1)} %x.3) | copy-start | bytes 61444
  3.5 9.1 %copy-start.6 = (f32[2048]{0:T(1024)S(1)}, f32[2048]{0:T(1024)}, u32[]{:S(2)}) copy-start(f32[2048]{0:T(1024)} %param.17) | copy-start | bytes 24580
  3.5 9.1 %copy-start.8 = (f32[8,128]{1,0:T(8,128)S(1)}, f32[8,128]{1,0:T(8,128)}, u32[]{:S(2)}) copy-start(f32[8,128]{1,0:T(8,128)} %get-tuple-element.28.after) | copy-start | bytes 12292
  3.5 9.1 %copy-start.9 = (s32[1,64]{1,0:T(1,128)S(1)}, s32[1,64]{1,0:T(1,128)}, u32[]{:S(2)}) copy-start(s32[1,64]{1,0:T(1,128)} %table.3) | copy-start | bytes 772
  3.5 39.4 %all-to-all-start = ((bf16[128,16,512]{2,1,0:T(8,128)(2,1)}), bf16[128,16,512]{2,1,0:T(8,128)(2,1)S(1)}, u32[]{:S(2)}, u32[]{:S(2)}) async-start(bf16[128,16,512]{2,1,0:T(8,128)(2,1)} %get-tuple-element.40), calls=%async_computation | async-start | bytes 4194304 | tf_op jit(solution)/shard_map/all_to_all | solution.py:509
  12.5 7.7 %copy-start.10 = (s32[8]{0:T(128)}, s32[8]{0:T(128)S(1)}, u32[]{:S(2)}) copy-start(s32[8]{0:T(128)S(1)} %compare_select_fusion.meta) | copy-start | bytes 100
  13.2 13.2 %collective-permute-start = (bf16[1,8,2048]{2,1,0:T(8,128)(2,1)S(1)}, bf16[1,8,2048]{2,1,0:T(8,128)(2,1)S(1)}, u32[]{:S(2)}, u32[]{:S(2)}) collective-permute-start(bf16[1,8,2048]{2,1,0:T(8,128)(2,1)S(1)} %pack.1), channel_id=1, source_target_pairs={{0,8},{2,10},{4,12},{6,14},{8,0},{10,2},{12,4},{14,6},{16,24},{18,... | collective-permute-start | bytes 98312 | tf_op jit(solution)/shard_map/ppermute | solution.py:520
  26.4 9.6 %collective-permute-start.3 = (bf16[2,8,2048]{2,1,0:T(8,128)(2,1)S(1)}, bf16[2,8,2048]{2,1,0:T(8,128)(2,1)S(1)}, u32[]{:S(2)}, u32[]{:S(2)}) collective-permute-start(bf16[2,8,2048]{2,1,0:T(8,128)(2,1)S(1)} %pad_maximum_fusion.1), channel_id=1, source_target_pairs={{0,6},{2,4},{4,2},{6,0},{8,14},{10,12},{12,10},{14,8},{16,22},{18,... | collective-permute-start | bytes 196616 | tf_op jit(solution)/shard_map/ppermute | solution.py:520
  28.2 7.9 %collective-permute-start.2 = (bf16[2,8,2048]{2,1,0:T(8,128)(2,1)S(1)}, bf16[2,8,2048]{2,1,0:T(8,128)(2,1)S(1)}, u32[]{:S(2)}, u32[]{:S(2)}) collective-permute-start(bf16[2,8,2048]{2,1,0:T(8,128)(2,1)S(1)} %pad_maximum_fusion.1), channel_id=1, source_target_pairs={{0,2},{2,0},{4,6},{6,4},{8,10},{10,8},{12,14},{14,12},{16,18},{18,... | collective-permute-start | bytes 196616 | tf_op jit(solution)/shard_map/ppermute | solution.py:520
  28.2 7.9 %collective-permute-start.1 = (bf16[2,8,2048]{2,1,0:T(8,128)(2,1)S(1)}, bf16[2,8,2048]{2,1,0:T(8,128)(2,1)S(1)}, u32[]{:S(2)}, u32[]{:S(2)}) collective-permute-start(bf16[2,8,2048]{2,1,0:T(8,128)(2,1)S(1)} %pad_maximum_fusion.1), channel_id=1, source_target_pairs={{0,4},{2,6},{4,0},{6,2},{8,12},{10,14},{12,8},{14,10},{16,20},{18,... | collective-permute-start | bytes 196616 | tf_op jit(solution)/shard_map/ppermute | solution.py:520
  30.1 8.2 %copy-start.7 = (f32[8,256]{1,0:T(8,128)S(1)}, f32[8,256]{1,0:T(8,128)}, u32[]{:S(2)}) copy-start(f32[8,256]{1,0:T(8,128)} %get-tuple-element.39.small) | copy-start | bytes 24580
  36.1 5.2 %collective-permute-start.4 = (bf16[256,2048]{1,0:T(8,128)(2,1)}, bf16[256,2048]{1,0:T(8,128)(2,1)S(1)}, u32[]{:S(2)}, u32[]{:S(2)}) collective-permute-start(bf16[256,2048]{1,0:T(8,128)(2,1)} %get-tuple-element.41.own), channel_id=1, source_target_pairs={{0,1},{1,0},{2,3},{3,2},{4,5},{5,4},{6,7},{7,6},{8,9},{9,8},{10,11... | collective-permute-start | bytes 3145736 | tf_op jit(solution)/shard_map/ppermute | solution.py:538
  38.3 3.0 %copy-start = (bf16[256,2048]{1,0:T(8,128)(2,1)S(1)}, bf16[256,2048]{1,0:T(8,128)(2,1)}, u32[]{:S(2)}) copy-start(bf16[256,2048]{1,0:T(8,128)(2,1)} %x.2) | copy-start | bytes 3145732
  38.3 3.0 %copy-start.1 = (bf16[256,2048]{1,0:T(8,128)(2,1)S(1)}, bf16[256,2048]{1,0:T(8,128)(2,1)}, u32[]{:S(2)}) copy-start(bf16[256,2048]{1,0:T(8,128)(2,1)} %get-tuple-element.41.own) | copy-start | bytes 3145732
  38.3 3.0 %copy-start.5 = (f32[2048]{0:T(1024)S(1)}, f32[2048]{0:T(1024)}, u32[]{:S(2)}) copy-start(f32[2048]{0:T(1024)} %param.22) | copy-start | bytes 24580
  42.8 12.9 %copy-start.4 = (f32[32,512]{1,0:T(8,128)S(1)}, f32[32,512]{1,0:T(8,128)}, u32[]{:S(2)}) copy-start(f32[32,512]{1,0:T(8,128)} %get-tuple-element.43.local) | copy-start | bytes 196612
  55.7 8.4 %copy-start.3 = (bf16[1,5,2048]{2,1,0:T(8,128)(2,1)S(1)}, bf16[1,5,2048]{2,1,0:T(8,128)(2,1)}, u32[]{:S(2)}) copy-start(bf16[1,5,2048]{2,1,0:T(8,128)(2,1)} %x.3) | copy-start | bytes 61444
  58.2 5.9 %collective-permute-start.5 = (f32[8,2048]{1,0:T(8,128)S(1)}, f32[8,2048]{1,0:T(8,128)S(1)}, u32[]{:S(2)}, u32[]{:S(2)}) collective-permute-start(f32[8,2048]{1,0:T(8,128)S(1)} %join.1.own), channel_id=1, source_target_pairs={{0,1},{1,0},{2,3},{3,2},{4,5},{5,4},{6,7},{7,6},{8,9},{9,8},{10,11... | collective-permute-start | bytes 196616 | tf_op jit(solution)/shard_map/ppermute | solution.py:547

commit v10 on v9

--- a/solution.py
+++ b/solution.py
@@ -323,7 +323,7 @@
     )(lengths, q, kv, query, draft_kv, pool, count, w_out)
 
 
-def remote_kernel(where, queries, pages, after, out):
+def remote_kernel(where, queries, pages, out):
     here = where[0]
     groups, rows = queries.shape[0], queries.shape[1]
     asked = [here ^ mask for mask in ORDER]
@@ -365,17 +365,17 @@
 ORDER = (0, 4, 2, 6, 1, 5, 3, 7)
 
 
-def remote_pieces(where, queries, pages, after):
+def remote_pieces(where, queries, pages):
     groups, rows, _ = queries.shape
     return pl.pallas_call(
         remote_kernel,
-        in_specs=[SMEM, VMEM, VMEM, VMEM],
+        in_specs=[SMEM, VMEM, VMEM],
         out_specs=VMEM,
         out_shape=jax.ShapeDtypeStruct((groups, rows, HEAD), bf16),
         compiler_params=pltpu.CompilerParams(vmem_limit_bytes=12 << 20),
         cost_estimate=pl.CostEstimate(flops=1 << 26, transcendentals=1 << 16, bytes_accessed=3 << 20),
         name="remote_pieces",
-    )(where, queries, pages, after)
+    )(where, queries, pages)
 
 
 def join_kernel(pieces, local, w_out, out, attn, weights, sems):
@@ -435,8 +435,7 @@
     )(pieces, local, w_out)
 
 
-def finish_kernel(side, own, other, x, gain, out, token):
-    token[...] = jnp.zeros_like(token)
+def finish_kernel(side, own, other, x, gain, after, out):
     half = out.shape[-1]
     total = own[...].astype(f32) + other[...].astype(f32)
     scale = lax.rsqrt(jnp.mean(total * total, axis=-1, keepdims=True) + eps_norm)
@@ -447,7 +446,7 @@
         out[...] = (x[...].astype(f32) + mine).astype(bf16)
 
 
-def finish(side, own, other, x, gain, name):
+def finish(side, own, other, x, gain, after, name):
     rows, width = own.shape
     half = width // 2
     block = min(rows, 128)
@@ -469,16 +468,17 @@
                 pl.BlockSpec((block, width), lambda i, s: (i, 0)),
                 x_spec,
                 pl.BlockSpec((1, half), lambda i, s: (0, s[0])),
+                pl.BlockSpec((8, 128), lambda i, s: (0, 0)),
             ],
-            out_specs=[o_spec, pl.BlockSpec(TOKEN.shape, lambda i, s: (0, 0))],
+            out_specs=o_spec,
         ),
-        out_shape=[jax.ShapeDtypeStruct(shape, bf16), TOKEN],
+        out_shape=jax.ShapeDtypeStruct(shape, bf16),
         compiler_params=pltpu.CompilerParams(vmem_limit_bytes=12 << 20),
         cost_estimate=pl.CostEstimate(
             flops=8 * rows * width, transcendentals=0, bytes_accessed=6 * rows * width
         ),
         name=name,
-    )(side, own, other, x, gain)
+    )(side, own, other, x, gain, after)
 
 
 def on_device(
@@ -536,16 +536,16 @@
     )
     asked, partial = lax.optimization_barrier((asked, partial))
     other = lax.ppermute(partial, "head", swap)
-    prefill_out, done = finish(side, partial, other, prefill_x, post_gain[None], "finish_prompts")
 
     queries = ask(where, asked, w_query, small)
-    pieces = remote_pieces(
-        where, queries, arrived.reshape(planes, DEEP, PAGE, -1), done
-    )
+    pieces = remote_pieces(where, queries, arrived.reshape(planes, DEEP, PAGE, -1))
     pieces = lax.all_to_all(pieces, "req", 0, 0, tiled=True, axis_index_groups=column)
-    partial = join(pieces, own, w_out)
-    other = lax.ppermute(partial, "head", swap)
-    verify_out, _ = finish(side, partial, other, verify_x, post_gain[None], "finish_drafts")
+    tail = join(pieces, own, w_out)
+    prefill_out = finish(
+        side, partial, other, prefill_x, post_gain[None], tail, "finish_prompts"
+    )
+    other = lax.ppermute(tail, "head", swap)
+    verify_out = finish(side, tail, other, verify_x, post_gain[None], tail, "finish_drafts")
     return (verify_out, prefill_out, verify_kv, prefill_kv)
 
 

time: 65.2 us -> 66 us (1.012)
  blocking collectives: 12.2 us -> 13.8 us
  waiting for transfers between devices: 0.92 us -> 0.02 us
    ppermute x0 -> x1, starting transfers between devices: none -> 4.97 us  [on_device(): other = lax.ppermute(tail, 'head', swap)]
    ppermute x2 -> x1, starting transfers between devices: 7.13 us -> 2.16 us  [on_device(): other = lax.ppermute(partial, 'head', swap)]
    all_to_all x1, blocking collectives: 12.2 us -> 13.8 us  [on_device(): lax.all_to_all(pieces, 'req', 0, 0, tiled=True, axis_index_groups=column)]
    ppermute x2 -> x1, waiting for transfers between devices: 0.9 us -> 0.01 us  [on_device(): other = lax.ppermute(partial, 'head', swap)]
  transfers between devices with their start and end apart: 7 -> 7, of which waited for: 1 -> 0; matrix products, arithmetic and copies ran while one was open for 0% -> 0% of each run, Pallas kernels for 27% -> 31%
where the time goes in v10:
time: 66 us; the launch traced here: 65.6 us
  starting transfers between devices  25.5 us (39%)
  Pallas kernels  24 us (36%)
  blocking collectives  13.8 us (21%)
  between operations  2.13 us (3%)
    all_to_all x1, blocking collectives, on_device(): lax.all_to_all(pieces, 'req', 0, 0, tiled=True, axis_index_groups=column)  13.8 us
    ppermute x4, starting transfers between devices, beside(): parts.append(lax.ppermute(values, 'req', pairs))  10.6 us
    all_to_all x1, starting transfers between devices, on_device(): lax.all_to_all(outgoing, 'req', 0, 0, tiled=True, axis_index_groups=plane)  7.73 us
    pallas_call x1, Pallas kernels, project(): pl.pallas_call(project_kernel, in_specs=[SMEM, SMEM, HBM, VMEM, VMEM, HBM...  6.17 us
    pallas_call x1, Pallas kernels, prompts(): pl.pallas_call(prompt_kernel, in_specs=[SMEM] + [VMEM] * 6 + [HBM], out_s...  5.96 us
    ppermute x1, starting transfers between devices, on_device(): other = lax.ppermute(tail, 'head', swap)  4.97 us
    pallas_call x1, Pallas kernels, ask(): pl.pallas_call(ask_kernel, in_specs=[SMEM, VMEM, HBM, VMEM], out_specs=VM...  2.87 us
    pallas_call x1, Pallas kernels, pick_pages(): pl.pallas_call(pick_kernel, in_specs=[SMEM, VMEM], out_specs=[VMEM, VMEM]...  2.83 us
  transfers between devices with their start and end apart: 7, of which 0 were waited for; matrix products, arithmetic and copies ran while one was open for 0% of the time, Pallas kernels for 31%

profile of v10, /device:TPU:1, one launch (start us, length us, event | category | flops | bytes accessed | tf_op | source)
XLA Modules:
  0.0 65.6 jit_solution(10946105532949288360)
XLA Ops:
  0.6 2.8 %pick_pages.1 = (bf16[128,16,512]{2,1,0:T(8,128)(2,1)}, f32[8,128]{1,0:T(8,128)}) custom-call(s32[1,128]{1,0:T(1,128)} %index.1, bf16[64,16,512]{2,1,0:T(8,128)(2,1)} %pool.1), custom_call_target="tpu_custom_call" | custom-call | bytes 4194304 | tf_op jit(solution)/shard_map/pick_pages/pallas_call | solution.py:61
  3.5 0.0 copy-start.9
  3.5 7.7 %all-to-all-start = ((bf16[128,16,512]{2,1,0:T(8,128)(2,1)}), bf16[128,16,512]{2,1,0:T(8,128)(2,1)S(1)}, u32[]{:S(2)}, u32[]{:S(2)}) async-start(bf16[128,16,512]{2,1,0:T(8,128)(2,1)} %get-tuple-element.37), calls=%async_computation | async-start | bytes 4194304 | tf_op jit(solution)/shard_map/all_to_all | solution.py:509
  12.6 0.7 pack.1
  13.2 7.0 %collective-permute-start = (bf16[1,8,2048]{2,1,0:T(8,128)(2,1)S(1)}, bf16[1,8,2048]{2,1,0:T(8,128)(2,1)S(1)}, u32[]{:S(2)}, u32[]{:S(2)}) collective-permute-start(bf16[1,8,2048]{2,1,0:T(8,128)(2,1)S(1)} %pack.1), channel_id=1, source_target_pairs={{0,8},{2,10},{4,12},{6,14},{8,0},{10,2},{12,4},{14,6},{16,24},{18,... | collective-permute-start | bytes 98312 | tf_op jit(solution)/shard_map/ppermute | solution.py:520
  20.2 6.2 %project.1 = (bf16[4,256,256]{2,1,0:T(8,128)(2,1)}, bf16[256,512]{1,0:T(8,128)(2,1)}, bf16[256,512]{1,0:T(8,128)(2,1)}, bf16[32,256]{1,0:T(8,128)(2,1)}, f32[8,5...) custom-call(s32[8]{0:T(128)} %copy-done.10, s32[1,4]{1,0:T(1,128)} %lengths.3, ...), custom_call_target="tpu_custom_call" | custom-call | flops 1711276032 | bytes 9437184 | tf_op jit(solution)/shard_map/project/pallas_call | solution.py:152
  26.4 0.0 collective-permute-done
  26.4 1.7 %collective-permute-start.3 = (bf16[2,8,2048]{2,1,0:T(8,128)(2,1)S(1)}, bf16[2,8,2048]{2,1,0:T(8,128)(2,1)S(1)}, u32[]{:S(2)}, u32[]{:S(2)}) collective-permute-start(bf16[2,8,2048]{2,1,0:T(8,128)(2,1)S(1)} %pad_maximum_fusion.1), channel_id=1, source_target_pairs={{0,6},{2,4},{4,2},{6,0},{8,14},{10,12},{12,10},{14,8},{16,22},{18,... | collective-permute-start | bytes 196616 | tf_op jit(solution)/shard_map/ppermute | solution.py:520
  28.2 0.0 collective-permute-start.2
  28.2 1.9 %collective-permute-start.1 = (bf16[2,8,2048]{2,1,0:T(8,128)(2,1)S(1)}, bf16[2,8,2048]{2,1,0:T(8,128)(2,1)S(1)}, u32[]{:S(2)}, u32[]{:S(2)}) collective-permute-start(bf16[2,8,2048]{2,1,0:T(8,128)(2,1)S(1)} %pad_maximum_fusion.1), channel_id=1, source_target_pairs={{0,4},{2,6},{4,0},{6,2},{8,12},{10,14},{12,8},{14,10},{16,20},{18,... | collective-permute-start | bytes 196616 | tf_op jit(solution)/shard_map/ppermute | solution.py:520
  30.1 6.0 %prompts.1 = (bf16[256,2048]{1,0:T(8,128)(2,1)}, f32[32,512]{1,0:T(8,128)}) custom-call(s32[1,4]{1,0:T(1,128)} %lengths.3, bf16[4,256,256]{2,1,0:T(8,128)(2,1)} %get-tuple-element.29.q, bf16[256,512]{1,0:T(8,128)(2,1)} %get-tuple-element.30.kv, bf16[32,256]{1,0:T(8,128)(2,1)} %get-tuple-element.31.query, f32[8,512]{1,0:T(8,128)} %get-tuple-element.32.draft_kv, ...), custom_call_target="tpu_custom_call" | custom-call | flops 268435456 | bytes 4194304 | tf_op jit(solution)/shard_map/prompts/pallas_call | solution.py:305
  36.0 0.0 collective-permute-done.3
  36.1 0.0 collective-permute-done.2
  36.1 0.0 collective-permute-done.1
  36.1 2.2 %collective-permute-start.5 = (bf16[256,2048]{1,0:T(8,128)(2,1)}, bf16[256,2048]{1,0:T(8,128)(2,1)S(1)}, u32[]{:S(2)}, u32[]{:S(2)}) collective-permute-start(bf16[256,2048]{1,0:T(8,128)(2,1)} %get-tuple-element.39.own), channel_id=1, source_target_pairs={{0,1},{1,0},{2,3},{3,2},{4,5},{5,4},{6,7},{7,6},{8,9},{9,8},{10,11... | collective-permute-start | bytes 3145736 | tf_op jit(solution)/shard_map/ppermute | solution.py:538
  38.3 2.9 %ask.1.queries = bf16[8,32,256]{2,1,0:T(8,128)(2,1)S(1)} custom-call(s32[1]{0:T(128)} %bitcast.1.where, bf16[8,8,2048]{2,1,0:T(8,128)(2,1)S(1)} %pad_maximum_fusion.x, bf16[2048,1024]{1,0:T(8,128)(2,1)} %wq.3, f32[8,256]{1,0:T(8,128)S(1)} %copy-done.7), custom_call_target="tpu_custom_call" | custom-call | flops 268435456 | bytes 5242880 | tf_op jit(solution)/shard_map/ask/pallas_call | solution.py:235
  41.2 0.7 %remote_pieces.1 = bf16[8,32,256]{2,1,0:T(8,128)(2,1)S(1)} custom-call(s32[1]{0:T(128)} %bitcast.1.where, bf16[8,32,256]{2,1,0:T(8,128)(2,1)S(1)} %ask.1.queries, bf16[16,8,16,512]{3,2,1,0:T(8,128)(2,1)S(1)} %bitcast.10), custom_call_target="tpu_custom_call" | custom-call | flops 67108864 | bytes 3145728 | tf_op jit(solution)/shard_map/remote_pieces/pallas_call | solution.py:370
  41.9 13.8 %all_to_all.10.pieces = bf16[8,32,256]{2,1,0:T(8,128)(2,1)S(1)} all-to-all(bf16[8,32,256]{2,1,0:T(8,128)(2,1)S(1)} %remote_pieces.1), channel_id=1, replica_groups={{0,2,4,6,8,10,12,14},{16,18,20,22,24,26,28,30},{32,34,36,38,40,42,44,46..., dimensions={0} | all-to-all | bytes 262144 | tf_op jit(solution)/shard_map/all_to_all | solution.py:542
  55.7 2.6 %join.1.own.after = f32[8,2048]{1,0:T(8,128)S(1)} custom-call(bf16[8,32,256]{2,1,0:T(8,128)(2,1)S(1)} %all_to_all.10.pieces, f32[32,512]{1,0:T(8,128)S(1)} %copy-done.4, bf16[1024,2048]{1,0:T(8,128)(2,1)} %w_out.3), custom_call_target="tpu_custom_call" | custom-call | flops 33554432 | bytes 4194304 | tf_op jit(solution)/shard_map/join/pallas_call | solution.py:422
  58.3 0.0 copy-start.3
  58.4 5.0 %collective-permute-start.4 = (f32[8,2048]{1,0:T(8,128)S(1)}, f32[8,2048]{1,0:T(8,128)S(1)}, u32[]{:S(2)}, u32[]{:S(2)}) collective-permute-start(f32[8,2048]{1,0:T(8,128)S(1)} %join.1.own.after), channel_id=1, source_target_pairs={{0,1},{1,0},{2,3},{3,2},{4,5},{5,4},{6,7},{7,6},{8,9},{9,8},{10,11... | collective-permute-start | bytes 196616 | tf_op jit(solution)/shard_map/ppermute | solution.py:547
  63.3 1.5 %finish_prompts.1 = bf16[256,1024]{1,0:T(8,128)(2,1)} custom-call(s32[1]{0:T(128)} %bitcast.side, bf16[256,2048]{1,0:T(8,128)(2,1)S(1)} %copy-done.1, bf16[256,2048]{1,0:T(8,128)(2,1)S(1)} %collective-permute-done.5.other, bf16[256,2048]{1,0:T(8,128)(2,1)S(1)} %copy-done, f32[1,2048]{1,0:T(1,128)S(1)} %bitcast.11, f32[8,2048]{1,0:T(8,128)S(1)} %join.1.own.after), custom_call_target="tpu_custom_call" | custom-call | flops 4194304 | bytes 3145728 | tf_op jit(solution)/shard_map/finish_prompts/pallas_call | solution.py:461
  64.8 0.0 collective-permute-done.4.other
  64.9 0.7 %finish_drafts.1 = bf16[1,5,1024]{2,1,0:T(8,128)(2,1)} custom-call(s32[1]{0:T(128)} %bitcast.side, f32[8,2048]{1,0:T(8,128)S(1)} %join.1.own.after, f32[8,2048]{1,0:T(8,128)S(1)} %collective-permute-done.4.other, bf16[1,5,2048]{2,1,0:T(8,128)(2,1)S(1)} %copy-done.3, f32[1,2048]{1,0:T(1,128)S(1)} %bitcast.12, f32[8,2048]{1,0:T(8,128)S(1)} %join.1.own.after), custom_call_target="tpu_custom_call" | custom-call | flops 131072 | bytes 98304 | tf_op jit(solution)/shard_map/finish_drafts/pallas_call | solution.py:461
  (25 shorter events, 0.1 us)
Async XLA Ops:
  3.5 9.1 %copy-start.2 = (bf16[1,5,2048]{2,1,0:T(8,128)(2,1)S(1)}, bf16[1,5,2048]{2,1,0:T(8,128)(2,1)}, u32[]{:S(2)}) copy-start(bf16[1,5,2048]{2,1,0:T(8,128)(2,1)} %x.2) | copy-start | bytes 61444
  3.5 9.1 %copy-start.6 = (f32[2048]{0:T(1024)S(1)}, f32[2048]{0:T(1024)}, u32[]{:S(2)}) copy-start(f32[2048]{0:T(1024)} %param.17) | copy-start | bytes 24580
  3.5 9.1 %copy-start.8 = (f32[8,128]{1,0:T(8,128)S(1)}, f32[8,128]{1,0:T(8,128)}, u32[]{:S(2)}) copy-start(f32[8,128]{1,0:T(8,128)} %get-tuple-element.25.after) | copy-start | bytes 12292
  3.5 9.1 %copy-start.9 = (s32[1,64]{1,0:T(1,128)S(1)}, s32[1,64]{1,0:T(1,128)}, u32[]{:S(2)}) copy-start(s32[1,64]{1,0:T(1,128)} %table.3) | copy-start | bytes 772
  3.5 37.7 %all-to-all-start = ((bf16[128,16,512]{2,1,0:T(8,128)(2,1)}), bf16[128,16,512]{2,1,0:T(8,128)(2,1)S(1)}, u32[]{:S(2)}, u32[]{:S(2)}) async-start(bf16[128,16,512]{2,1,0:T(8,128)(2,1)} %get-tuple-element.37), calls=%async_computation | async-start | bytes 4194304 | tf_op jit(solution)/shard_map/all_to_all | solution.py:509
  12.5 7.7 %copy-start.10 = (s32[8]{0:T(128)}, s32[8]{0:T(128)S(1)}, u32[]{:S(2)}) copy-start(s32[8]{0:T(128)S(1)} %compare_select_fusion.meta) | copy-start | bytes 100
  13.2 13.2 %collective-permute-start = (bf16[1,8,2048]{2,1,0:T(8,128)(2,1)S(1)}, bf16[1,8,2048]{2,1,0:T(8,128)(2,1)S(1)}, u32[]{:S(2)}, u32[]{:S(2)}) collective-permute-start(bf16[1,8,2048]{2,1,0:T(8,128)(2,1)S(1)} %pack.1), channel_id=1, source_target_pairs={{0,8},{2,10},{4,12},{6,14},{8,0},{10,2},{12,4},{14,6},{16,24},{18,... | collective-permute-start | bytes 98312 | tf_op jit(solution)/shard_map/ppermute | solution.py:520
  26.4 9.6 %collective-permute-start.3 = (bf16[2,8,2048]{2,1,0:T(8,128)(2,1)S(1)}, bf16[2,8,2048]{2,1,0:T(8,128)(2,1)S(1)}, u32[]{:S(2)}, u32[]{:S(2)}) collective-permute-start(bf16[2,8,2048]{2,1,0:T(8,128)(2,1)S(1)} %pad_maximum_fusion.1), channel_id=1, source_target_pairs={{0,6},{2,4},{4,2},{6,0},{8,14},{10,12},{12,10},{14,8},{16,22},{18,... | collective-permute-start | bytes 196616 | tf_op jit(solution)/shard_map/ppermute | solution.py:520
  28.2 7.9 %collective-permute-start.2 = (bf16[2,8,2048]{2,1,0:T(8,128)(2,1)S(1)}, bf16[2,8,2048]{2,1,0:T(8,128)(2,1)S(1)}, u32[]{:S(2)}, u32[]{:S(2)}) collective-permute-start(bf16[2,8,2048]{2,1,0:T(8,128)(2,1)S(1)} %pad_maximum_fusion.1), channel_id=1, source_target_pairs={{0,2},{2,0},{4,6},{6,4},{8,10},{10,8},{12,14},{14,12},{16,18},{18,... | collective-permute-start | bytes 196616 | tf_op jit(solution)/shard_map/ppermute | solution.py:520
  28.2 7.9 %collective-permute-start.1 = (bf16[2,8,2048]{2,1,0:T(8,128)(2,1)S(1)}, bf16[2,8,2048]{2,1,0:T(8,128)(2,1)S(1)}, u32[]{:S(2)}, u32[]{:S(2)}) collective-permute-start(bf16[2,8,2048]{2,1,0:T(8,128)(2,1)S(1)} %pad_maximum_fusion.1), channel_id=1, source_target_pairs={{0,4},{2,6},{4,0},{6,2},{8,12},{10,14},{12,8},{14,10},{16,20},{18,... | collective-permute-start | bytes 196616 | tf_op jit(solution)/shard_map/ppermute | solution.py:520
  30.1 8.2 %copy-start.7 = (f32[8,256]{1,0:T(8,128)S(1)}, f32[8,256]{1,0:T(8,128)}, u32[]{:S(2)}) copy-start(f32[8,256]{1,0:T(8,128)} %get-tuple-element.36.small) | copy-start | bytes 24580
  36.1 27.2 %collective-permute-start.5 = (bf16[256,2048]{1,0:T(8,128)(2,1)}, bf16[256,2048]{1,0:T(8,128)(2,1)S(1)}, u32[]{:S(2)}, u32[]{:S(2)}) collective-permute-start(bf16[256,2048]{1,0:T(8,128)(2,1)} %get-tuple-element.39.own), channel_id=1, source_target_pairs={{0,1},{1,0},{2,3},{3,2},{4,5},{5,4},{6,7},{7,6},{8,9},{9,8},{10,11... | collective-permute-start | bytes 3145736 | tf_op jit(solution)/shard_map/ppermute | solution.py:538
  41.2 14.5 %copy-start.4 = (f32[32,512]{1,0:T(8,128)S(1)}, f32[32,512]{1,0:T(8,128)}, u32[]{:S(2)}) copy-start(f32[32,512]{1,0:T(8,128)} %get-tuple-element.38.local) | copy-start | bytes 196612
  55.7 7.6 %copy-start = (bf16[256,2048]{1,0:T(8,128)(2,1)S(1)}, bf16[256,2048]{1,0:T(8,128)(2,1)}, u32[]{:S(2)}) copy-start(bf16[256,2048]{1,0:T(8,128)(2,1)} %x.3) | copy-start | bytes 3145732
  55.7 7.6 %copy-start.1 = (bf16[256,2048]{1,0:T(8,128)(2,1)S(1)}, bf16[256,2048]{1,0:T(8,128)(2,1)}, u32[]{:S(2)}) copy-start(bf16[256,2048]{1,0:T(8,128)(2,1)} %get-tuple-element.39.own) | copy-start | bytes 3145732
  55.7 7.6 %copy-start.5 = (f32[2048]{0:T(1024)S(1)}, f32[2048]{0:T(1024)}, u32[]{:S(2)}) copy-start(f32[2048]{0:T(1024)} %param.22) | copy-start | bytes 24580
  58.3 6.5 %copy-start.3 = (bf16[1,5,2048]{2,1,0:T(8,128)(2,1)S(1)}, bf16[1,5,2048]{2,1,0:T(8,128)(2,1)}, u32[]{:S(2)}) copy-start(bf16[1,5,2048]{2,1,0:T(8,128)(2,1)} %x.2) | copy-start | bytes 61444
  58.4 6.5 %collective-permute-start.4 = (f32[8,2048]{1,0:T(8,128)S(1)}, f32[8,2048]{1,0:T(8,128)S(1)}, u32[]{:S(2)}, u32[]{:S(2)}) collective-permute-start(f32[8,2048]{1,0:T(8,128)S(1)} %join.1.own.after), channel_id=1, source_target_pairs={{0,1},{1,0},{2,3},{3,2},{4,5},{5,4},{6,7},{7,6},{8,9},{9,8},{10,11... | collective-permute-start | bytes 196616 | tf_op jit(solution)/shard_map/ppermute | solution.py:547
